TPU v7x, 256 devices: a whole 4x4x8 slice. The times are simulated.
256 devices in a mesh: mem: 64 (over x, z_lo, y, core), head: 4 (over z_hi).
Axes of the slice: x: 4, y: 4, z: 8 (z_hi: 4, z_lo: 2; z = z_hi * 2 + z_lo), core: 2. Of those that a mesh axis runs over, the one named last changes fastest.
Arguments:
- queries: bfloat16 [8192, 4096], P('mem', 'head'), may hold values from -200 to 200
- mem_keys: bfloat16 [6144, 4096], P('mem', 'head'), may hold values from -6 to 6
- mem_values: bfloat16 [6144, 4096], P('mem', 'head'), may hold values from -24 to 24
- own_values: bfloat16 [8192, 4096], P('mem', 'head'), may hold values from -6 to 6
- gate_bias: float32 [32], P('head'), may hold values from -2 to 2
- w_out: bfloat16 [4096, 4096], P('head'), may hold values from -0.09375 to 0.09375
- probes: int32 [8192, 8], P('mem'), may hold values from 0 to 383, as said below
- pattern: int32 [64, 64], replicated, may hold values from 0 to 1, as said below
Outputs:
- projected: bfloat16 [8192, 4096], P(('mem', 'head'))
Inputs may be any that keep to these rules, and one draw needn't show every extreme that they name: `pattern`: entries are 0 or 1; every row has at least one 1. `probes`: the 8 clusters of a query are distinct. The first lies in a cluster block b with pattern[r, b] = 1, r being the query's block of 128 rows.
All inputs are finite; a program needn't handle non-finite values.
Results may differ from a plain program's by a relative error of at most 0.012.
Values may be sent and summed in bfloat16 or wider, within the bound.
No kernel may reach another device: no remote copies, remote signals or barrier semaphores. Data moves between devices by JAX's collectives and lax.ppermute only.
A program may use at most 128 MiB of HBM per device.

v0:
```python
import math

import jax
import jax.numpy as jnp
from jax import lax
from jax.experimental import pallas as pl
from jax.experimental.pallas import tpu as pltpu
from jax.sharding import Mesh
from jax.sharding import PartitionSpec as P

HD = 128
CSIZE = 16
NEG = -1e30
EXP2_SCALE = math.log2(math.e) / math.sqrt(HD)


B_AXES = ("zl", "y")
NX, NB, NC, NH = 4, 8, 2, 4
ROWS_Q, ROWS_M, ROWS_P, ROWS_O = 128, 96, 32, 32
NQ = NB * ROWS_Q
HALF = NB * ROWS_M
OFFSETS = (0, 3, 1, 2)
TILE_Q = 256


def in_vmem(array):
    return pltpu.with_memory_space_constraint(array, pltpu.VMEM)


VMEM_SPEC = pl.BlockSpec(memory_space=pltpu.VMEM)
SMEM_SPEC = pl.BlockSpec(memory_space=pltpu.SMEM)


def bias_body(place_ref, probe_ref, pattern_ref, bias_ref):
    x = place_ref[0]
    core = place_ref[1]
    pattern = pattern_ref[...].astype(jnp.float32)
    row = lax.broadcasted_iota(jnp.int32, (8, 64), 0)
    own_rows = (x * NB + row) * NC + core
    pick = (lax.broadcasted_iota(jnp.int32, (8, 64), 1) == own_rows).astype(jnp.float32)
    allowed_rows = jnp.dot(pick, pattern, preferred_element_type=jnp.float32)
    per_block = ROWS_M // CSIZE
    per_slot = HALF // CSIZE
    block = lax.broadcasted_iota(jnp.int32, (64, 128), 0)
    col = lax.broadcasted_iota(jnp.int32, (64, 128), 1)
    slot = jnp.where((block % NC) == core, 0, 1)
    first_col = slot * per_slot + ((block // NC) % NB) * per_block
    inside = (col >= first_col) & (col < first_col + per_block)
    allowed = []
    for offset in OFFSETS:
        spread = inside & ((block // (NC * NB)) == lax.rem(x + offset, NX))
        spread = jnp.where(spread, 1.0, 0.0)
        picked = jnp.dot(allowed_rows, spread, preferred_element_type=jnp.float32)
        allowed.append(jnp.where(picked > 0.5, 0.0, NEG))
    lane = lax.broadcasted_iota(jnp.int32, (1, 128), 1)
    targets = []
    for offset in OFFSETS:
        targets.append((lane + lax.rem(x + offset, NX) * 128).astype(jnp.float32))
    for b in range(NB):
        coded = probe_ref[b].astype(jnp.float32)
        code = coded[0:8] * 128.0 + coded[8:16]
        code = code + jnp.where(coded[16:24] == core.astype(jnp.float32), 0.0, float(per_slot))
        code = jnp.concatenate([code] * 16, axis=0).T
        for row in range(0, ROWS_Q, 32):
            live = [jnp.full((32, 128), NEG, jnp.float32)] * NX
            for j in range(8):
                spread = jnp.broadcast_to(code[row : row + 32, j : j + 1], (32, 128))
                for k in range(NX):
                    live[k] = jnp.where(spread == targets[k], allowed[k][b : b + 1, :], live[k])
            for k in range(NX):
                span = slice(b * ROWS_Q + row, b * ROWS_Q + row + 32)
                bias_ref[k, span, :] = live[k].astype(jnp.bfloat16)


def make_bias(place, probe_rows, pattern):
    return pl.pallas_call(
        bias_body,
        in_specs=[SMEM_SPEC, VMEM_SPEC, VMEM_SPEC],
        out_specs=VMEM_SPEC,
        out_shape=pltpu.VMEM((NX, NQ, 128), jnp.bfloat16),
        compiler_params=pltpu.CompilerParams(vmem_limit_bytes=16 << 20),
        name="bias",
    )(place, in_vmem(probe_rows), in_vmem(pattern))


def chunk_body(k, parts, *refs):
    first = k == 0
    last = k == NX - 1
    received_ref, bias_ref = refs[:2]
    kv_refs = refs[2 : 2 + 2 * parts]
    rest = refs[2 + 2 * parts :]
    if not first:
        m_in, acc_in = rest[:2]
        rest = rest[2:]
    if last:
        out_ref, score_ref, peak_ref = rest
    else:
        m_out, acc_out, score_ref, peak_ref = rest
    width = 256
    entry = lax.broadcasted_iota(jnp.int32, (2 * HALF, 128), 0) // CSIZE
    onehot = (entry == lax.broadcasted_iota(jnp.int32, (2 * HALF, 128), 1)).astype(jnp.bfloat16)
    if parts == 1:
        keys = [r[:, :ROWS_M, :].reshape(HALF, HD) for r in kv_refs]
        values = [r[:, ROWS_M:, :].reshape(HALF, HD) for r in kv_refs]
    else:
        keys = [r[...].reshape(HALF, HD) for r in kv_refs[0::2]]
        values = [r[...].reshape(HALF, HD) for r in kv_refs[1::2]]
    keys = jnp.concatenate([jnp.concatenate(keys, axis=0), onehot], axis=1)
    values = jnp.concatenate([jnp.concatenate(values, axis=0), jnp.ones((2 * HALF, 128), jnp.bfloat16)], axis=1)
    rows = received_ref[:, :ROWS_Q, :].reshape(NQ, HD)
    rows = jnp.concatenate([rows, bias_ref[k]], axis=1)
    for j in range(2 * HALF // width):
        span = slice(j * width, (j + 1) * width)
        scores = lax.dot_general(rows, keys[span], (((1,), (1,)), ((), ())), preferred_element_type=jnp.float32)
        score_ref[:, span] = scores
        peak = jnp.maximum(scores[:, :128], scores[:, 128:])
        if j:
            peak = jnp.maximum(peak, peak_ref[...])
        peak_ref[...] = peak
    for t in range(NQ // TILE_Q):
        span = slice(t * TILE_Q, (t + 1) * TILE_Q)
        peak = jnp.max(peak_ref[span, :], axis=1, keepdims=True)
        if first:
            peak = jnp.maximum(peak, NEG / 2)
        else:
            old = m_in[span, 0:1]
            peak = jnp.maximum(peak, old)
        weights = jnp.exp2((score_ref[span, :] - peak) * EXP2_SCALE).astype(jnp.bfloat16)
        acc = jnp.dot(weights, values, preferred_element_type=jnp.float32)
        if not first:
            acc = acc + acc_in[span, :] * jnp.exp2((old - peak) * EXP2_SCALE)
        if last:
            out = (acc[:, :HD] / acc[:, HD:]).astype(jnp.bfloat16)
            per = TILE_Q // ROWS_Q
            out_ref[t * per : (t + 1) * per] = out.reshape(per, ROWS_Q, HD)
        else:
            m_out[span, :] = jnp.broadcast_to(peak, (TILE_Q, 128))
            acc_out[span, :] = acc


def attend(k, received, bias, kv, state):
    first = k == 0
    last = k == NX - 1
    parts = len(kv) // 2
    args = [received, bias, *kv]
    if not first:
        args += list(state)
    if last:
        out_shape = pltpu.VMEM((NB, ROWS_Q, HD), jnp.bfloat16)
    else:
        out_shape = [pltpu.VMEM((NQ, 128), jnp.float32), pltpu.VMEM((NQ, 2 * HD), jnp.float32)]
    return pl.pallas_call(
        lambda *refs: chunk_body(k, parts, *refs),
        in_specs=[VMEM_SPEC] * len(args),
        out_specs=VMEM_SPEC if last else [VMEM_SPEC] * 2,
        out_shape=out_shape,
        scratch_shapes=[pltpu.VMEM((NQ, 2 * HALF), jnp.float32), pltpu.VMEM((NQ, 128), jnp.float32)],
        cost_estimate=pl.CostEstimate(flops=1 << 20, bytes_accessed=1 << 10, transcendentals=0),
        compiler_params=pltpu.CompilerParams(vmem_limit_bytes=24 << 20),
    )(*[in_vmem(arg) for arg in args])


def project_body(place_ref, gate_ref, rec_ref, own_ref, w_ref, top_ref, bottom_ref, up_ref, up_free_ref, down_ref, down_free_ref, here_ref):
    plane = place_ref[2]
    order = [pl.multiple_of(lax.rem(plane + away, NH) * ROWS_O, ROWS_O) for away in (2, 1, 3, 0)]
    mixed = []
    for h in range(NB):
        gate = 1.0 / (1.0 + jnp.exp(jnp.full((1, 128), -gate_ref[h], jnp.float32)))
        span = slice(h * HD, (h + 1) * HD)
        rows = []
        for start in order:
            recalled = rec_ref[h, pl.ds(start, ROWS_O), :].astype(jnp.float32)
            blended = gate * recalled + (1.0 - gate) * own_ref[pl.ds(start, ROWS_O), span].astype(jnp.float32)
            rows.append(blended.astype(jnp.bfloat16))
        mixed.append(jnp.concatenate(rows, axis=0))
    mixed = jnp.concatenate(mixed, axis=1)
    width = 512
    half = ROWS_O // 2
    outs = (top_ref, bottom_ref, up_ref, up_free_ref, down_free_ref, down_ref)
    for i in range(w_ref.shape[1] // width):
        span = slice(i * width, (i + 1) * width)
        part = jnp.dot(mixed, w_ref[:, span], preferred_element_type=jnp.float32)
        for n, out_ref in enumerate(outs):
            out_ref[:, span] = part[n * half : (n + 1) * half].astype(jnp.bfloat16)
        here_ref[:, span] = part[3 * ROWS_O :]


def project(place, gate_bias, recalled, own_values, w_out):
    half = pltpu.VMEM((ROWS_O // 2, w_out.shape[1]), jnp.bfloat16)
    return pl.pallas_call(
        project_body,
        in_specs=[SMEM_SPEC, SMEM_SPEC, VMEM_SPEC, VMEM_SPEC, VMEM_SPEC],
        out_specs=[VMEM_SPEC] * 7,
        out_shape=[half] * 6 + [pltpu.VMEM((ROWS_O, w_out.shape[1]), jnp.float32)],
        cost_estimate=pl.CostEstimate(flops=2 * ROWS_Q * w_out.size, bytes_accessed=10 << 20, transcendentals=0),
        compiler_params=pltpu.CompilerParams(vmem_limit_bytes=16 << 20),
        name="project",
    )(place, gate_bias, in_vmem(recalled), in_vmem(own_values), in_vmem(w_out))


def add_body(a_ref, b_ref, c_ref, d_ref, up_ref, down_ref):
    up_ref[...] = (a_ref[...].astype(jnp.float32) + b_ref[...].astype(jnp.float32)).astype(jnp.bfloat16)
    down_ref[...] = (c_ref[...].astype(jnp.float32) + d_ref[...].astype(jnp.float32)).astype(jnp.bfloat16)


def add_pairs(*args):
    half = pltpu.VMEM(args[0].shape, jnp.bfloat16)
    return pl.pallas_call(
        add_body,
        in_specs=[VMEM_SPEC] * 4,
        out_specs=[VMEM_SPEC] * 2,
        out_shape=[half] * 2,
        compiler_params=pltpu.CompilerParams(vmem_limit_bytes=16 << 20),
        name="add_pairs",
    )(*[in_vmem(arg) for arg in args])


def finish_body(here_ref, up_ref, up_free_ref, down_ref, down_free_ref, out_ref):
    half = ROWS_O // 2
    for span, a_ref, b_ref in ((slice(0, half), up_ref, down_free_ref), (slice(half, 2 * half), up_free_ref, down_ref)):
        total = here_ref[span, :] + a_ref[...].astype(jnp.float32) + b_ref[...].astype(jnp.float32)
        out_ref[span, :] = total.astype(jnp.bfloat16)


def finish(*args):
    return pl.pallas_call(
        finish_body,
        in_specs=[VMEM_SPEC] * 5,
        out_shape=jax.ShapeDtypeStruct(args[0].shape, jnp.bfloat16),
        compiler_params=pltpu.CompilerParams(vmem_limit_bytes=16 << 20),
        name="finish",
    )(*[in_vmem(arg) for arg in args])


def pack_body(q_ref, k_ref, v_ref, probe_ref, out_ref, sems):
    copies = []
    for h in range(NB):
        span = slice(h * HD, (h + 1) * HD)
        row = 0
        for source in (q_ref, k_ref, v_ref):
            size = source.shape[0]
            place = out_ref.at[h, row : row + size, :]
            copies.append(pltpu.make_async_copy(source.at[:, span], place, sems.at[len(copies)]))
            row += size
    for copy in copies:
        copy.start()
    per_block = ROWS_M // CSIZE
    number = probe_ref[...].astype(jnp.float32)
    block = jnp.floor((number + 0.5) * (1.0 / per_block))
    rest = number - per_block * block
    pair = jnp.floor(block * (1.0 / NC))
    source_x = jnp.floor(block * (1.0 / (NC * NB)))
    column = (pair - NB * source_x) * per_block + rest
    coded = jnp.concatenate([source_x, column, block - NC * pair, jnp.zeros_like(block)], axis=0)
    coded = coded.astype(jnp.bfloat16)
    for h in range(NB):
        out_ref[h, ROWS_Q + 2 * ROWS_M :, :] = coded
    for copy in copies:
        copy.wait()


def pack(queries, mem_keys, mem_values, probe_rows):
    anywhere = pl.BlockSpec(memory_space=pltpu.HBM)
    return pl.pallas_call(
        pack_body,
        in_specs=[anywhere, anywhere, anywhere, VMEM_SPEC],
        out_specs=VMEM_SPEC,
        out_shape=pltpu.VMEM((NB, ROWS_Q + 2 * ROWS_M + ROWS_P, HD), jnp.bfloat16),
        scratch_shapes=[pltpu.SemaphoreType.DMA((3 * NB,))],
        compiler_params=pltpu.CompilerParams(vmem_limit_bytes=16 << 20),
        name="pack",
    )(*[pltpu.with_memory_space_constraint(a, pltpu.HBM) for a in (queries, mem_keys, mem_values)], probe_rows)


def local(queries, mem_keys, mem_values, own_values, gate_bias, w_out, probes, pattern):
    received = lax.all_to_all(pack(queries, mem_keys, mem_values, probes.T), B_AXES, 0, 0, tiled=True)
    own = received[:, ROWS_Q : ROWS_Q + 2 * ROWS_M, :]

    def shift(array, by):
        return lax.ppermute(array, "x", [(i, (i + by) % NX) for i in range(NX)])

    def swap(array):
        return lax.ppermute(array, "c", [(0, 1), (1, 0)])

    place = jnp.stack([lax.axis_index("x"), lax.axis_index("c"), lax.axis_index("h")]).astype(jnp.int32)
    left = shift(own, 1)
    right = shift(own, 3)
    opposite = shift(own, 2)
    own_far = swap(own)
    bias = make_bias(place, received[:, ROWS_Q + 2 * ROWS_M :, :], pattern)
    state = attend(0, received, bias, (own, own_far), None)
    left, right, *state = lax.optimization_barrier((left, right, *state))
    left_far = swap(left)
    right_far = swap(right)
    state = attend(1, received, bias, (left, left_far), state)
    opposite, *state = lax.optimization_barrier((opposite, *state))
    state = attend(2, received, bias, (right, right_far), state)
    state = attend(3, received, bias, (opposite, swap(opposite)), state)
    recalled = lax.all_to_all(state, B_AXES, 0, 0, tiled=True)

    def plane_shift(array, by):
        return lax.ppermute(array, "h", [(i, (i + by) % NH) for i in range(NH)])

    top, bottom, up, up_free, down, down_free, here = project(place, gate_bias, recalled, own_values, w_out)
    top = plane_shift(top, 1)
    bottom = plane_shift(bottom, 3)
    up_free = plane_shift(up_free, 1)
    down_free = plane_shift(down_free, 3)
    up, down = add_pairs(up, top, down, bottom)
    up = plane_shift(up, 1)
    down = plane_shift(down, 3)
    return finish(here, up, up_free, down, down_free)


def solution(mesh):
    fine = Mesh(mesh.devices.reshape(NX, 2, 4, NC, 4), ("x", "zl", "y", "c", "h"))
    mem = ("x", "zl", "y", "c")
    in_specs = (
        P(mem, "h"),
        P(mem, "h"),
        P(mem, "h"),
        P(mem, "h"),
        P("h"),
        P("h", None),
        P(mem, None),
        P(),
    )
    return jax.shard_map(local, mesh=fine, in_specs=in_specs, out_specs=P((*mem, "h"), None), check_vma=False)
```

profile of v0, /device:TPU:8, one launch (start us, length us, event | category | flops | bytes accessed | tf_op | source)
XLA Modules:
  0.0 91.6 jit_solution(2548970456029533519)
XLA Ops:
  0.0 0.0 copy-start.2
  0.0 0.7 copy-done.2
  0.7 1.3 %pack.1 = bf16[8,352,128]{2,1,0:T(8,128)(2,1)S(1)} custom-call(bf16[128,1024]{1,0:T(8,128)(2,1)} %q_ref.1, bf16[96,1024]{1,0:T(8,128)(2,1)} %k_ref.1, bf16[96,1024]{1,0:T(8,128)(2,1)} %v_ref.1, s32[8,128]{1,0:T(8,128)S(1)} %bitcast.6), custom_call_target="tpu_custom_call" | custom-call | tf_op jit(solution)/shard_map/pack/pallas_call | solution.py:264
  2.0 16.7 %all_to_all.10.refs_0_ = bf16[8,352,128]{2,1,0:T(8,128)(2,1)S(1)} all-to-all(bf16[8,352,128]{2,1,0:T(8,128)(2,1)S(1)} %pack.1), channel_id=1, replica_groups=mesh['x'=4,'zl'=2,'y'=4,'c'=2,'h'=4] {'zl','y'}, dimensions={0} | all-to-all | bytes 1441792 | tf_op jit(solution)/shard_map/all_to_all | solution.py:276
  18.6 0.1 collective-permute-start.3
  18.7 2.8 %collective-permute-start.2 = (bf16[8,192,128]{2,1,0:T(8,128)(2,1)S(1)}, bf16[8,192,128]{2,1,0:T(8,128)(2,1)S(1)}, u32[]{:S(2)}, u32[]{:S(2)}) collective-permute-start(bf16[8,192,128]{2,1,0:T(8,128)(2,1)S(1)} %slice.9.refs_2_), channel_id=1, source_target_pairs={{0,192},{64,0},{128,64},{192,128},{1,193},{65,1},{129,65},{193,129... | collective-permute-start | bytes 1179656 | tf_op jit(solution)/shard_map/ppermute | solution.py:280
  21.6 0.0 collective-permute-start.1
  21.6 0.1 pad_add_fusion.place_ref
  21.7 0.0 copy-start.1
  21.7 0.8 copy-done.1
  22.4 0.0 slice-start
  22.4 0.0 copy-start
  22.4 2.4 %bias.1.refs_1_ = bf16[4,1024,128]{2,1,0:T(8,128)(2,1)S(1)} custom-call(s32[3]{0:T(128)S(1)} %pad_add_fusion.place_ref, bf16[8,32,128]{2,1,0:T(8,128)(2,1)S(1)} %slice.8.probe_ref, s32[64,64]{1,0:T(8,128)S(1)} %copy-done.1), custom_call_target="tpu_custom_call" | custom-call | tf_op jit(solution)/shard_map/bias/pallas_call | solution.py:76
  24.8 0.0 collective-permute-done.3.refs_3_
  24.8 1.9 %shard_map.82 = (f32[1024,128]{1,0:T(8,128)S(1)}, f32[1024,256]{1,0:T(8,128)S(1)}) custom-call(bf16[8,352,128]{2,1,0:T(8,128)(2,1)S(1)} %all_to_all.10.refs_0_, bf16[4,1024,128]{2,1,0:T(8,128)(2,1)S(1)} %bias.1.refs_1_, bf16[8,192,128]{2,1,0:T(8,128)(2,1)S(1)} %slice.9.refs_2_, bf16[8,192,128]{2,1,0:T(8,128)(2,1)S(1)} %collective-permute-done.3.refs_3_), custom_call_target="tpu_custom_call" | custom-call | flops 1048576 | bytes 1024 | tf_op jit(solution)/shard_map/pallas_call | solution.py:152
  26.7 3.9 %collective-permute-done.2.refs_2_ = bf16[8,192,128]{2,1,0:T(8,128)(2,1)S(1)} collective-permute-done((bf16[8,192,128]{2,1,0:T(8,128)(2,1)S(1)}, bf16[8,192,128]{2,1,0:T(8,128)(2,1)S(1)}, u32[]{:S(2)}, u32[]{:S(2)}) %collective-permute-start.2) | collective-permute-done | bytes 393248 | tf_op jit(solution)/shard_map/ppermute | solution.py:280
  30.5 3.4 %collective-permute-done.1.refs_2_ = bf16[8,192,128]{2,1,0:T(8,128)(2,1)S(1)} collective-permute-done((bf16[8,192,128]{2,1,0:T(8,128)(2,1)S(1)}, bf16[8,192,128]{2,1,0:T(8,128)(2,1)S(1)}, u32[]{:S(2)}, u32[]{:S(2)}) %collective-permute-start.1) | collective-permute-done | bytes 393248 | tf_op jit(solution)/shard_map/ppermute | solution.py:280
  34.0 0.0 collective-permute-start.4
  34.0 0.0 collective-permute-start
  34.0 0.5 collective-permute-start.6
  34.5 1.2 %collective-permute-done.4.refs_3_ = bf16[8,192,128]{2,1,0:T(8,128)(2,1)S(1)} collective-permute-done((bf16[8,192,128]{2,1,0:T(8,128)(2,1)S(1)}, bf16[8,192,128]{2,1,0:T(8,128)(2,1)S(1)}, u32[]{:S(2)}, u32[]{:S(2)}) %collective-permute-start.4) | collective-permute-done | bytes 393248 | tf_op jit(solution)/shard_map/ppermute | solution.py:283
  35.7 2.1 %shard_map.83 = (f32[1024,128]{1,0:T(8,128)S(1)}, f32[1024,256]{1,0:T(8,128)S(1)}) custom-call(bf16[8,352,128]{2,1,0:T(8,128)(2,1)S(1)} %all_to_all.10.refs_0_, bf16[4,1024,128]{2,1,0:T(8,128)(2,1)S(1)} %bias.1.refs_1_, bf16[8,192,128]{2,1,0:T(8,128)(2,1)S(1)} %collective-permute-done.1.refs_2_, bf16[8,192,128]{2,1,0:T(8,128)(2,1)S(1)} %collective-permute-done.4.refs_3_, ...), custom_call_target="tpu_custom_call" | custom-call | flops 1048576 | bytes 1024 | tf_op jit(solution)/shard_map/pallas_call | solution.py:152
  37.8 9.2 %collective-permute-done.refs_2_ = bf16[8,192,128]{2,1,0:T(8,128)(2,1)S(1)} collective-permute-done((bf16[8,192,128]{2,1,0:T(8,128)(2,1)S(1)}, bf16[8,192,128]{2,1,0:T(8,128)(2,1)S(1)}, u32[]{:S(2)}, u32[]{:S(2)}) %collective-permute-start) | collective-permute-done | bytes 393248 | tf_op jit(solution)/shard_map/ppermute | solution.py:280
  47.0 0.0 collective-permute-start.5
  47.0 0.0 collective-permute-done.6.refs_3_
  47.0 2.1 %shard_map.84 = (f32[1024,128]{1,0:T(8,128)S(1)}, f32[1024,256]{1,0:T(8,128)S(1)}) custom-call(bf16[8,352,128]{2,1,0:T(8,128)(2,1)S(1)} %all_to_all.10.refs_0_, bf16[4,1024,128]{2,1,0:T(8,128)(2,1)S(1)} %bias.1.refs_1_, bf16[8,192,128]{2,1,0:T(8,128)(2,1)S(1)} %collective-permute-done.2.refs_2_, bf16[8,192,128]{2,1,0:T(8,128)(2,1)S(1)} %collective-permute-done.6.refs_3_, ...), custom_call_target="tpu_custom_call" | custom-call | flops 1048576 | bytes 1024 | tf_op jit(solution)/shard_map/pallas_call | solution.py:152
  49.1 0.0 collective-permute-done.5.refs_3_
  49.1 2.1 %shard_map.85 = bf16[8,128,128]{2,1,0:T(8,128)(2,1)S(1)} custom-call(bf16[8,352,128]{2,1,0:T(8,128)(2,1)S(1)} %all_to_all.10.refs_0_, bf16[4,1024,128]{2,1,0:T(8,128)(2,1)S(1)} %bias.1.refs_1_, bf16[8,192,128]{2,1,0:T(8,128)(2,1)S(1)} %collective-permute-done.refs_2_, bf16[8,192,128]{2,1,0:T(8,128)(2,1)S(1)} %collective-permute-done.5.refs_3_, ...), custom_call_target="tpu_custom_call" | custom-call | flops 1048576 | bytes 1024 | tf_op jit(solution)/shard_map/pallas_call | solution.py:152
  51.3 10.2 %all_to_all.11.rec_ref = bf16[8,128,128]{2,1,0:T(8,128)(2,1)S(1)} all-to-all(bf16[8,128,128]{2,1,0:T(8,128)(2,1)S(1)} %shard_map.85), channel_id=1, replica_groups=mesh['x'=4,'zl'=2,'y'=4,'c'=2,'h'=4] {'zl','y'}, dimensions={0} | all-to-all | bytes 524288 | tf_op jit(solution)/shard_map/all_to_all | solution.py:299
  61.5 0.0 slice-done
  61.5 0.0 copy-done
  61.5 0.0 copy-done.3
  61.5 0.0 slice-done.1
  61.5 1.8 %project.1 = (bf16[16,4096]{1,0:T(8,128)(2,1)S(1)}, bf16[16,4096]{1,0:T(8,128)(2,1)S(1)}, bf16[16,4096]{1,0:T(8,128)(2,1)S(1)}, bf16[16,4096]{1,0:T(8,128)(2,1)S...) custom-call(s32[3]{0:T(128)S(1)} %pad_add_fusion.place_ref, ...), custom_call_target="tpu_custom_call" | custom-call | flops 1073741824 | bytes 10485760 | tf_op jit(solution)/shard_map/project/pallas_call | solution.py:190
  63.4 3.4 %collective-permute-start.7 = (bf16[16,4096]{1,0:T(8,128)(2,1)S(1)}, bf16[16,4096]{1,0:T(8,128)(2,1)S(1)}, u32[]{:S(2)}, u32[]{:S(2)}) collective-permute-start(bf16[16,4096]{1,0:T(8,128)(2,1)S(1)} %get-tuple-element.42), channel_id=1, source_target_pairs={{0,1},{1,2},{2,3},{3,0},{4,5},{5,6},{6,7},{7,4},{8,9},{9,10},{10,1... | collective-permute-start | bytes 393224 | tf_op jit(solution)/shard_map/ppermute | solution.py:302
  66.7 2.2 %collective-permute-start.8 = (bf16[16,4096]{1,0:T(8,128)(2,1)S(1)}, bf16[16,4096]{1,0:T(8,128)(2,1)S(1)}, u32[]{:S(2)}, u32[]{:S(2)}) collective-permute-start(bf16[16,4096]{1,0:T(8,128)(2,1)S(1)} %get-tuple-element.44), channel_id=1, source_target_pairs={{0,3},{1,0},{2,1},{3,2},{4,7},{5,4},{6,5},{7,6},{8,11},{9,8},{10,9... | collective-permute-start | bytes 393224 | tf_op jit(solution)/shard_map/ppermute | solution.py:302
  69.0 1.4 %collective-permute-start.10 = (bf16[16,4096]{1,0:T(8,128)(2,1)S(1)}, bf16[16,4096]{1,0:T(8,128)(2,1)S(1)}, u32[]{:S(2)}, u32[]{:S(2)}) collective-permute-start(bf16[16,4096]{1,0:T(8,128)(2,1)S(1)} %get-tuple-element.46), channel_id=1, source_target_pairs={{0,1},{1,2},{2,3},{3,0},{4,5},{5,6},{6,7},{7,4},{8,9},{9,10},{10,1... | collective-permute-start | bytes 393224 | tf_op jit(solution)/shard_map/ppermute | solution.py:302
  70.3 2.8 %collective-permute-start.12 = (bf16[16,4096]{1,0:T(8,128)(2,1)S(1)}, bf16[16,4096]{1,0:T(8,128)(2,1)S(1)}, u32[]{:S(2)}, u32[]{:S(2)}) collective-permute-start(bf16[16,4096]{1,0:T(8,128)(2,1)S(1)} %get-tuple-element.48), channel_id=1, source_target_pairs={{0,3},{1,0},{2,1},{3,2},{4,7},{5,4},{6,5},{7,6},{8,11},{9,8},{10,9... | collective-permute-start | bytes 393224 | tf_op jit(solution)/shard_map/ppermute | solution.py:302
  73.1 0.0 collective-permute-done.7.b_ref
  73.1 6.2 %collective-permute-done.8.d_ref = bf16[16,4096]{1,0:T(8,128)(2,1)S(1)} collective-permute-done((bf16[16,4096]{1,0:T(8,128)(2,1)S(1)}, bf16[16,4096]{1,0:T(8,128)(2,1)S(1)}, u32[]{:S(2)}, u32[]{:S(2)}) %collective-permute-start.8) | collective-permute-done | bytes 131104 | tf_op jit(solution)/shard_map/ppermute | solution.py:302
  79.3 0.1 add_pairs.1
  79.3 5.0 %collective-permute-start.9 = (bf16[16,4096]{1,0:T(8,128)(2,1)S(1)}, bf16[16,4096]{1,0:T(8,128)(2,1)S(1)}, u32[]{:S(2)}, u32[]{:S(2)}) collective-permute-start(bf16[16,4096]{1,0:T(8,128)(2,1)S(1)} %get-tuple-element.45), channel_id=1, source_target_pairs={{0,1},{1,2},{2,3},{3,0},{4,5},{5,6},{6,7},{7,4},{8,9},{9,10},{10,1... | collective-permute-start | bytes 393224 | tf_op jit(solution)/shard_map/ppermute | solution.py:302
  84.3 0.0 collective-permute-start.11
  84.3 0.0 collective-permute-done.10.up_free_ref
  84.3 0.0 collective-permute-done.12.down_free_ref
  84.3 3.6 %collective-permute-done.9.up_ref = bf16[16,4096]{1,0:T(8,128)(2,1)S(1)} collective-permute-done((bf16[16,4096]{1,0:T(8,128)(2,1)S(1)}, bf16[16,4096]{1,0:T(8,128)(2,1)S(1)}, u32[]{:S(2)}, u32[]{:S(2)}) %collective-permute-start.9) | collective-permute-done | bytes 131104 | tf_op jit(solution)/shard_map/ppermute | solution.py:302
  87.9 2.9 %collective-permute-done.11.down_ref = bf16[16,4096]{1,0:T(8,128)(2,1)S(1)} collective-permute-done((bf16[16,4096]{1,0:T(8,128)(2,1)S(1)}, bf16[16,4096]{1,0:T(8,128)(2,1)S(1)}, u32[]{:S(2)}, u32[]{:S(2)}) %collective-permute-start.11) | collective-permute-done | bytes 131104 | tf_op jit(solution)/shard_map/ppermute | solution.py:302
  90.8 0.8 finish.1
  (5 shorter events, 0.0 us)
Async XLA Ops:
  0.0 0.7 copy-start.2
  18.6 6.1 %collective-permute-start.3 = (bf16[8,192,128]{2,1,0:T(8,128)(2,1)S(1)}, bf16[8,192,128]{2,1,0:T(8,128)(2,1)S(1)}, u32[]{:S(2)}, u32[]{:S(2)}) collective-permute-start(bf16[8,192,128]{2,1,0:T(8,128)(2,1)S(1)} %slice.9.refs_2_), channel_id=1, source_target_pairs={{0,4},{4,0},{1,5},{5,1},{2,6},{6,2},{3,7},{7,3},{8,12},{12,8},{9,1... | collective-permute-start | bytes 1179656 | tf_op jit(solution)/shard_map/ppermute | solution.py:283
  18.7 11.8 %collective-permute-start.2 = (bf16[8,192,128]{2,1,0:T(8,128)(2,1)S(1)}, bf16[8,192,128]{2,1,0:T(8,128)(2,1)S(1)}, u32[]{:S(2)}, u32[]{:S(2)}) collective-permute-start(bf16[8,192,128]{2,1,0:T(8,128)(2,1)S(1)} %slice.9.refs_2_), channel_id=1, source_target_pairs={{0,192},{64,0},{128,64},{192,128},{1,193},{65,1},{129,65},{193,129... | collective-permute-start | bytes 1179656 | tf_op jit(solution)/shard_map/ppermute | solution.py:280
  21.6 12.4 %collective-permute-start.1 = (bf16[8,192,128]{2,1,0:T(8,128)(2,1)S(1)}, bf16[8,192,128]{2,1,0:T(8,128)(2,1)S(1)}, u32[]{:S(2)}, u32[]{:S(2)}) collective-permute-start(bf16[8,192,128]{2,1,0:T(8,128)(2,1)S(1)} %slice.9.refs_2_), channel_id=1, source_target_pairs={{0,64},{64,128},{128,192},{192,0},{1,65},{65,129},{129,193},{193,1... | collective-permute-start | bytes 1179656 | tf_op jit(solution)/shard_map/ppermute | solution.py:280
  21.7 0.8 copy-start.1
  22.4 39.1 %slice-start = ((s8[8388608]{0:T(1024)(128)(4,1)}), s8[4194304]{0:T(1024)(128)(4,1)S(1)}, s32[]{:S(2)}) async-start(s8[8388608]{0:T(1024)(128)(4,1)} %bitcast.4), calls=%async_computation.2 | async-start | bytes 8388608
  22.4 39.1 %copy-start = (bf16[128,1024]{1,0:T(8,128)(2,1)S(1)}, bf16[128,1024]{1,0:T(8,128)(2,1)}, u32[]{:S(2)}) copy-start(bf16[128,1024]{1,0:T(8,128)(2,1)} %own_ref.1) | copy-start | bytes 786436
  22.4 39.1 %copy-start.3 = (f32[8]{0:T(128)S(1)}, f32[8]{0:T(128)}, u32[]{:S(2)}) copy-start(f32[8]{0:T(128)} %gate_ref.1) | copy-start | bytes 100
  34.0 1.7 %collective-permute-start.4 = (bf16[8,192,128]{2,1,0:T(8,128)(2,1)S(1)}, bf16[8,192,128]{2,1,0:T(8,128)(2,1)S(1)}, u32[]{:S(2)}, u32[]{:S(2)}) collective-permute-start(bf16[8,192,128]{2,1,0:T(8,128)(2,1)S(1)} %collective-permute-done.1.refs_2_), channel_id=1, source_target_pairs={{0,4},{4,0},{1,5},{5,1},{2,6},{6,2},{3,7},{7,3},{8,12},{12,8},{9,1... | collective-permute-start | bytes 1179656 | tf_op jit(solution)/shard_map/ppermute | solution.py:283
  34.0 13.0 %collective-permute-start = (bf16[8,192,128]{2,1,0:T(8,128)(2,1)S(1)}, bf16[8,192,128]{2,1,0:T(8,128)(2,1)S(1)}, u32[]{:S(2)}, u32[]{:S(2)}) collective-permute-start(bf16[8,192,128]{2,1,0:T(8,128)(2,1)S(1)} %slice.9.refs_2_), channel_id=1, source_target_pairs={{0,128},{64,192},{128,0},{192,64},{1,129},{65,193},{129,1},{193,65... | collective-permute-start | bytes 1179656 | tf_op jit(solution)/shard_map/ppermute | solution.py:280
  34.0 13.0 %collective-permute-start.6 = (bf16[8,192,128]{2,1,0:T(8,128)(2,1)S(1)}, bf16[8,192,128]{2,1,0:T(8,128)(2,1)S(1)}, u32[]{:S(2)}, u32[]{:S(2)}) collective-permute-start(bf16[8,192,128]{2,1,0:T(8,128)(2,1)S(1)} %collective-permute-done.2.refs_2_), channel_id=1, source_target_pairs={{0,4},{4,0},{1,5},{5,1},{2,6},{6,2},{3,7},{7,3},{8,12},{12,8},{9,1... | collective-permute-start | bytes 1179656 | tf_op jit(solution)/shard_map/ppermute | solution.py:283
  47.0 14.5 %slice-start.1 = ((s8[8388608]{0:T(1024)(128)(4,1)}), s8[4194304]{0:T(1024)(128)(4,1)S(1)}, s32[]{:S(2)}) async-start(s8[8388608]{0:T(1024)(128)(4,1)} %bitcast.4), calls=%async_computation.3 | async-start | bytes 8388608
  47.0 2.1 %collective-permute-start.5 = (bf16[8,192,128]{2,1,0:T(8,128)(2,1)S(1)}, bf16[8,192,128]{2,1,0:T(8,128)(2,1)S(1)}, u32[]{:S(2)}, u32[]{:S(2)}) collective-permute-start(bf16[8,192,128]{2,1,0:T(8,128)(2,1)S(1)} %collective-permute-done.refs_2_), channel_id=1, source_target_pairs={{0,4},{4,0},{1,5},{5,1},{2,6},{6,2},{3,7},{7,3},{8,12},{12,8},{9,1... | collective-permute-start | bytes 1179656 | tf_op jit(solution)/shard_map/ppermute | solution.py:283
  63.4 9.7 %collective-permute-start.7 = (bf16[16,4096]{1,0:T(8,128)(2,1)S(1)}, bf16[16,4096]{1,0:T(8,128)(2,1)S(1)}, u32[]{:S(2)}, u32[]{:S(2)}) collective-permute-start(bf16[16,4096]{1,0:T(8,128)(2,1)S(1)} %get-tuple-element.42), channel_id=1, source_target_pairs={{0,1},{1,2},{2,3},{3,0},{4,5},{5,6},{6,7},{7,4},{8,9},{9,10},{10,1... | collective-permute-start | bytes 393224 | tf_op jit(solution)/shard_map/ppermute | solution.py:302
  66.7 12.5 %collective-permute-start.8 = (bf16[16,4096]{1,0:T(8,128)(2,1)S(1)}, bf16[16,4096]{1,0:T(8,128)(2,1)S(1)}, u32[]{:S(2)}, u32[]{:S(2)}) collective-permute-start(bf16[16,4096]{1,0:T(8,128)(2,1)S(1)} %get-tuple-element.44), channel_id=1, source_target_pairs={{0,3},{1,0},{2,1},{3,2},{4,7},{5,4},{6,5},{7,6},{8,11},{9,8},{10,9... | collective-permute-start | bytes 393224 | tf_op jit(solution)/shard_map/ppermute | solution.py:302
  69.0 15.4 %collective-permute-start.10 = (bf16[16,4096]{1,0:T(8,128)(2,1)S(1)}, bf16[16,4096]{1,0:T(8,128)(2,1)S(1)}, u32[]{:S(2)}, u32[]{:S(2)}) collective-permute-start(bf16[16,4096]{1,0:T(8,128)(2,1)S(1)} %get-tuple-element.46), channel_id=1, source_target_pairs={{0,1},{1,2},{2,3},{3,0},{4,5},{5,6},{6,7},{7,4},{8,9},{9,10},{10,1... | collective-permute-start | bytes 393224 | tf_op jit(solution)/shard_map/ppermute | solution.py:302
  70.3 14.0 %collective-permute-start.12 = (bf16[16,4096]{1,0:T(8,128)(2,1)S(1)}, bf16[16,4096]{1,0:T(8,128)(2,1)S(1)}, u32[]{:S(2)}, u32[]{:S(2)}) collective-permute-start(bf16[16,4096]{1,0:T(8,128)(2,1)S(1)} %get-tuple-element.48), channel_id=1, source_target_pairs={{0,3},{1,0},{2,1},{3,2},{4,7},{5,4},{6,5},{7,6},{8,11},{9,8},{10,9... | collective-permute-start | bytes 393224 | tf_op jit(solution)/shard_map/ppermute | solution.py:302
  79.3 8.6 %collective-permute-start.9 = (bf16[16,4096]{1,0:T(8,128)(2,1)S(1)}, bf16[16,4096]{1,0:T(8,128)(2,1)S(1)}, u32[]{:S(2)}, u32[]{:S(2)}) collective-permute-start(bf16[16,4096]{1,0:T(8,128)(2,1)S(1)} %get-tuple-element.45), channel_id=1, source_target_pairs={{0,1},{1,2},{2,3},{3,0},{4,5},{5,6},{6,7},{7,4},{8,9},{9,10},{10,1... | collective-permute-start | bytes 393224 | tf_op jit(solution)/shard_map/ppermute | solution.py:302
  84.3 6.5 %collective-permute-start.11 = (bf16[16,4096]{1,0:T(8,128)(2,1)S(1)}, bf16[16,4096]{1,0:T(8,128)(2,1)S(1)}, u32[]{:S(2)}, u32[]{:S(2)}) collective-permute-start(bf16[16,4096]{1,0:T(8,128)(2,1)S(1)} %get-tuple-element.47), channel_id=1, source_target_pairs={{0,3},{1,0},{2,1},{3,2},{4,7},{5,4},{6,5},{7,6},{8,11},{9,8},{10,9... | collective-permute-start | bytes 393224 | tf_op jit(solution)/shard_map/ppermute | solution.py:302
where the time goes:
time: 92 us; the launch traced here: 91.6 us
  waiting for transfers between devices  30.4 us (33%)
  blocking collectives  26.9 us (29%)
  starting transfers between devices  18.1 us (20%)
  Pallas kernels  14.5 us (16%)
  local copies, waits for them, and re-layouts  1.49 us (2%)
    all_to_all x1, blocking collectives, local(): lax.all_to_all(pack(queries, mem_keys, mem_values, probes.T), B_AXES, 0,...  16.7 us
    ppermute x3, waiting for transfers between devices, shift(): return lax.ppermute(array, 'x', [(i, (i + by) % NX) for i in range(NX)])  16.5 us
    ppermute x6, starting transfers between devices, plane_shift(): return lax.ppermute(array, 'h', [(i, (i + by) % NH) for i in range(NH)])  14.7 us
    ppermute x6, waiting for transfers between devices, plane_shift(): return lax.ppermute(array, 'h', [(i, (i + by) % NH) for i in range(NH)])  12.7 us
    all_to_all x1, blocking collectives, local(): recalled = lax.all_to_all(state, B_AXES, 0, 0, tiled=True)  10.2 us
    pallas_call x4, Pallas kernels, attend(): pl.pallas_call(lambda *refs: chunk_body(k, parts, *refs), in_specs=[VMEM_...  8.24 us
    ppermute x3, starting transfers between devices, shift(): return lax.ppermute(array, 'x', [(i, (i + by) % NX) for i in range(NX)])  2.84 us
    pallas_call x1, Pallas kernels, make_bias(): pl.pallas_call(bias_body, in_specs=[SMEM_SPEC, VMEM_SPEC, VMEM_SPEC], out...  2.35 us
  transfers between devices with their start and end apart: 13, of which 7 were waited for; matrix products, arithmetic and copies ran while one was open for 0% of the time, Pallas kernels for 9%

commit v1 on v0

--- a/solution.py
+++ b/solution.py
@@ -16,7 +16,7 @@
 
 B_AXES = ("zl", "y")
 NX, NB, NC, NH = 4, 8, 2, 4
-ROWS_Q, ROWS_M, ROWS_P, ROWS_O = 128, 96, 32, 32
+ROWS_Q, ROWS_M, ROWS_P, ROWS_O = 128, 96, 16, 32
 NQ = NB * ROWS_Q
 HALF = NB * ROWS_M
 OFFSETS = (0, 3, 1, 2)
@@ -58,8 +58,9 @@
         targets.append((lane + lax.rem(x + offset, NX) * 128).astype(jnp.float32))
     for b in range(NB):
         coded = probe_ref[b].astype(jnp.float32)
-        code = coded[0:8] * 128.0 + coded[8:16]
-        code = code + jnp.where(coded[16:24] == core.astype(jnp.float32), 0.0, float(per_slot))
+        source_x = jnp.floor(coded[0:8] * (1.0 / NC))
+        code = source_x * 128.0 + coded[8:16]
+        code = code + jnp.where(coded[0:8] - NC * source_x == core.astype(jnp.float32), 0.0, float(per_slot))
         code = jnp.concatenate([code] * 16, axis=0).T
         for row in range(0, ROWS_Q, 32):
             live = [jnp.full((32, 128), NEG, jnp.float32)] * NX
@@ -198,20 +199,17 @@
     )(place, gate_bias, in_vmem(recalled), in_vmem(own_values), in_vmem(w_out))
 
 
-def add_body(a_ref, b_ref, c_ref, d_ref, up_ref, down_ref):
-    up_ref[...] = (a_ref[...].astype(jnp.float32) + b_ref[...].astype(jnp.float32)).astype(jnp.bfloat16)
-    down_ref[...] = (c_ref[...].astype(jnp.float32) + d_ref[...].astype(jnp.float32)).astype(jnp.bfloat16)
-
-
-def add_pairs(*args):
-    half = pltpu.VMEM(args[0].shape, jnp.bfloat16)
+def add_body(a_ref, b_ref, out_ref):
+    out_ref[...] = (a_ref[...].astype(jnp.float32) + b_ref[...].astype(jnp.float32)).astype(jnp.bfloat16)
+
+
+def add(*args):
     return pl.pallas_call(
         add_body,
-        in_specs=[VMEM_SPEC] * 4,
-        out_specs=[VMEM_SPEC] * 2,
-        out_shape=[half] * 2,
-        compiler_params=pltpu.CompilerParams(vmem_limit_bytes=16 << 20),
-        name="add_pairs",
+        in_specs=[VMEM_SPEC] * 2,
+        out_specs=VMEM_SPEC,
+        out_shape=pltpu.VMEM(args[0].shape, jnp.bfloat16),
+        compiler_params=pltpu.CompilerParams(vmem_limit_bytes=16 << 20),
     )(*[in_vmem(arg) for arg in args])
 
 
@@ -232,7 +230,9 @@
     )(*[in_vmem(arg) for arg in args])
 
 
-def pack_body(q_ref, k_ref, v_ref, probe_ref, out_ref, sems):
+def pack_body(q_ref, k_ref, v_ref, probe_hbm, out_ref, probe_ref, sems):
+    probe_copy = pltpu.make_async_copy(probe_hbm, probe_ref, sems.at[3 * NB])
+    probe_copy.start()
     copies = []
     for h in range(NB):
         span = slice(h * HD, (h + 1) * HD)
@@ -244,6 +244,7 @@
             row += size
     for copy in copies:
         copy.start()
+    probe_copy.wait()
     per_block = ROWS_M // CSIZE
     number = probe_ref[...].astype(jnp.float32)
     block = jnp.floor((number + 0.5) * (1.0 / per_block))
@@ -251,7 +252,7 @@
     pair = jnp.floor(block * (1.0 / NC))
     source_x = jnp.floor(block * (1.0 / (NC * NB)))
     column = (pair - NB * source_x) * per_block + rest
-    coded = jnp.concatenate([source_x, column, block - NC * pair, jnp.zeros_like(block)], axis=0)
+    coded = jnp.concatenate([source_x * NC + block - NC * pair, column], axis=0)
     coded = coded.astype(jnp.bfloat16)
     for h in range(NB):
         out_ref[h, ROWS_Q + 2 * ROWS_M :, :] = coded
@@ -263,13 +264,13 @@
     anywhere = pl.BlockSpec(memory_space=pltpu.HBM)
     return pl.pallas_call(
         pack_body,
-        in_specs=[anywhere, anywhere, anywhere, VMEM_SPEC],
+        in_specs=[anywhere] * 4,
         out_specs=VMEM_SPEC,
         out_shape=pltpu.VMEM((NB, ROWS_Q + 2 * ROWS_M + ROWS_P, HD), jnp.bfloat16),
-        scratch_shapes=[pltpu.SemaphoreType.DMA((3 * NB,))],
+        scratch_shapes=[pltpu.VMEM(probe_rows.shape, probe_rows.dtype), pltpu.SemaphoreType.DMA((3 * NB + 1,))],
         compiler_params=pltpu.CompilerParams(vmem_limit_bytes=16 << 20),
         name="pack",
-    )(*[pltpu.with_memory_space_constraint(a, pltpu.HBM) for a in (queries, mem_keys, mem_values)], probe_rows)
+    )(*[pltpu.with_memory_space_constraint(a, pltpu.HBM) for a in (queries, mem_keys, mem_values, probe_rows)])
 
 
 def local(queries, mem_keys, mem_values, own_values, gate_bias, w_out, probes, pattern):
@@ -306,9 +307,8 @@
     bottom = plane_shift(bottom, 3)
     up_free = plane_shift(up_free, 1)
     down_free = plane_shift(down_free, 3)
-    up, down = add_pairs(up, top, down, bottom)
-    up = plane_shift(up, 1)
-    down = plane_shift(down, 3)
+    up = plane_shift(add(up, top), 1)
+    down = plane_shift(add(down, bottom), 3)
     return finish(here, up, up_free, down, down_free)
 
 
@@ -325,4 +325,5 @@
         P(mem, None),
         P(),
     )
+
     return jax.shard_map(local, mesh=fine, in_specs=in_specs, out_specs=P((*mem, "h"), None), check_vma=False)

time: 92 us -> 90.7 us (0.986)
  the two profiles are of different devices: /device:TPU:8 before, /device:TPU:72 now
where the time goes in v1:
time: 90.7 us; the launch traced here: 90.5 us
  waiting for transfers between devices  32 us (35%)
  blocking collectives  26.5 us (29%)
  starting transfers between devices  16.2 us (18%)
  Pallas kernels  14.6 us (16%)
  local copies, waits for them, and re-layouts  0.95 us (1%)
    all_to_all x1, blocking collectives, local(): lax.all_to_all(pack(queries, mem_keys, mem_values, probes.T), B_AXES, 0,...  16.3 us
    ppermute x3, waiting for transfers between devices, shift(): return lax.ppermute(array, 'x', [(i, (i + by) % NX) for i in range(NX)])  16.3 us
    ppermute x6, waiting for transfers between devices, plane_shift(): return lax.ppermute(array, 'h', [(i, (i + by) % NH) for i in range(NH)])  14.5 us
    ppermute x6, starting transfers between devices, plane_shift(): return lax.ppermute(array, 'h', [(i, (i + by) % NH) for i in range(NH)])  12.7 us
    all_to_all x1, blocking collectives, local(): recalled = lax.all_to_all(state, B_AXES, 0, 0, tiled=True)  10.2 us
    pallas_call x4, Pallas kernels, attend(): pl.pallas_call(lambda *refs: chunk_body(k, parts, *refs), in_specs=[VMEM_...  8.25 us
    ppermute x3, starting transfers between devices, shift(): return lax.ppermute(array, 'x', [(i, (i + by) % NX) for i in range(NX)])  2.84 us
    pallas_call x1, Pallas kernels, make_bias(): pl.pallas_call(bias_body, in_specs=[SMEM_SPEC, VMEM_SPEC, VMEM_SPEC], out...  2.35 us
  transfers between devices with their start and end apart: 13, of which 7 were waited for; matrix products, arithmetic and copies ran while one was open for 0% of the time, Pallas kernels for 9%

profile of v1, /device:TPU:72, one launch (start us, length us, event | category | flops | bytes accessed | tf_op | source)
XLA Modules:
  0.0 90.5 jit_solution(9136953631757768929)
XLA Ops:
  0.0 1.3 %pack.1 = bf16[8,336,128]{2,1,0:T(8,128)(2,1)S(1)} custom-call(bf16[128,1024]{1,0:T(8,128)(2,1)} %q_ref.1, bf16[96,1024]{1,0:T(8,128)(2,1)} %k_ref.1, bf16[96,1024]{1,0:T(8,128)(2,1)} %v_ref.1, s32[8,128]{1,0:T(8,128)} %bitcast.6), custom_call_target="tpu_custom_call" | custom-call | tf_op jit(solution)/shard_map/pack/pallas_call | solution.py:265
  1.3 16.3 %all_to_all.10.refs_0_ = bf16[8,336,128]{2,1,0:T(8,128)(2,1)S(1)} all-to-all(bf16[8,336,128]{2,1,0:T(8,128)(2,1)S(1)} %pack.1), channel_id=1, replica_groups=mesh['x'=4,'zl'=2,'y'=4,'c'=2,'h'=4] {'zl','y'}, dimensions={0} | all-to-all | bytes 1376256 | tf_op jit(solution)/shard_map/all_to_all | solution.py:277
  17.7 0.1 collective-permute-start.3
  17.8 2.8 %collective-permute-start.2 = (bf16[8,192,128]{2,1,0:T(8,128)(2,1)S(1)}, bf16[8,192,128]{2,1,0:T(8,128)(2,1)S(1)}, u32[]{:S(2)}, u32[]{:S(2)}) collective-permute-start(bf16[8,192,128]{2,1,0:T(8,128)(2,1)S(1)} %slice.9.refs_2_), channel_id=1, source_target_pairs={{0,192},{64,0},{128,64},{192,128},{1,193},{65,1},{129,65},{193,129... | collective-permute-start | bytes 1179656 | tf_op jit(solution)/shard_map/ppermute | solution.py:281
  20.6 0.0 collective-permute-start.1
  20.6 0.1 pad_add_fusion.place_ref
  20.7 0.0 slice-start
  20.7 0.0 copy-start
  20.7 0.0 copy-start.1
  20.7 0.9 copy-done.1
  21.6 0.0 copy-start.2
  21.6 2.4 %bias.1.refs_1_ = bf16[4,1024,128]{2,1,0:T(8,128)(2,1)S(1)} custom-call(s32[3]{0:T(128)S(1)} %pad_add_fusion.place_ref, bf16[8,16,128]{2,1,0:T(8,128)(2,1)S(1)} %slice.8.probe_ref, s32[64,64]{1,0:T(8,128)S(1)} %copy-done.1), custom_call_target="tpu_custom_call" | custom-call | tf_op jit(solution)/shard_map/bias/pallas_call | solution.py:77
  24.0 0.0 collective-permute-done.3.refs_3_
  24.0 1.9 %shard_map.82 = (f32[1024,128]{1,0:T(8,128)S(1)}, f32[1024,256]{1,0:T(8,128)S(1)}) custom-call(bf16[8,336,128]{2,1,0:T(8,128)(2,1)S(1)} %all_to_all.10.refs_0_, bf16[4,1024,128]{2,1,0:T(8,128)(2,1)S(1)} %bias.1.refs_1_, bf16[8,192,128]{2,1,0:T(8,128)(2,1)S(1)} %slice.9.refs_2_, bf16[8,192,128]{2,1,0:T(8,128)(2,1)S(1)} %collective-permute-done.3.refs_3_), custom_call_target="tpu_custom_call" | custom-call | flops 1048576 | bytes 1024 | tf_op jit(solution)/shard_map/pallas_call | solution.py:153
  25.9 3.7 %collective-permute-done.2.refs_2_ = bf16[8,192,128]{2,1,0:T(8,128)(2,1)S(1)} collective-permute-done((bf16[8,192,128]{2,1,0:T(8,128)(2,1)S(1)}, bf16[8,192,128]{2,1,0:T(8,128)(2,1)S(1)}, u32[]{:S(2)}, u32[]{:S(2)}) %collective-permute-start.2) | collective-permute-done | bytes 393248 | tf_op jit(solution)/shard_map/ppermute | solution.py:281
  29.6 3.4 %collective-permute-done.1.refs_2_ = bf16[8,192,128]{2,1,0:T(8,128)(2,1)S(1)} collective-permute-done((bf16[8,192,128]{2,1,0:T(8,128)(2,1)S(1)}, bf16[8,192,128]{2,1,0:T(8,128)(2,1)S(1)}, u32[]{:S(2)}, u32[]{:S(2)}) %collective-permute-start.1) | collective-permute-done | bytes 393248 | tf_op jit(solution)/shard_map/ppermute | solution.py:281
  33.0 0.0 collective-permute-start.4
  33.0 0.0 collective-permute-start
  33.0 0.5 collective-permute-start.6
  33.5 1.2 %collective-permute-done.4.refs_3_ = bf16[8,192,128]{2,1,0:T(8,128)(2,1)S(1)} collective-permute-done((bf16[8,192,128]{2,1,0:T(8,128)(2,1)S(1)}, bf16[8,192,128]{2,1,0:T(8,128)(2,1)S(1)}, u32[]{:S(2)}, u32[]{:S(2)}) %collective-permute-start.4) | collective-permute-done | bytes 393248 | tf_op jit(solution)/shard_map/ppermute | solution.py:284
  34.7 2.1 %shard_map.83 = (f32[1024,128]{1,0:T(8,128)S(1)}, f32[1024,256]{1,0:T(8,128)S(1)}) custom-call(bf16[8,336,128]{2,1,0:T(8,128)(2,1)S(1)} %all_to_all.10.refs_0_, bf16[4,1024,128]{2,1,0:T(8,128)(2,1)S(1)} %bias.1.refs_1_, bf16[8,192,128]{2,1,0:T(8,128)(2,1)S(1)} %collective-permute-done.1.refs_2_, bf16[8,192,128]{2,1,0:T(8,128)(2,1)S(1)} %collective-permute-done.4.refs_3_, ...), custom_call_target="tpu_custom_call" | custom-call | flops 1048576 | bytes 1024 | tf_op jit(solution)/shard_map/pallas_call | solution.py:153
  36.8 9.2 %collective-permute-done.refs_2_ = bf16[8,192,128]{2,1,0:T(8,128)(2,1)S(1)} collective-permute-done((bf16[8,192,128]{2,1,0:T(8,128)(2,1)S(1)}, bf16[8,192,128]{2,1,0:T(8,128)(2,1)S(1)}, u32[]{:S(2)}, u32[]{:S(2)}) %collective-permute-start) | collective-permute-done | bytes 393248 | tf_op jit(solution)/shard_map/ppermute | solution.py:281
  46.0 0.0 slice-start.1
  46.0 0.0 collective-permute-start.5
  46.0 0.0 collective-permute-done.6.refs_3_
  46.0 2.1 %shard_map.84 = (f32[1024,128]{1,0:T(8,128)S(1)}, f32[1024,256]{1,0:T(8,128)S(1)}) custom-call(bf16[8,336,128]{2,1,0:T(8,128)(2,1)S(1)} %all_to_all.10.refs_0_, bf16[4,1024,128]{2,1,0:T(8,128)(2,1)S(1)} %bias.1.refs_1_, bf16[8,192,128]{2,1,0:T(8,128)(2,1)S(1)} %collective-permute-done.2.refs_2_, bf16[8,192,128]{2,1,0:T(8,128)(2,1)S(1)} %collective-permute-done.6.refs_3_, ...), custom_call_target="tpu_custom_call" | custom-call | flops 1048576 | bytes 1024 | tf_op jit(solution)/shard_map/pallas_call | solution.py:153
  48.2 0.0 collective-permute-done.5.refs_3_
  48.2 2.1 %shard_map.85 = bf16[8,128,128]{2,1,0:T(8,128)(2,1)S(1)} custom-call(bf16[8,336,128]{2,1,0:T(8,128)(2,1)S(1)} %all_to_all.10.refs_0_, bf16[4,1024,128]{2,1,0:T(8,128)(2,1)S(1)} %bias.1.refs_1_, bf16[8,192,128]{2,1,0:T(8,128)(2,1)S(1)} %collective-permute-done.refs_2_, bf16[8,192,128]{2,1,0:T(8,128)(2,1)S(1)} %collective-permute-done.5.refs_3_, ...), custom_call_target="tpu_custom_call" | custom-call | flops 1048576 | bytes 1024 | tf_op jit(solution)/shard_map/pallas_call | solution.py:153
  50.3 10.2 %all_to_all.11.rec_ref = bf16[8,128,128]{2,1,0:T(8,128)(2,1)S(1)} all-to-all(bf16[8,128,128]{2,1,0:T(8,128)(2,1)S(1)} %shard_map.85), channel_id=1, replica_groups=mesh['x'=4,'zl'=2,'y'=4,'c'=2,'h'=4] {'zl','y'}, dimensions={0} | all-to-all | bytes 524288 | tf_op jit(solution)/shard_map/all_to_all | solution.py:300
  60.5 0.0 slice-done
  60.5 0.0 copy-done
  60.5 0.0 copy-done.2
  60.5 0.0 slice-done.1
  60.5 1.8 %project.1 = (bf16[16,4096]{1,0:T(8,128)(2,1)S(1)}, bf16[16,4096]{1,0:T(8,128)(2,1)S(1)}, bf16[16,4096]{1,0:T(8,128)(2,1)S(1)}, bf16[16,4096]{1,0:T(8,128)(2,1)S...) custom-call(s32[3]{0:T(128)S(1)} %pad_add_fusion.place_ref, ...), custom_call_target="tpu_custom_call" | custom-call | flops 1073741824 | bytes 10485760 | tf_op jit(solution)/shard_map/project/pallas_call | solution.py:191
  62.4 3.7 %collective-permute-start.7 = (bf16[16,4096]{1,0:T(8,128)(2,1)S(1)}, bf16[16,4096]{1,0:T(8,128)(2,1)S(1)}, u32[]{:S(2)}, u32[]{:S(2)}) collective-permute-start(bf16[16,4096]{1,0:T(8,128)(2,1)S(1)} %get-tuple-element.40), channel_id=1, source_target_pairs={{0,1},{1,2},{2,3},{3,0},{4,5},{5,6},{6,7},{7,4},{8,9},{9,10},{10,1... | collective-permute-start | bytes 393224 | tf_op jit(solution)/shard_map/ppermute | solution.py:303
  66.0 0.0 collective-permute-start.10
  66.0 4.1 %collective-permute-start.9 = (bf16[16,4096]{1,0:T(8,128)(2,1)S(1)}, bf16[16,4096]{1,0:T(8,128)(2,1)S(1)}, u32[]{:S(2)}, u32[]{:S(2)}) collective-permute-start(bf16[16,4096]{1,0:T(8,128)(2,1)S(1)} %get-tuple-element.41), channel_id=1, source_target_pairs={{0,1},{1,2},{2,3},{3,0},{4,5},{5,6},{6,7},{7,4},{8,9},{9,10},{10,1... | collective-permute-start | bytes 393224 | tf_op jit(solution)/shard_map/ppermute | solution.py:303
  70.2 0.0 collective-permute-start.12
  70.2 0.0 collective-permute-done.7.b_ref
  70.2 4.9 %collective-permute-start.8 = (bf16[16,4096]{1,0:T(8,128)(2,1)S(1)}, bf16[16,4096]{1,0:T(8,128)(2,1)S(1)}, u32[]{:S(2)}, u32[]{:S(2)}) collective-permute-start(bf16[16,4096]{1,0:T(8,128)(2,1)S(1)} %shard_map.86), channel_id=1, source_target_pairs={{0,1},{1,2},{2,3},{3,0},{4,5},{5,6},{6,7},{7,4},{8,9},{9,10},{10,1... | collective-permute-start | bytes 393224 | tf_op jit(solution)/shard_map/ppermute | solution.py:303
  75.1 4.8 %collective-permute-done.10.b_ref = bf16[16,4096]{1,0:T(8,128)(2,1)S(1)} collective-permute-done((bf16[16,4096]{1,0:T(8,128)(2,1)S(1)}, bf16[16,4096]{1,0:T(8,128)(2,1)S(1)}, u32[]{:S(2)}, u32[]{:S(2)}) %collective-permute-start.10) | collective-permute-done | bytes 131104 | tf_op jit(solution)/shard_map/ppermute | solution.py:303
  79.9 0.1 collective-permute-start.11
  79.9 0.0 collective-permute-done.9.up_free_ref
  80.0 2.8 %collective-permute-done.12.down_free_ref = bf16[16,4096]{1,0:T(8,128)(2,1)S(1)} collective-permute-done((bf16[16,4096]{1,0:T(8,128)(2,1)S(1)}, bf16[16,4096]{1,0:T(8,128)(2,1)S(1)}, u32[]{:S(2)}, u32[]{:S(2)}) %collective-permute-start.12) | collective-permute-done | bytes 131104 | tf_op jit(solution)/shard_map/ppermute | solution.py:303
  82.7 0.0 collective-permute-done.8.up_ref
  82.7 6.9 %collective-permute-done.11.down_ref = bf16[16,4096]{1,0:T(8,128)(2,1)S(1)} collective-permute-done((bf16[16,4096]{1,0:T(8,128)(2,1)S(1)}, bf16[16,4096]{1,0:T(8,128)(2,1)S(1)}, u32[]{:S(2)}, u32[]{:S(2)}) %collective-permute-start.11) | collective-permute-done | bytes 131104 | tf_op jit(solution)/shard_map/ppermute | solution.py:303
  89.7 0.8 finish.1
  (5 shorter events, 0.1 us)
Async XLA Ops:
  17.7 6.3 %collective-permute-start.3 = (bf16[8,192,128]{2,1,0:T(8,128)(2,1)S(1)}, bf16[8,192,128]{2,1,0:T(8,128)(2,1)S(1)}, u32[]{:S(2)}, u32[]{:S(2)}) collective-permute-start(bf16[8,192,128]{2,1,0:T(8,128)(2,1)S(1)} %slice.9.refs_2_), channel_id=1, source_target_pairs={{0,4},{4,0},{1,5},{5,1},{2,6},{6,2},{3,7},{7,3},{8,12},{12,8},{9,1... | collective-permute-start | bytes 1179656 | tf_op jit(solution)/shard_map/ppermute | solution.py:284
  17.8 11.8 %collective-permute-start.2 = (bf16[8,192,128]{2,1,0:T(8,128)(2,1)S(1)}, bf16[8,192,128]{2,1,0:T(8,128)(2,1)S(1)}, u32[]{:S(2)}, u32[]{:S(2)}) collective-permute-start(bf16[8,192,128]{2,1,0:T(8,128)(2,1)S(1)} %slice.9.refs_2_), channel_id=1, source_target_pairs={{0,192},{64,0},{128,64},{192,128},{1,193},{65,1},{129,65},{193,129... | collective-permute-start | bytes 1179656 | tf_op jit(solution)/shard_map/ppermute | solution.py:281
  20.6 12.4 %collective-permute-start.1 = (bf16[8,192,128]{2,1,0:T(8,128)(2,1)S(1)}, bf16[8,192,128]{2,1,0:T(8,128)(2,1)S(1)}, u32[]{:S(2)}, u32[]{:S(2)}) collective-permute-start(bf16[8,192,128]{2,1,0:T(8,128)(2,1)S(1)} %slice.9.refs_2_), channel_id=1, source_target_pairs={{0,64},{64,128},{128,192},{192,0},{1,65},{65,129},{129,193},{193,1... | collective-permute-start | bytes 1179656 | tf_op jit(solution)/shard_map/ppermute | solution.py:281
  20.7 39.8 %slice-start = ((s8[8388608]{0:T(1024)(128)(4,1)}), s8[4194304]{0:T(1024)(128)(4,1)S(1)}, s32[]{:S(2)}) async-start(s8[8388608]{0:T(1024)(128)(4,1)} %bitcast.4), calls=%async_computation.2 | async-start | bytes 8388608
  20.7 39.8 %copy-start = (bf16[128,1024]{1,0:T(8,128)(2,1)S(1)}, bf16[128,1024]{1,0:T(8,128)(2,1)}, u32[]{:S(2)}) copy-start(bf16[128,1024]{1,0:T(8,128)(2,1)} %own_ref.1) | copy-start | bytes 786436
  20.7 0.9 %copy-start.1 = (s32[64,64]{1,0:T(8,128)S(1)}, s32[64,64]{1,0:T(8,128)}, u32[]{:S(2)}) copy-start(s32[64,64]{1,0:T(8,128)} %pattern_ref.1) | copy-start | bytes 49156
  21.6 38.9 %copy-start.2 = (f32[8]{0:T(128)S(1)}, f32[8]{0:T(128)}, u32[]{:S(2)}) copy-start(f32[8]{0:T(128)} %gate_ref.1) | copy-start | bytes 100
  33.0 1.7 %collective-permute-start.4 = (bf16[8,192,128]{2,1,0:T(8,128)(2,1)S(1)}, bf16[8,192,128]{2,1,0:T(8,128)(2,1)S(1)}, u32[]{:S(2)}, u32[]{:S(2)}) collective-permute-start(bf16[8,192,128]{2,1,0:T(8,128)(2,1)S(1)} %collective-permute-done.1.refs_2_), channel_id=1, source_target_pairs={{0,4},{4,0},{1,5},{5,1},{2,6},{6,2},{3,7},{7,3},{8,12},{12,8},{9,1... | collective-permute-start | bytes 1179656 | tf_op jit(solution)/shard_map/ppermute | solution.py:284
  33.0 13.0 %collective-permute-start = (bf16[8,192,128]{2,1,0:T(8,128)(2,1)S(1)}, bf16[8,192,128]{2,1,0:T(8,128)(2,1)S(1)}, u32[]{:S(2)}, u32[]{:S(2)}) collective-permute-start(bf16[8,192,128]{2,1,0:T(8,128)(2,1)S(1)} %slice.9.refs_2_), channel_id=1, source_target_pairs={{0,128},{64,192},{128,0},{192,64},{1,129},{65,193},{129,1},{193,65... | collective-permute-start | bytes 1179656 | tf_op jit(solution)/shard_map/ppermute | solution.py:281
  33.0 13.0 %collective-permute-start.6 = (bf16[8,192,128]{2,1,0:T(8,128)(2,1)S(1)}, bf16[8,192,128]{2,1,0:T(8,128)(2,1)S(1)}, u32[]{:S(2)}, u32[]{:S(2)}) collective-permute-start(bf16[8,192,128]{2,1,0:T(8,128)(2,1)S(1)} %collective-permute-done.2.refs_2_), channel_id=1, source_target_pairs={{0,4},{4,0},{1,5},{5,1},{2,6},{6,2},{3,7},{7,3},{8,12},{12,8},{9,1... | collective-permute-start | bytes 1179656 | tf_op jit(solution)/shard_map/ppermute | solution.py:284
  46.0 14.5 %slice-start.1 = ((s8[8388608]{0:T(1024)(128)(4,1)}), s8[4194304]{0:T(1024)(128)(4,1)S(1)}, s32[]{:S(2)}) async-start(s8[8388608]{0:T(1024)(128)(4,1)} %bitcast.4), calls=%async_computation.3 | async-start | bytes 8388608
  46.0 2.2 %collective-permute-start.5 = (bf16[8,192,128]{2,1,0:T(8,128)(2,1)S(1)}, bf16[8,192,128]{2,1,0:T(8,128)(2,1)S(1)}, u32[]{:S(2)}, u32[]{:S(2)}) collective-permute-start(bf16[8,192,128]{2,1,0:T(8,128)(2,1)S(1)} %collective-permute-done.refs_2_), channel_id=1, source_target_pairs={{0,4},{4,0},{1,5},{5,1},{2,6},{6,2},{3,7},{7,3},{8,12},{12,8},{9,1... | collective-permute-start | bytes 1179656 | tf_op jit(solution)/shard_map/ppermute | solution.py:284
  62.4 7.8 %collective-permute-start.7 = (bf16[16,4096]{1,0:T(8,128)(2,1)S(1)}, bf16[16,4096]{1,0:T(8,128)(2,1)S(1)}, u32[]{:S(2)}, u32[]{:S(2)}) collective-permute-start(bf16[16,4096]{1,0:T(8,128)(2,1)S(1)} %get-tuple-element.40), channel_id=1, source_target_pairs={{0,1},{1,2},{2,3},{3,0},{4,5},{5,6},{6,7},{7,4},{8,9},{9,10},{10,1... | collective-permute-start | bytes 393224 | tf_op jit(solution)/shard_map/ppermute | solution.py:303
  66.0 13.8 %collective-permute-start.10 = (bf16[16,4096]{1,0:T(8,128)(2,1)S(1)}, bf16[16,4096]{1,0:T(8,128)(2,1)S(1)}, u32[]{:S(2)}, u32[]{:S(2)}) collective-permute-start(bf16[16,4096]{1,0:T(8,128)(2,1)S(1)} %get-tuple-element.43), channel_id=1, source_target_pairs={{0,3},{1,0},{2,1},{3,2},{4,7},{5,4},{6,5},{7,6},{8,11},{9,8},{10,9... | collective-permute-start | bytes 393224 | tf_op jit(solution)/shard_map/ppermute | solution.py:303
  66.0 13.9 %collective-permute-start.9 = (bf16[16,4096]{1,0:T(8,128)(2,1)S(1)}, bf16[16,4096]{1,0:T(8,128)(2,1)S(1)}, u32[]{:S(2)}, u32[]{:S(2)}) collective-permute-start(bf16[16,4096]{1,0:T(8,128)(2,1)S(1)} %get-tuple-element.41), channel_id=1, source_target_pairs={{0,1},{1,2},{2,3},{3,0},{4,5},{5,6},{6,7},{7,4},{8,9},{9,10},{10,1... | collective-permute-start | bytes 393224 | tf_op jit(solution)/shard_map/ppermute | solution.py:303
  70.2 12.6 %collective-permute-start.12 = (bf16[16,4096]{1,0:T(8,128)(2,1)S(1)}, bf16[16,4096]{1,0:T(8,128)(2,1)S(1)}, u32[]{:S(2)}, u32[]{:S(2)}) collective-permute-start(bf16[16,4096]{1,0:T(8,128)(2,1)S(1)} %get-tuple-element.44), channel_id=1, source_target_pairs={{0,3},{1,0},{2,1},{3,2},{4,7},{5,4},{6,5},{7,6},{8,11},{9,8},{10,9... | collective-permute-start | bytes 393224 | tf_op jit(solution)/shard_map/ppermute | solution.py:303
  70.2 12.5 %collective-permute-start.8 = (bf16[16,4096]{1,0:T(8,128)(2,1)S(1)}, bf16[16,4096]{1,0:T(8,128)(2,1)S(1)}, u32[]{:S(2)}, u32[]{:S(2)}) collective-permute-start(bf16[16,4096]{1,0:T(8,128)(2,1)S(1)} %shard_map.86), channel_id=1, source_target_pairs={{0,1},{1,2},{2,3},{3,0},{4,5},{5,6},{6,7},{7,4},{8,9},{9,10},{10,1... | collective-permute-start | bytes 393224 | tf_op jit(solution)/shard_map/ppermute | solution.py:303
  79.9 9.8 %collective-permute-start.11 = (bf16[16,4096]{1,0:T(8,128)(2,1)S(1)}, bf16[16,4096]{1,0:T(8,128)(2,1)S(1)}, u32[]{:S(2)}, u32[]{:S(2)}) collective-permute-start(bf16[16,4096]{1,0:T(8,128)(2,1)S(1)} %shard_map.87), channel_id=1, source_target_pairs={{0,3},{1,0},{2,1},{3,2},{4,7},{5,4},{6,5},{7,6},{8,11},{9,8},{10,9... | collective-permute-start | bytes 393224 | tf_op jit(solution)/shard_map/ppermute | solution.py:303

commit v2 on v1

--- a/solution.py
+++ b/solution.py
@@ -84,12 +84,11 @@
     )(place, in_vmem(probe_rows), in_vmem(pattern))
 
 
-def chunk_body(k, parts, *refs):
-    first = k == 0
-    last = k == NX - 1
+def chunk_body(k, slots, parts, first, last, *refs):
     received_ref, bias_ref = refs[:2]
-    kv_refs = refs[2 : 2 + 2 * parts]
-    rest = refs[2 + 2 * parts :]
+    count = parts * len(slots)
+    kv_refs = refs[2 : 2 + count]
+    rest = refs[2 + count :]
     if not first:
         m_in, acc_in = rest[:2]
         rest = rest[2:]
@@ -98,8 +97,9 @@
     else:
         m_out, acc_out, score_ref, peak_ref = rest
     width = 256
-    entry = lax.broadcasted_iota(jnp.int32, (2 * HALF, 128), 0) // CSIZE
-    onehot = (entry == lax.broadcasted_iota(jnp.int32, (2 * HALF, 128), 1)).astype(jnp.bfloat16)
+    size = HALF * len(slots)
+    entry = lax.broadcasted_iota(jnp.int32, (size, 128), 0) // CSIZE + slots[0] * (HALF // CSIZE)
+    onehot = (entry == lax.broadcasted_iota(jnp.int32, (size, 128), 1)).astype(jnp.bfloat16)
     if parts == 1:
         keys = [r[:, :ROWS_M, :].reshape(HALF, HD) for r in kv_refs]
         values = [r[:, ROWS_M:, :].reshape(HALF, HD) for r in kv_refs]
@@ -107,10 +107,10 @@
         keys = [r[...].reshape(HALF, HD) for r in kv_refs[0::2]]
         values = [r[...].reshape(HALF, HD) for r in kv_refs[1::2]]
     keys = jnp.concatenate([jnp.concatenate(keys, axis=0), onehot], axis=1)
-    values = jnp.concatenate([jnp.concatenate(values, axis=0), jnp.ones((2 * HALF, 128), jnp.bfloat16)], axis=1)
+    values = jnp.concatenate([jnp.concatenate(values, axis=0), jnp.ones((size, 128), jnp.bfloat16)], axis=1)
     rows = received_ref[:, :ROWS_Q, :].reshape(NQ, HD)
     rows = jnp.concatenate([rows, bias_ref[k]], axis=1)
-    for j in range(2 * HALF // width):
+    for j in range(size // width):
         span = slice(j * width, (j + 1) * width)
         scores = lax.dot_general(rows, keys[span], (((1,), (1,)), ((), ())), preferred_element_type=jnp.float32)
         score_ref[:, span] = scores
@@ -139,10 +139,9 @@
             acc_out[span, :] = acc
 
 
-def attend(k, received, bias, kv, state):
-    first = k == 0
-    last = k == NX - 1
-    parts = len(kv) // 2
+def attend(k, received, bias, kv, state, slots=(0, 1), last=False):
+    first = state is None
+    parts = len(kv) // len(slots)
     args = [received, bias, *kv]
     if not first:
         args += list(state)
@@ -151,11 +150,11 @@
     else:
         out_shape = [pltpu.VMEM((NQ, 128), jnp.float32), pltpu.VMEM((NQ, 2 * HD), jnp.float32)]
     return pl.pallas_call(
-        lambda *refs: chunk_body(k, parts, *refs),
+        lambda *refs: chunk_body(k, slots, parts, first, last, *refs),
         in_specs=[VMEM_SPEC] * len(args),
         out_specs=VMEM_SPEC if last else [VMEM_SPEC] * 2,
         out_shape=out_shape,
-        scratch_shapes=[pltpu.VMEM((NQ, 2 * HALF), jnp.float32), pltpu.VMEM((NQ, 128), jnp.float32)],
+        scratch_shapes=[pltpu.VMEM((NQ, HALF * len(slots)), jnp.float32), pltpu.VMEM((NQ, 128), jnp.float32)],
         cost_estimate=pl.CostEstimate(flops=1 << 20, bytes_accessed=1 << 10, transcendentals=0),
         compiler_params=pltpu.CompilerParams(vmem_limit_bytes=24 << 20),
     )(*[in_vmem(arg) for arg in args])
@@ -286,17 +285,20 @@
     place = jnp.stack([lax.axis_index("x"), lax.axis_index("c"), lax.axis_index("h")]).astype(jnp.int32)
     left = shift(own, 1)
     right = shift(own, 3)
-    opposite = shift(own, 2)
     own_far = swap(own)
     bias = make_bias(place, received[:, ROWS_Q + 2 * ROWS_M :, :], pattern)
     state = attend(0, received, bias, (own, own_far), None)
     left, right, *state = lax.optimization_barrier((left, right, *state))
+    opposite_k = shift(left[:, :ROWS_M], 1)
+    opposite_v = shift(right[:, ROWS_M:], 3)
     left_far = swap(left)
     right_far = swap(right)
     state = attend(1, received, bias, (left, left_far), state)
-    opposite, *state = lax.optimization_barrier((opposite, *state))
     state = attend(2, received, bias, (right, right_far), state)
-    state = attend(3, received, bias, (opposite, swap(opposite)), state)
+    opposite_k, opposite_v, *state = lax.optimization_barrier((opposite_k, opposite_v, *state))
+    opposite_far = (swap(opposite_k), swap(opposite_v))
+    state = attend(3, received, bias, (opposite_k, opposite_v), state, slots=(0,))
+    state = attend(3, received, bias, opposite_far, state, slots=(1,), last=True)
     recalled = lax.all_to_all(state, B_AXES, 0, 0, tiled=True)
 
     def plane_shift(array, by):

time: 90.7 us -> 84.3 us (0.929)
  the two profiles are of different devices: /device:TPU:72 before, /device:TPU:46 now
where the time goes in v2:
time: 84.3 us; the launch traced here: 83.9 us
  blocking collectives  25.5 us (30%)
  waiting for transfers between devices  20.4 us (24%)
  starting transfers between devices  20.1 us (24%)
  Pallas kernels  16.8 us (20%)
    all_to_all x1, blocking collectives, local(): lax.all_to_all(pack(queries, mem_keys, mem_values, probes.T), B_AXES, 0,...  15.4 us
    ppermute x6, starting transfers between devices, plane_shift(): return lax.ppermute(array, 'h', [(i, (i + by) % NH) for i in range(NH)])  14.8 us
    ppermute x6, waiting for transfers between devices, plane_shift(): return lax.ppermute(array, 'h', [(i, (i + by) % NH) for i in range(NH)])  12.7 us
    pallas_call x5, Pallas kernels, attend(): pl.pallas_call(lambda *refs: chunk_body(k, slots, parts, first, last, *re...  10.5 us
    all_to_all x1, blocking collectives, local(): recalled = lax.all_to_all(state, B_AXES, 0, 0, tiled=True)  10.2 us
    ppermute x4, waiting for transfers between devices, shift(): return lax.ppermute(array, 'x', [(i, (i + by) % NX) for i in range(NX)])  7.69 us
    ppermute x4, starting transfers between devices, shift(): return lax.ppermute(array, 'x', [(i, (i + by) % NX) for i in range(NX)])  4.21 us
    pallas_call x1, Pallas kernels, make_bias(): pl.pallas_call(bias_body, in_specs=[SMEM_SPEC, VMEM_SPEC, VMEM_SPEC], out...  2.35 us
  transfers between devices with their start and end apart: 15, of which 8 were waited for; matrix products, arithmetic and copies ran while one was open for 0% of the time, Pallas kernels for 13%

profile of v2, /device:TPU:46, one launch (start us, length us, event | category | flops | bytes accessed | tf_op | source)
XLA Modules:
  0.0 83.9 jit_solution(138431350812334272)
XLA Ops:
  0.0 1.3 %pack.1 = bf16[8,336,128]{2,1,0:T(8,128)(2,1)S(1)} custom-call(bf16[128,1024]{1,0:T(8,128)(2,1)} %q_ref.1, bf16[96,1024]{1,0:T(8,128)(2,1)} %k_ref.1, bf16[96,1024]{1,0:T(8,128)(2,1)} %v_ref.1, s32[8,128]{1,0:T(8,128)} %bitcast.6), custom_call_target="tpu_custom_call" | custom-call | tf_op jit(solution)/shard_map/pack/pallas_call | solution.py:264
  1.3 15.4 %all_to_all.10.refs_0_ = bf16[8,336,128]{2,1,0:T(8,128)(2,1)S(1)} all-to-all(bf16[8,336,128]{2,1,0:T(8,128)(2,1)S(1)} %pack.1), channel_id=1, replica_groups=mesh['x'=4,'zl'=2,'y'=4,'c'=2,'h'=4] {'zl','y'}, dimensions={0} | all-to-all | bytes 1376256 | tf_op jit(solution)/shard_map/all_to_all | solution.py:276
  16.7 0.1 collective-permute-start.2
  16.8 0.6 collective-permute-start
  17.4 1.5 %collective-permute-start.1 = (bf16[8,192,128]{2,1,0:T(8,128)(2,1)S(1)}, bf16[8,192,128]{2,1,0:T(8,128)(2,1)S(1)}, u32[]{:S(2)}, u32[]{:S(2)}) collective-permute-start(bf16[8,192,128]{2,1,0:T(8,128)(2,1)S(1)} %slice.17.refs_2_), channel_id=1, source_target_pairs={{0,192},{64,0},{128,64},{192,128},{1,193},{65,1},{129,65},{193,129... | collective-permute-start | bytes 1179656 | tf_op jit(solution)/shard_map/ppermute | solution.py:280
  18.9 0.1 pad_add_fusion.place_ref
  19.0 0.8 copy-done.1
  19.7 2.4 %bias.1.refs_1_ = bf16[4,1024,128]{2,1,0:T(8,128)(2,1)S(1)} custom-call(s32[3]{0:T(128)S(1)} %pad_add_fusion.place_ref, bf16[8,16,128]{2,1,0:T(8,128)(2,1)S(1)} %slice.16.probe_ref, s32[64,64]{1,0:T(8,128)S(1)} %copy-done.1), custom_call_target="tpu_custom_call" | custom-call | tf_op jit(solution)/shard_map/bias/pallas_call | solution.py:77
  22.1 0.0 collective-permute-done.2.refs_3_
  22.1 1.9 %shard_map.82 = (f32[1024,128]{1,0:T(8,128)S(1)}, f32[1024,256]{1,0:T(8,128)S(1)}) custom-call(bf16[8,336,128]{2,1,0:T(8,128)(2,1)S(1)} %all_to_all.10.refs_0_, bf16[4,1024,128]{2,1,0:T(8,128)(2,1)S(1)} %bias.1.refs_1_, bf16[8,192,128]{2,1,0:T(8,128)(2,1)S(1)} %slice.17.refs_2_, bf16[8,192,128]{2,1,0:T(8,128)(2,1)S(1)} %collective-permute-done.2.refs_3_), custom_call_target="tpu_custom_call" | custom-call | flops 1048576 | bytes 1024 | tf_op jit(solution)/shard_map/pallas_call | solution.py:152
  24.0 4.3 %collective-permute-done.refs_2_ = bf16[8,192,128]{2,1,0:T(8,128)(2,1)S(1)} collective-permute-done((bf16[8,192,128]{2,1,0:T(8,128)(2,1)S(1)}, bf16[8,192,128]{2,1,0:T(8,128)(2,1)S(1)}, u32[]{:S(2)}, u32[]{:S(2)}) %collective-permute-start) | collective-permute-done | bytes 393248 | tf_op jit(solution)/shard_map/ppermute | solution.py:280
  28.3 1.4 %collective-permute-done.1.refs_2_ = bf16[8,192,128]{2,1,0:T(8,128)(2,1)S(1)} collective-permute-done((bf16[8,192,128]{2,1,0:T(8,128)(2,1)S(1)}, bf16[8,192,128]{2,1,0:T(8,128)(2,1)S(1)}, u32[]{:S(2)}, u32[]{:S(2)}) %collective-permute-start.1) | collective-permute-done | bytes 393248 | tf_op jit(solution)/shard_map/ppermute | solution.py:280
  29.7 0.0 collective-permute-start.6
  29.7 0.5 collective-permute-start.5
  30.3 0.0 slice-start
  30.3 0.0 copy-start
  30.3 0.0 copy-start.2
  30.3 0.4 collective-permute-start.3
  30.7 1.7 %collective-permute-start.4 = (bf16[8,96,128]{2,1,0:T(8,128)(2,1)S(1)}, bf16[8,96,128]{2,1,0:T(8,128)(2,1)S(1)}, u32[]{:S(2)}, u32[]{:S(2)}) collective-permute-start(bf16[8,96,128]{2,1,0:T(8,128)(2,1)S(1)} %slice.15), channel_id=1, source_target_pairs={{0,192},{64,0},{128,64},{192,128},{1,193},{65,1},{129,65},{193,129... | collective-permute-start | bytes 589832 | tf_op jit(solution)/shard_map/ppermute | solution.py:280
  32.4 0.0 collective-permute-done.6.refs_3_
  32.4 2.1 %shard_map.83 = (f32[1024,128]{1,0:T(8,128)S(1)}, f32[1024,256]{1,0:T(8,128)S(1)}) custom-call(bf16[8,336,128]{2,1,0:T(8,128)(2,1)S(1)} %all_to_all.10.refs_0_, bf16[4,1024,128]{2,1,0:T(8,128)(2,1)S(1)} %bias.1.refs_1_, bf16[8,192,128]{2,1,0:T(8,128)(2,1)S(1)} %collective-permute-done.refs_2_, bf16[8,192,128]{2,1,0:T(8,128)(2,1)S(1)} %collective-permute-done.6.refs_3_, ...), custom_call_target="tpu_custom_call" | custom-call | flops 1048576 | bytes 1024 | tf_op jit(solution)/shard_map/pallas_call | solution.py:152
  34.6 0.0 collective-permute-done.5.refs_3_
  34.6 0.0 slice-start.1
  34.6 2.1 %shard_map.84 = (f32[1024,128]{1,0:T(8,128)S(1)}, f32[1024,256]{1,0:T(8,128)S(1)}) custom-call(bf16[8,336,128]{2,1,0:T(8,128)(2,1)S(1)} %all_to_all.10.refs_0_, bf16[4,1024,128]{2,1,0:T(8,128)(2,1)S(1)} %bias.1.refs_1_, bf16[8,192,128]{2,1,0:T(8,128)(2,1)S(1)} %collective-permute-done.1.refs_2_, bf16[8,192,128]{2,1,0:T(8,128)(2,1)S(1)} %collective-permute-done.5.refs_3_, ...), custom_call_target="tpu_custom_call" | custom-call | flops 1048576 | bytes 1024 | tf_op jit(solution)/shard_map/pallas_call | solution.py:152
  36.7 0.5 collective-permute-done.3.refs_2_
  37.2 1.5 %collective-permute-done.4.refs_3_ = bf16[8,96,128]{2,1,0:T(8,128)(2,1)S(1)} collective-permute-done((bf16[8,96,128]{2,1,0:T(8,128)(2,1)S(1)}, bf16[8,96,128]{2,1,0:T(8,128)(2,1)S(1)}, u32[]{:S(2)}, u32[]{:S(2)}) %collective-permute-start.4) | collective-permute-done | bytes 196640 | tf_op jit(solution)/shard_map/ppermute | solution.py:280
  38.7 0.0 collective-permute-start.7
  38.7 0.5 collective-permute-start.8
  39.2 2.2 %shard_map.85 = (f32[1024,128]{1,0:T(8,128)S(1)}, f32[1024,256]{1,0:T(8,128)S(1)}) custom-call(bf16[8,336,128]{2,1,0:T(8,128)(2,1)S(1)} %all_to_all.10.refs_0_, bf16[4,1024,128]{2,1,0:T(8,128)(2,1)S(1)} %bias.1.refs_1_, bf16[8,96,128]{2,1,0:T(8,128)(2,1)S(1)} %collective-permute-done.3.refs_2_, bf16[8,96,128]{2,1,0:T(8,128)(2,1)S(1)} %collective-permute-done.4.refs_3_, ...), custom_call_target="tpu_custom_call" | custom-call | flops 1048576 | bytes 1024 | tf_op jit(solution)/shard_map/pallas_call | solution.py:152
  41.4 0.0 collective-permute-done.7.refs_2_
  41.4 0.0 collective-permute-done.8.refs_3_
  41.4 2.2 %shard_map.86 = bf16[8,128,128]{2,1,0:T(8,128)(2,1)S(1)} custom-call(bf16[8,336,128]{2,1,0:T(8,128)(2,1)S(1)} %all_to_all.10.refs_0_, bf16[4,1024,128]{2,1,0:T(8,128)(2,1)S(1)} %bias.1.refs_1_, bf16[8,96,128]{2,1,0:T(8,128)(2,1)S(1)} %collective-permute-done.7.refs_2_, bf16[8,96,128]{2,1,0:T(8,128)(2,1)S(1)} %collective-permute-done.8.refs_3_, ...), custom_call_target="tpu_custom_call" | custom-call | flops 1048576 | bytes 1024 | tf_op jit(solution)/shard_map/pallas_call | solution.py:152
  43.6 10.2 %all_to_all.11.rec_ref = bf16[8,128,128]{2,1,0:T(8,128)(2,1)S(1)} all-to-all(bf16[8,128,128]{2,1,0:T(8,128)(2,1)S(1)} %shard_map.86), channel_id=1, replica_groups=mesh['x'=4,'zl'=2,'y'=4,'c'=2,'h'=4] {'zl','y'}, dimensions={0} | all-to-all | bytes 524288 | tf_op jit(solution)/shard_map/all_to_all | solution.py:302
  53.7 0.0 copy-done.2
  53.8 1.8 %project.1 = (bf16[16,4096]{1,0:T(8,128)(2,1)S(1)}, bf16[16,4096]{1,0:T(8,128)(2,1)S(1)}, bf16[16,4096]{1,0:T(8,128)(2,1)S(1)}, bf16[16,4096]{1,0:T(8,128)(2,1)S...) custom-call(s32[3]{0:T(128)S(1)} %pad_add_fusion.place_ref, ...), custom_call_target="tpu_custom_call" | custom-call | flops 1073741824 | bytes 10485760 | tf_op jit(solution)/shard_map/project/pallas_call | solution.py:190
  55.6 5.5 %collective-permute-start.12 = (bf16[16,4096]{1,0:T(8,128)(2,1)S(1)}, bf16[16,4096]{1,0:T(8,128)(2,1)S(1)}, u32[]{:S(2)}, u32[]{:S(2)}) collective-permute-start(bf16[16,4096]{1,0:T(8,128)(2,1)S(1)} %get-tuple-element.49), channel_id=1, source_target_pairs={{0,3},{1,0},{2,1},{3,2},{4,7},{5,4},{6,5},{7,6},{8,11},{9,8},{10,9... | collective-permute-start | bytes 393224 | tf_op jit(solution)/shard_map/ppermute | solution.py:305
  61.1 0.0 collective-permute-start.9
  61.1 2.0 %collective-permute-start.11 = (bf16[16,4096]{1,0:T(8,128)(2,1)S(1)}, bf16[16,4096]{1,0:T(8,128)(2,1)S(1)}, u32[]{:S(2)}, u32[]{:S(2)}) collective-permute-start(bf16[16,4096]{1,0:T(8,128)(2,1)S(1)} %get-tuple-element.47), channel_id=1, source_target_pairs={{0,1},{1,2},{2,3},{3,0},{4,5},{5,6},{6,7},{7,4},{8,9},{9,10},{10,1... | collective-permute-start | bytes 393224 | tf_op jit(solution)/shard_map/ppermute | solution.py:305
  63.1 2.1 %collective-permute-start.14 = (bf16[16,4096]{1,0:T(8,128)(2,1)S(1)}, bf16[16,4096]{1,0:T(8,128)(2,1)S(1)}, u32[]{:S(2)}, u32[]{:S(2)}) collective-permute-start(bf16[16,4096]{1,0:T(8,128)(2,1)S(1)} %get-tuple-element.50), channel_id=1, source_target_pairs={{0,3},{1,0},{2,1},{3,2},{4,7},{5,4},{6,5},{7,6},{8,11},{9,8},{10,9... | collective-permute-start | bytes 393224 | tf_op jit(solution)/shard_map/ppermute | solution.py:305
  65.2 1.1 %collective-permute-done.12.b_ref = bf16[16,4096]{1,0:T(8,128)(2,1)S(1)} collective-permute-done((bf16[16,4096]{1,0:T(8,128)(2,1)S(1)}, bf16[16,4096]{1,0:T(8,128)(2,1)S(1)}, u32[]{:S(2)}, u32[]{:S(2)}) %collective-permute-start.12) | collective-permute-done | bytes 131104 | tf_op jit(solution)/shard_map/ppermute | solution.py:305
  66.4 5.1 %collective-permute-start.13 = (bf16[16,4096]{1,0:T(8,128)(2,1)S(1)}, bf16[16,4096]{1,0:T(8,128)(2,1)S(1)}, u32[]{:S(2)}, u32[]{:S(2)}) collective-permute-start(bf16[16,4096]{1,0:T(8,128)(2,1)S(1)} %shard_map.88), channel_id=1, source_target_pairs={{0,3},{1,0},{2,1},{3,2},{4,7},{5,4},{6,5},{7,6},{8,11},{9,8},{10,9... | collective-permute-start | bytes 393224 | tf_op jit(solution)/shard_map/ppermute | solution.py:305
  71.5 3.5 %collective-permute-done.9.b_ref = bf16[16,4096]{1,0:T(8,128)(2,1)S(1)} collective-permute-done((bf16[16,4096]{1,0:T(8,128)(2,1)S(1)}, bf16[16,4096]{1,0:T(8,128)(2,1)S(1)}, u32[]{:S(2)}, u32[]{:S(2)}) %collective-permute-start.9) | collective-permute-done | bytes 131104 | tf_op jit(solution)/shard_map/ppermute | solution.py:305
  75.0 0.1 collective-permute-start.10
  75.1 2.8 %collective-permute-done.11.up_free_ref = bf16[16,4096]{1,0:T(8,128)(2,1)S(1)} collective-permute-done((bf16[16,4096]{1,0:T(8,128)(2,1)S(1)}, bf16[16,4096]{1,0:T(8,128)(2,1)S(1)}, u32[]{:S(2)}, u32[]{:S(2)}) %collective-permute-start.11) | collective-permute-done | bytes 131104 | tf_op jit(solution)/shard_map/ppermute | solution.py:305
  77.9 0.0 collective-permute-done.14.down_free_ref
  77.9 0.0 collective-permute-done.13.down_ref
  77.9 5.2 %collective-permute-done.10.up_ref = bf16[16,4096]{1,0:T(8,128)(2,1)S(1)} collective-permute-done((bf16[16,4096]{1,0:T(8,128)(2,1)S(1)}, bf16[16,4096]{1,0:T(8,128)(2,1)S(1)}, u32[]{:S(2)}, u32[]{:S(2)}) %collective-permute-start.10) | collective-permute-done | bytes 131104 | tf_op jit(solution)/shard_map/ppermute | solution.py:305
  83.1 0.8 finish.1
  (11 shorter events, 0.1 us)
Async XLA Ops:
  16.7 5.4 %collective-permute-start.2 = (bf16[8,192,128]{2,1,0:T(8,128)(2,1)S(1)}, bf16[8,192,128]{2,1,0:T(8,128)(2,1)S(1)}, u32[]{:S(2)}, u32[]{:S(2)}) collective-permute-start(bf16[8,192,128]{2,1,0:T(8,128)(2,1)S(1)} %slice.17.refs_2_), channel_id=1, source_target_pairs={{0,4},{4,0},{1,5},{5,1},{2,6},{6,2},{3,7},{7,3},{8,12},{12,8},{9,1... | collective-permute-start | bytes 1179656 | tf_op jit(solution)/shard_map/ppermute | solution.py:283
  16.8 11.5 %collective-permute-start = (bf16[8,192,128]{2,1,0:T(8,128)(2,1)S(1)}, bf16[8,192,128]{2,1,0:T(8,128)(2,1)S(1)}, u32[]{:S(2)}, u32[]{:S(2)}) collective-permute-start(bf16[8,192,128]{2,1,0:T(8,128)(2,1)S(1)} %slice.17.refs_2_), channel_id=1, source_target_pairs={{0,64},{64,128},{128,192},{192,0},{1,65},{65,129},{129,193},{193,1... | collective-permute-start | bytes 1179656 | tf_op jit(solution)/shard_map/ppermute | solution.py:280
  17.4 12.4 %collective-permute-start.1 = (bf16[8,192,128]{2,1,0:T(8,128)(2,1)S(1)}, bf16[8,192,128]{2,1,0:T(8,128)(2,1)S(1)}, u32[]{:S(2)}, u32[]{:S(2)}) collective-permute-start(bf16[8,192,128]{2,1,0:T(8,128)(2,1)S(1)} %slice.17.refs_2_), channel_id=1, source_target_pairs={{0,192},{64,0},{128,64},{192,128},{1,193},{65,1},{129,65},{193,129... | collective-permute-start | bytes 1179656 | tf_op jit(solution)/shard_map/ppermute | solution.py:280
  19.0 0.8 copy-start.1
  29.7 2.7 %collective-permute-start.6 = (bf16[8,192,128]{2,1,0:T(8,128)(2,1)S(1)}, bf16[8,192,128]{2,1,0:T(8,128)(2,1)S(1)}, u32[]{:S(2)}, u32[]{:S(2)}) collective-permute-start(bf16[8,192,128]{2,1,0:T(8,128)(2,1)S(1)} %collective-permute-done.refs_2_), channel_id=1, source_target_pairs={{0,4},{4,0},{1,5},{5,1},{2,6},{6,2},{3,7},{7,3},{8,12},{12,8},{9,1... | collective-permute-start | bytes 1179656 | tf_op jit(solution)/shard_map/ppermute | solution.py:283
  29.7 4.8 %collective-permute-start.5 = (bf16[8,192,128]{2,1,0:T(8,128)(2,1)S(1)}, bf16[8,192,128]{2,1,0:T(8,128)(2,1)S(1)}, u32[]{:S(2)}, u32[]{:S(2)}) collective-permute-start(bf16[8,192,128]{2,1,0:T(8,128)(2,1)S(1)} %collective-permute-done.1.refs_2_), channel_id=1, source_target_pairs={{0,4},{4,0},{1,5},{5,1},{2,6},{6,2},{3,7},{7,3},{8,12},{12,8},{9,1... | collective-permute-start | bytes 1179656 | tf_op jit(solution)/shard_map/ppermute | solution.py:283
  30.3 23.5 %slice-start = ((s8[8388608]{0:T(1024)(128)(4,1)}), s8[4194304]{0:T(1024)(128)(4,1)S(1)}, s32[]{:S(2)}) async-start(s8[8388608]{0:T(1024)(128)(4,1)} %bitcast.4), calls=%async_computation.2 | async-start | bytes 8388608
  30.3 23.5 %copy-start = (bf16[128,1024]{1,0:T(8,128)(2,1)S(1)}, bf16[128,1024]{1,0:T(8,128)(2,1)}, u32[]{:S(2)}) copy-start(bf16[128,1024]{1,0:T(8,128)(2,1)} %own_ref.1) | copy-start | bytes 786436
  30.3 23.5 %copy-start.2 = (f32[8]{0:T(128)S(1)}, f32[8]{0:T(128)}, u32[]{:S(2)}) copy-start(f32[8]{0:T(128)} %gate_ref.1) | copy-start | bytes 100
  30.3 6.9 %collective-permute-start.3 = (bf16[8,96,128]{2,1,0:T(8,128)(2,1)S(1)}, bf16[8,96,128]{2,1,0:T(8,128)(2,1)S(1)}, u32[]{:S(2)}, u32[]{:S(2)}) collective-permute-start(bf16[8,96,128]{2,1,0:T(8,128)(2,1)S(1)} %slice.14), channel_id=1, source_target_pairs={{0,64},{64,128},{128,192},{192,0},{1,65},{65,129},{129,193},{193,1... | collective-permute-start | bytes 589832 | tf_op jit(solution)/shard_map/ppermute | solution.py:280
  30.7 8.0 %collective-permute-start.4 = (bf16[8,96,128]{2,1,0:T(8,128)(2,1)S(1)}, bf16[8,96,128]{2,1,0:T(8,128)(2,1)S(1)}, u32[]{:S(2)}, u32[]{:S(2)}) collective-permute-start(bf16[8,96,128]{2,1,0:T(8,128)(2,1)S(1)} %slice.15), channel_id=1, source_target_pairs={{0,192},{64,0},{128,64},{192,128},{1,193},{65,1},{129,65},{193,129... | collective-permute-start | bytes 589832 | tf_op jit(solution)/shard_map/ppermute | solution.py:280
  34.6 19.2 %slice-start.1 = ((s8[8388608]{0:T(1024)(128)(4,1)}), s8[4194304]{0:T(1024)(128)(4,1)S(1)}, s32[]{:S(2)}) async-start(s8[8388608]{0:T(1024)(128)(4,1)} %bitcast.4), calls=%async_computation.3 | async-start | bytes 8388608
  38.7 2.7 %collective-permute-start.7 = (bf16[8,96,128]{2,1,0:T(8,128)(2,1)S(1)}, bf16[8,96,128]{2,1,0:T(8,128)(2,1)S(1)}, u32[]{:S(2)}, u32[]{:S(2)}) collective-permute-start(bf16[8,96,128]{2,1,0:T(8,128)(2,1)S(1)} %collective-permute-done.3.refs_2_), channel_id=1, source_target_pairs={{0,4},{4,0},{1,5},{5,1},{2,6},{6,2},{3,7},{7,3},{8,12},{12,8},{9,1... | collective-permute-start | bytes 589832 | tf_op jit(solution)/shard_map/ppermute | solution.py:283
  38.7 2.7 %collective-permute-start.8 = (bf16[8,96,128]{2,1,0:T(8,128)(2,1)S(1)}, bf16[8,96,128]{2,1,0:T(8,128)(2,1)S(1)}, u32[]{:S(2)}, u32[]{:S(2)}) collective-permute-start(bf16[8,96,128]{2,1,0:T(8,128)(2,1)S(1)} %collective-permute-done.4.refs_3_), channel_id=1, source_target_pairs={{0,4},{4,0},{1,5},{5,1},{2,6},{6,2},{3,7},{7,3},{8,12},{12,8},{9,1... | collective-permute-start | bytes 589832 | tf_op jit(solution)/shard_map/ppermute | solution.py:283
  55.6 10.8 %collective-permute-start.12 = (bf16[16,4096]{1,0:T(8,128)(2,1)S(1)}, bf16[16,4096]{1,0:T(8,128)(2,1)S(1)}, u32[]{:S(2)}, u32[]{:S(2)}) collective-permute-start(bf16[16,4096]{1,0:T(8,128)(2,1)S(1)} %get-tuple-element.49), channel_id=1, source_target_pairs={{0,3},{1,0},{2,1},{3,2},{4,7},{5,4},{6,5},{7,6},{8,11},{9,8},{10,9... | collective-permute-start | bytes 393224 | tf_op jit(solution)/shard_map/ppermute | solution.py:305
  61.1 13.9 %collective-permute-start.9 = (bf16[16,4096]{1,0:T(8,128)(2,1)S(1)}, bf16[16,4096]{1,0:T(8,128)(2,1)S(1)}, u32[]{:S(2)}, u32[]{:S(2)}) collective-permute-start(bf16[16,4096]{1,0:T(8,128)(2,1)S(1)} %get-tuple-element.46), channel_id=1, source_target_pairs={{0,1},{1,2},{2,3},{3,0},{4,5},{5,6},{6,7},{7,4},{8,9},{9,10},{10,1... | collective-permute-start | bytes 393224 | tf_op jit(solution)/shard_map/ppermute | solution.py:305
  61.1 16.8 %collective-permute-start.11 = (bf16[16,4096]{1,0:T(8,128)(2,1)S(1)}, bf16[16,4096]{1,0:T(8,128)(2,1)S(1)}, u32[]{:S(2)}, u32[]{:S(2)}) collective-permute-start(bf16[16,4096]{1,0:T(8,128)(2,1)S(1)} %get-tuple-element.47), channel_id=1, source_target_pairs={{0,1},{1,2},{2,3},{3,0},{4,5},{5,6},{6,7},{7,4},{8,9},{9,10},{10,1... | collective-permute-start | bytes 393224 | tf_op jit(solution)/shard_map/ppermute | solution.py:305
  63.1 14.8 %collective-permute-start.14 = (bf16[16,4096]{1,0:T(8,128)(2,1)S(1)}, bf16[16,4096]{1,0:T(8,128)(2,1)S(1)}, u32[]{:S(2)}, u32[]{:S(2)}) collective-permute-start(bf16[16,4096]{1,0:T(8,128)(2,1)S(1)} %get-tuple-element.50), channel_id=1, source_target_pairs={{0,3},{1,0},{2,1},{3,2},{4,7},{5,4},{6,5},{7,6},{8,11},{9,8},{10,9... | collective-permute-start | bytes 393224 | tf_op jit(solution)/shard_map/ppermute | solution.py:305
  66.4 11.5 %collective-permute-start.13 = (bf16[16,4096]{1,0:T(8,128)(2,1)S(1)}, bf16[16,4096]{1,0:T(8,128)(2,1)S(1)}, u32[]{:S(2)}, u32[]{:S(2)}) collective-permute-start(bf16[16,4096]{1,0:T(8,128)(2,1)S(1)} %shard_map.88), channel_id=1, source_target_pairs={{0,3},{1,0},{2,1},{3,2},{4,7},{5,4},{6,5},{7,6},{8,11},{9,8},{10,9... | collective-permute-start | bytes 393224 | tf_op jit(solution)/shard_map/ppermute | solution.py:305
  75.0 8.1 %collective-permute-start.10 = (bf16[16,4096]{1,0:T(8,128)(2,1)S(1)}, bf16[16,4096]{1,0:T(8,128)(2,1)S(1)}, u32[]{:S(2)}, u32[]{:S(2)}) collective-permute-start(bf16[16,4096]{1,0:T(8,128)(2,1)S(1)} %shard_map.87), channel_id=1, source_target_pairs={{0,1},{1,2},{2,3},{3,0},{4,5},{5,6},{6,7},{7,4},{8,9},{9,10},{10,1... | collective-permute-start | bytes 393224 | tf_op jit(solution)/shard_map/ppermute | solution.py:305

commit v3 on v2

--- a/solution.py
+++ b/solution.py
@@ -20,7 +20,6 @@
 NQ = NB * ROWS_Q
 HALF = NB * ROWS_M
 OFFSETS = (0, 3, 1, 2)
-TILE_Q = 256
 
 
 def in_vmem(array):
@@ -118,24 +117,29 @@
         if j:
             peak = jnp.maximum(peak, peak_ref[...])
         peak_ref[...] = peak
-    for t in range(NQ // TILE_Q):
-        span = slice(t * TILE_Q, (t + 1) * TILE_Q)
-        peak = jnp.max(peak_ref[span, :], axis=1, keepdims=True)
+
+    def wide(lanes, times):
+        return jnp.concatenate([lanes] * times, axis=1)
+
+    tile = 512 // len(slots) ** 2
+    for t in range(NQ // tile):
+        span = slice(t * tile, (t + 1) * tile)
+        peak = jnp.broadcast_to(jnp.max(peak_ref[span, :], axis=1, keepdims=True), (tile, 128))
         if first:
             peak = jnp.maximum(peak, NEG / 2)
         else:
-            old = m_in[span, 0:1]
+            old = m_in[span, :]
             peak = jnp.maximum(peak, old)
-        weights = jnp.exp2((score_ref[span, :] - peak) * EXP2_SCALE).astype(jnp.bfloat16)
+        weights = jnp.exp2((score_ref[span, :] - wide(peak, size // 128)) * EXP2_SCALE).astype(jnp.bfloat16)
         acc = jnp.dot(weights, values, preferred_element_type=jnp.float32)
         if not first:
-            acc = acc + acc_in[span, :] * jnp.exp2((old - peak) * EXP2_SCALE)
+            acc = acc + acc_in[span, :] * wide(jnp.exp2((old - peak) * EXP2_SCALE), 2)
         if last:
             out = (acc[:, :HD] / acc[:, HD:]).astype(jnp.bfloat16)
-            per = TILE_Q // ROWS_Q
+            per = tile // ROWS_Q
             out_ref[t * per : (t + 1) * per] = out.reshape(per, ROWS_Q, HD)
         else:
-            m_out[span, :] = jnp.broadcast_to(peak, (TILE_Q, 128))
+            m_out[span, :] = peak
             acc_out[span, :] = acc
 
 

time: 84.3 us -> 82.7 us (0.981)
  the two profiles are of different devices: /device:TPU:46 before, /device:TPU:4 now
where the time goes in v3:
time: 82.7 us; the launch traced here: 81.5 us
  blocking collectives  27.7 us (33%)
  starting transfers between devices  20 us (24%)
  waiting for transfers between devices  18.1 us (22%)
  Pallas kernels  14.6 us (18%)
  local copies, waits for them, and re-layouts  0.84 us (1%)
    all_to_all x1, blocking collectives, local(): lax.all_to_all(pack(queries, mem_keys, mem_values, probes.T), B_AXES, 0,...  17.5 us
    ppermute x6, starting transfers between devices, plane_shift(): return lax.ppermute(array, 'h', [(i, (i + by) % NH) for i in range(NH)])  14.7 us
    ppermute x6, waiting for transfers between devices, plane_shift(): return lax.ppermute(array, 'h', [(i, (i + by) % NH) for i in range(NH)])  10.6 us
    all_to_all x1, blocking collectives, local(): recalled = lax.all_to_all(state, B_AXES, 0, 0, tiled=True)  10.2 us
    pallas_call x5, Pallas kernels, attend(): pl.pallas_call(lambda *refs: chunk_body(k, slots, parts, first, last, *re...  8.29 us
    ppermute x4, waiting for transfers between devices, shift(): return lax.ppermute(array, 'x', [(i, (i + by) % NX) for i in range(NX)])  7.52 us
    ppermute x4, starting transfers between devices, shift(): return lax.ppermute(array, 'x', [(i, (i + by) % NX) for i in range(NX)])  4.21 us
    pallas_call x1, Pallas kernels, make_bias(): pl.pallas_call(bias_body, in_specs=[SMEM_SPEC, VMEM_SPEC, VMEM_SPEC], out...  2.35 us
  transfers between devices with their start and end apart: 15, of which 9 were waited for; matrix products, arithmetic and copies ran while one was open for 0% of the time, Pallas kernels for 12%

profile of v3, /device:TPU:4, one launch (start us, length us, event | category | flops | bytes accessed | tf_op | source)
XLA Modules:
  0.0 81.5 jit_solution(7303035244106762322)
XLA Ops:
  0.0 1.3 %pack.1 = bf16[8,336,128]{2,1,0:T(8,128)(2,1)S(1)} custom-call(bf16[128,1024]{1,0:T(8,128)(2,1)} %q_ref.1, bf16[96,1024]{1,0:T(8,128)(2,1)} %k_ref.1, bf16[96,1024]{1,0:T(8,128)(2,1)} %v_ref.1, s32[8,128]{1,0:T(8,128)} %bitcast.6), custom_call_target="tpu_custom_call" | custom-call | tf_op jit(solution)/shard_map/pack/pallas_call | solution.py:268
  1.3 17.5 %all_to_all.10.refs_0_ = bf16[8,336,128]{2,1,0:T(8,128)(2,1)S(1)} all-to-all(bf16[8,336,128]{2,1,0:T(8,128)(2,1)S(1)} %pack.1), channel_id=1, replica_groups=mesh['x'=4,'zl'=2,'y'=4,'c'=2,'h'=4] {'zl','y'}, dimensions={0} | all-to-all | bytes 1376256 | tf_op jit(solution)/shard_map/all_to_all | solution.py:280
  18.8 0.1 collective-permute-start.2
  18.9 1.3 %collective-permute-start = (bf16[8,192,128]{2,1,0:T(8,128)(2,1)S(1)}, bf16[8,192,128]{2,1,0:T(8,128)(2,1)S(1)}, u32[]{:S(2)}, u32[]{:S(2)}) collective-permute-start(bf16[8,192,128]{2,1,0:T(8,128)(2,1)S(1)} %slice.17.refs_2_), channel_id=1, source_target_pairs={{0,64},{64,128},{128,192},{192,0},{1,65},{65,129},{129,193},{193,1... | collective-permute-start | bytes 1179656 | tf_op jit(solution)/shard_map/ppermute | solution.py:284
  20.2 0.8 %collective-permute-start.1 = (bf16[8,192,128]{2,1,0:T(8,128)(2,1)S(1)}, bf16[8,192,128]{2,1,0:T(8,128)(2,1)S(1)}, u32[]{:S(2)}, u32[]{:S(2)}) collective-permute-start(bf16[8,192,128]{2,1,0:T(8,128)(2,1)S(1)} %slice.17.refs_2_), channel_id=1, source_target_pairs={{0,192},{64,0},{128,64},{192,128},{1,193},{65,1},{129,65},{193,129... | collective-permute-start | bytes 1179656 | tf_op jit(solution)/shard_map/ppermute | solution.py:284
  21.0 0.1 pad_add_fusion.place_ref
  21.1 0.8 copy-done.1
  21.9 2.4 %bias.1.refs_1_ = bf16[4,1024,128]{2,1,0:T(8,128)(2,1)S(1)} custom-call(s32[3]{0:T(128)S(1)} %pad_add_fusion.place_ref, bf16[8,16,128]{2,1,0:T(8,128)(2,1)S(1)} %slice.16.probe_ref, s32[64,64]{1,0:T(8,128)S(1)} %copy-done.1), custom_call_target="tpu_custom_call" | custom-call | tf_op jit(solution)/shard_map/bias/pallas_call | solution.py:76
  24.2 0.0 collective-permute-done.2.refs_3_
  24.2 1.9 %shard_map.82 = (f32[1024,128]{1,0:T(8,128)S(1)}, f32[1024,256]{1,0:T(8,128)S(1)}) custom-call(bf16[8,336,128]{2,1,0:T(8,128)(2,1)S(1)} %all_to_all.10.refs_0_, bf16[4,1024,128]{2,1,0:T(8,128)(2,1)S(1)} %bias.1.refs_1_, bf16[8,192,128]{2,1,0:T(8,128)(2,1)S(1)} %slice.17.refs_2_, bf16[8,192,128]{2,1,0:T(8,128)(2,1)S(1)} %collective-permute-done.2.refs_3_), custom_call_target="tpu_custom_call" | custom-call | flops 1048576 | bytes 1024 | tf_op jit(solution)/shard_map/pallas_call | solution.py:156
  26.1 4.3 %collective-permute-done.refs_2_ = bf16[8,192,128]{2,1,0:T(8,128)(2,1)S(1)} collective-permute-done((bf16[8,192,128]{2,1,0:T(8,128)(2,1)S(1)}, bf16[8,192,128]{2,1,0:T(8,128)(2,1)S(1)}, u32[]{:S(2)}, u32[]{:S(2)}) %collective-permute-start) | collective-permute-done | bytes 393248 | tf_op jit(solution)/shard_map/ppermute | solution.py:284
  30.4 0.9 %collective-permute-done.1.refs_2_ = bf16[8,192,128]{2,1,0:T(8,128)(2,1)S(1)} collective-permute-done((bf16[8,192,128]{2,1,0:T(8,128)(2,1)S(1)}, bf16[8,192,128]{2,1,0:T(8,128)(2,1)S(1)}, u32[]{:S(2)}, u32[]{:S(2)}) %collective-permute-start.1) | collective-permute-done | bytes 393248 | tf_op jit(solution)/shard_map/ppermute | solution.py:284
  31.4 0.0 collective-permute-start.6
  31.4 0.5 collective-permute-start.5
  31.9 0.0 slice-start
  31.9 0.0 copy-start
  31.9 0.0 copy-start.2
  31.9 1.8 %collective-permute-start.3 = (bf16[8,96,128]{2,1,0:T(8,128)(2,1)S(1)}, bf16[8,96,128]{2,1,0:T(8,128)(2,1)S(1)}, u32[]{:S(2)}, u32[]{:S(2)}) collective-permute-start(bf16[8,96,128]{2,1,0:T(8,128)(2,1)S(1)} %slice.14), channel_id=1, source_target_pairs={{0,64},{64,128},{128,192},{192,0},{1,65},{65,129},{129,193},{193,1... | collective-permute-start | bytes 589832 | tf_op jit(solution)/shard_map/ppermute | solution.py:284
  33.7 0.3 collective-permute-start.4
  34.1 0.0 collective-permute-done.6.refs_3_
  34.1 1.9 %shard_map.83 = (f32[1024,128]{1,0:T(8,128)S(1)}, f32[1024,256]{1,0:T(8,128)S(1)}) custom-call(bf16[8,336,128]{2,1,0:T(8,128)(2,1)S(1)} %all_to_all.10.refs_0_, bf16[4,1024,128]{2,1,0:T(8,128)(2,1)S(1)} %bias.1.refs_1_, bf16[8,192,128]{2,1,0:T(8,128)(2,1)S(1)} %collective-permute-done.refs_2_, bf16[8,192,128]{2,1,0:T(8,128)(2,1)S(1)} %collective-permute-done.6.refs_3_, ...), custom_call_target="tpu_custom_call" | custom-call | flops 1048576 | bytes 1024 | tf_op jit(solution)/shard_map/pallas_call | solution.py:156
  36.0 0.0 collective-permute-done.5.refs_3_
  36.0 0.0 slice-start.1
  36.0 1.9 %shard_map.84 = (f32[1024,128]{1,0:T(8,128)S(1)}, f32[1024,256]{1,0:T(8,128)S(1)}) custom-call(bf16[8,336,128]{2,1,0:T(8,128)(2,1)S(1)} %all_to_all.10.refs_0_, bf16[4,1024,128]{2,1,0:T(8,128)(2,1)S(1)} %bias.1.refs_1_, bf16[8,192,128]{2,1,0:T(8,128)(2,1)S(1)} %collective-permute-done.1.refs_2_, bf16[8,192,128]{2,1,0:T(8,128)(2,1)S(1)} %collective-permute-done.5.refs_3_, ...), custom_call_target="tpu_custom_call" | custom-call | flops 1048576 | bytes 1024 | tf_op jit(solution)/shard_map/pallas_call | solution.py:156
  38.0 0.9 %collective-permute-done.3.refs_2_ = bf16[8,96,128]{2,1,0:T(8,128)(2,1)S(1)} collective-permute-done((bf16[8,96,128]{2,1,0:T(8,128)(2,1)S(1)}, bf16[8,96,128]{2,1,0:T(8,128)(2,1)S(1)}, u32[]{:S(2)}, u32[]{:S(2)}) %collective-permute-start.3) | collective-permute-done | bytes 196640 | tf_op jit(solution)/shard_map/ppermute | solution.py:284
  38.8 1.4 %collective-permute-done.4.refs_3_ = bf16[8,96,128]{2,1,0:T(8,128)(2,1)S(1)} collective-permute-done((bf16[8,96,128]{2,1,0:T(8,128)(2,1)S(1)}, bf16[8,96,128]{2,1,0:T(8,128)(2,1)S(1)}, u32[]{:S(2)}, u32[]{:S(2)}) %collective-permute-start.4) | collective-permute-done | bytes 196640 | tf_op jit(solution)/shard_map/ppermute | solution.py:284
  40.2 0.0 collective-permute-start.7
  40.2 0.5 collective-permute-start.8
  40.8 1.3 %shard_map.85 = (f32[1024,128]{1,0:T(8,128)S(1)}, f32[1024,256]{1,0:T(8,128)S(1)}) custom-call(bf16[8,336,128]{2,1,0:T(8,128)(2,1)S(1)} %all_to_all.10.refs_0_, bf16[4,1024,128]{2,1,0:T(8,128)(2,1)S(1)} %bias.1.refs_1_, bf16[8,96,128]{2,1,0:T(8,128)(2,1)S(1)} %collective-permute-done.3.refs_2_, bf16[8,96,128]{2,1,0:T(8,128)(2,1)S(1)} %collective-permute-done.4.refs_3_, ...), custom_call_target="tpu_custom_call" | custom-call | flops 1048576 | bytes 1024 | tf_op jit(solution)/shard_map/pallas_call | solution.py:156
  42.0 0.0 collective-permute-done.7.refs_2_
  42.0 0.0 collective-permute-done.8.refs_3_
  42.1 1.3 %shard_map.86 = bf16[8,128,128]{2,1,0:T(8,128)(2,1)S(1)} custom-call(bf16[8,336,128]{2,1,0:T(8,128)(2,1)S(1)} %all_to_all.10.refs_0_, bf16[4,1024,128]{2,1,0:T(8,128)(2,1)S(1)} %bias.1.refs_1_, bf16[8,96,128]{2,1,0:T(8,128)(2,1)S(1)} %collective-permute-done.7.refs_2_, bf16[8,96,128]{2,1,0:T(8,128)(2,1)S(1)} %collective-permute-done.8.refs_3_, ...), custom_call_target="tpu_custom_call" | custom-call | flops 1048576 | bytes 1024 | tf_op jit(solution)/shard_map/pallas_call | solution.py:156
  43.3 10.2 %all_to_all.11.rec_ref = bf16[8,128,128]{2,1,0:T(8,128)(2,1)S(1)} all-to-all(bf16[8,128,128]{2,1,0:T(8,128)(2,1)S(1)} %shard_map.86), channel_id=1, replica_groups=mesh['x'=4,'zl'=2,'y'=4,'c'=2,'h'=4] {'zl','y'}, dimensions={0} | all-to-all | bytes 524288 | tf_op jit(solution)/shard_map/all_to_all | solution.py:306
  53.5 0.0 copy-done
  53.5 1.8 %project.1 = (bf16[16,4096]{1,0:T(8,128)(2,1)S(1)}, bf16[16,4096]{1,0:T(8,128)(2,1)S(1)}, bf16[16,4096]{1,0:T(8,128)(2,1)S(1)}, bf16[16,4096]{1,0:T(8,128)(2,1)S...) custom-call(s32[3]{0:T(128)S(1)} %pad_add_fusion.place_ref, ...), custom_call_target="tpu_custom_call" | custom-call | flops 1073741824 | bytes 10485760 | tf_op jit(solution)/shard_map/project/pallas_call | solution.py:194
  55.4 5.5 %collective-permute-start.12 = (bf16[16,4096]{1,0:T(8,128)(2,1)S(1)}, bf16[16,4096]{1,0:T(8,128)(2,1)S(1)}, u32[]{:S(2)}, u32[]{:S(2)}) collective-permute-start(bf16[16,4096]{1,0:T(8,128)(2,1)S(1)} %get-tuple-element.49), channel_id=1, source_target_pairs={{0,3},{1,0},{2,1},{3,2},{4,7},{5,4},{6,5},{7,6},{8,11},{9,8},{10,9... | collective-permute-start | bytes 393224 | tf_op jit(solution)/shard_map/ppermute | solution.py:309
  60.9 0.0 collective-permute-start.9
  60.9 2.0 %collective-permute-start.11 = (bf16[16,4096]{1,0:T(8,128)(2,1)S(1)}, bf16[16,4096]{1,0:T(8,128)(2,1)S(1)}, u32[]{:S(2)}, u32[]{:S(2)}) collective-permute-start(bf16[16,4096]{1,0:T(8,128)(2,1)S(1)} %get-tuple-element.47), channel_id=1, source_target_pairs={{0,1},{1,2},{2,3},{3,0},{4,5},{5,6},{6,7},{7,4},{8,9},{9,10},{10,1... | collective-permute-start | bytes 393224 | tf_op jit(solution)/shard_map/ppermute | solution.py:309
  62.9 2.2 %collective-permute-start.14 = (bf16[16,4096]{1,0:T(8,128)(2,1)S(1)}, bf16[16,4096]{1,0:T(8,128)(2,1)S(1)}, u32[]{:S(2)}, u32[]{:S(2)}) collective-permute-start(bf16[16,4096]{1,0:T(8,128)(2,1)S(1)} %get-tuple-element.50), channel_id=1, source_target_pairs={{0,3},{1,0},{2,1},{3,2},{4,7},{5,4},{6,5},{7,6},{8,11},{9,8},{10,9... | collective-permute-start | bytes 393224 | tf_op jit(solution)/shard_map/ppermute | solution.py:309
  65.0 1.0 %collective-permute-done.12.b_ref = bf16[16,4096]{1,0:T(8,128)(2,1)S(1)} collective-permute-done((bf16[16,4096]{1,0:T(8,128)(2,1)S(1)}, bf16[16,4096]{1,0:T(8,128)(2,1)S(1)}, u32[]{:S(2)}, u32[]{:S(2)}) %collective-permute-start.12) | collective-permute-done | bytes 131104 | tf_op jit(solution)/shard_map/ppermute | solution.py:309
  66.1 5.0 %collective-permute-start.13 = (bf16[16,4096]{1,0:T(8,128)(2,1)S(1)}, bf16[16,4096]{1,0:T(8,128)(2,1)S(1)}, u32[]{:S(2)}, u32[]{:S(2)}) collective-permute-start(bf16[16,4096]{1,0:T(8,128)(2,1)S(1)} %shard_map.88), channel_id=1, source_target_pairs={{0,3},{1,0},{2,1},{3,2},{4,7},{5,4},{6,5},{7,6},{8,11},{9,8},{10,9... | collective-permute-start | bytes 393224 | tf_op jit(solution)/shard_map/ppermute | solution.py:309
  71.1 0.0 collective-permute-done.9.b_ref
  71.1 0.1 collective-permute-start.10
  71.2 0.7 collective-permute-done.11.up_free_ref
  71.9 0.7 collective-permute-done.14.down_free_ref
  72.6 3.8 %collective-permute-done.13.down_ref = bf16[16,4096]{1,0:T(8,128)(2,1)S(1)} collective-permute-done((bf16[16,4096]{1,0:T(8,128)(2,1)S(1)}, bf16[16,4096]{1,0:T(8,128)(2,1)S(1)}, u32[]{:S(2)}, u32[]{:S(2)}) %collective-permute-start.13) | collective-permute-done | bytes 131104 | tf_op jit(solution)/shard_map/ppermute | solution.py:309
  76.4 4.3 %collective-permute-done.10.up_ref = bf16[16,4096]{1,0:T(8,128)(2,1)S(1)} collective-permute-done((bf16[16,4096]{1,0:T(8,128)(2,1)S(1)}, bf16[16,4096]{1,0:T(8,128)(2,1)S(1)}, u32[]{:S(2)}, u32[]{:S(2)}) %collective-permute-start.10) | collective-permute-done | bytes 131104 | tf_op jit(solution)/shard_map/ppermute | solution.py:309
  80.7 0.8 finish.1
  (11 shorter events, 0.1 us)
Async XLA Ops:
  18.8 5.4 %collective-permute-start.2 = (bf16[8,192,128]{2,1,0:T(8,128)(2,1)S(1)}, bf16[8,192,128]{2,1,0:T(8,128)(2,1)S(1)}, u32[]{:S(2)}, u32[]{:S(2)}) collective-permute-start(bf16[8,192,128]{2,1,0:T(8,128)(2,1)S(1)} %slice.17.refs_2_), channel_id=1, source_target_pairs={{0,4},{4,0},{1,5},{5,1},{2,6},{6,2},{3,7},{7,3},{8,12},{12,8},{9,1... | collective-permute-start | bytes 1179656 | tf_op jit(solution)/shard_map/ppermute | solution.py:287
  18.9 11.5 %collective-permute-start = (bf16[8,192,128]{2,1,0:T(8,128)(2,1)S(1)}, bf16[8,192,128]{2,1,0:T(8,128)(2,1)S(1)}, u32[]{:S(2)}, u32[]{:S(2)}) collective-permute-start(bf16[8,192,128]{2,1,0:T(8,128)(2,1)S(1)} %slice.17.refs_2_), channel_id=1, source_target_pairs={{0,64},{64,128},{128,192},{192,0},{1,65},{65,129},{129,193},{193,1... | collective-permute-start | bytes 1179656 | tf_op jit(solution)/shard_map/ppermute | solution.py:284
  20.2 11.2 %collective-permute-start.1 = (bf16[8,192,128]{2,1,0:T(8,128)(2,1)S(1)}, bf16[8,192,128]{2,1,0:T(8,128)(2,1)S(1)}, u32[]{:S(2)}, u32[]{:S(2)}) collective-permute-start(bf16[8,192,128]{2,1,0:T(8,128)(2,1)S(1)} %slice.17.refs_2_), channel_id=1, source_target_pairs={{0,192},{64,0},{128,64},{192,128},{1,193},{65,1},{129,65},{193,129... | collective-permute-start | bytes 1179656 | tf_op jit(solution)/shard_map/ppermute | solution.py:284
  21.1 0.8 copy-start.1
  31.4 2.7 %collective-permute-start.6 = (bf16[8,192,128]{2,1,0:T(8,128)(2,1)S(1)}, bf16[8,192,128]{2,1,0:T(8,128)(2,1)S(1)}, u32[]{:S(2)}, u32[]{:S(2)}) collective-permute-start(bf16[8,192,128]{2,1,0:T(8,128)(2,1)S(1)} %collective-permute-done.refs_2_), channel_id=1, source_target_pairs={{0,4},{4,0},{1,5},{5,1},{2,6},{6,2},{3,7},{7,3},{8,12},{12,8},{9,1... | collective-permute-start | bytes 1179656 | tf_op jit(solution)/shard_map/ppermute | solution.py:287
  31.4 4.6 %collective-permute-start.5 = (bf16[8,192,128]{2,1,0:T(8,128)(2,1)S(1)}, bf16[8,192,128]{2,1,0:T(8,128)(2,1)S(1)}, u32[]{:S(2)}, u32[]{:S(2)}) collective-permute-start(bf16[8,192,128]{2,1,0:T(8,128)(2,1)S(1)} %collective-permute-done.1.refs_2_), channel_id=1, source_target_pairs={{0,4},{4,0},{1,5},{5,1},{2,6},{6,2},{3,7},{7,3},{8,12},{12,8},{9,1... | collective-permute-start | bytes 1179656 | tf_op jit(solution)/shard_map/ppermute | solution.py:287
  31.9 21.6 %slice-start = ((s8[8388608]{0:T(1024)(128)(4,1)}), s8[4194304]{0:T(1024)(128)(4,1)S(1)}, s32[]{:S(2)}) async-start(s8[8388608]{0:T(1024)(128)(4,1)} %bitcast.4), calls=%async_computation.2 | async-start | bytes 8388608
  31.9 21.6 %copy-start = (bf16[128,1024]{1,0:T(8,128)(2,1)S(1)}, bf16[128,1024]{1,0:T(8,128)(2,1)}, u32[]{:S(2)}) copy-start(bf16[128,1024]{1,0:T(8,128)(2,1)} %own_ref.1) | copy-start | bytes 786436
  31.9 21.6 %copy-start.2 = (f32[8]{0:T(128)S(1)}, f32[8]{0:T(128)}, u32[]{:S(2)}) copy-start(f32[8]{0:T(128)} %gate_ref.1) | copy-start | bytes 100
  31.9 6.9 %collective-permute-start.3 = (bf16[8,96,128]{2,1,0:T(8,128)(2,1)S(1)}, bf16[8,96,128]{2,1,0:T(8,128)(2,1)S(1)}, u32[]{:S(2)}, u32[]{:S(2)}) collective-permute-start(bf16[8,96,128]{2,1,0:T(8,128)(2,1)S(1)} %slice.14), channel_id=1, source_target_pairs={{0,64},{64,128},{128,192},{192,0},{1,65},{65,129},{129,193},{193,1... | collective-permute-start | bytes 589832 | tf_op jit(solution)/shard_map/ppermute | solution.py:284
  33.7 6.5 %collective-permute-start.4 = (bf16[8,96,128]{2,1,0:T(8,128)(2,1)S(1)}, bf16[8,96,128]{2,1,0:T(8,128)(2,1)S(1)}, u32[]{:S(2)}, u32[]{:S(2)}) collective-permute-start(bf16[8,96,128]{2,1,0:T(8,128)(2,1)S(1)} %slice.15), channel_id=1, source_target_pairs={{0,192},{64,0},{128,64},{192,128},{1,193},{65,1},{129,65},{193,129... | collective-permute-start | bytes 589832 | tf_op jit(solution)/shard_map/ppermute | solution.py:284
  36.0 17.5 %slice-start.1 = ((s8[8388608]{0:T(1024)(128)(4,1)}), s8[4194304]{0:T(1024)(128)(4,1)S(1)}, s32[]{:S(2)}) async-start(s8[8388608]{0:T(1024)(128)(4,1)} %bitcast.4), calls=%async_computation.3 | async-start | bytes 8388608
  40.2 1.8 %collective-permute-start.7 = (bf16[8,96,128]{2,1,0:T(8,128)(2,1)S(1)}, bf16[8,96,128]{2,1,0:T(8,128)(2,1)S(1)}, u32[]{:S(2)}, u32[]{:S(2)}) collective-permute-start(bf16[8,96,128]{2,1,0:T(8,128)(2,1)S(1)} %collective-permute-done.3.refs_2_), channel_id=1, source_target_pairs={{0,4},{4,0},{1,5},{5,1},{2,6},{6,2},{3,7},{7,3},{8,12},{12,8},{9,1... | collective-permute-start | bytes 589832 | tf_op jit(solution)/shard_map/ppermute | solution.py:287
  40.2 1.8 %collective-permute-start.8 = (bf16[8,96,128]{2,1,0:T(8,128)(2,1)S(1)}, bf16[8,96,128]{2,1,0:T(8,128)(2,1)S(1)}, u32[]{:S(2)}, u32[]{:S(2)}) collective-permute-start(bf16[8,96,128]{2,1,0:T(8,128)(2,1)S(1)} %collective-permute-done.4.refs_3_), channel_id=1, source_target_pairs={{0,4},{4,0},{1,5},{5,1},{2,6},{6,2},{3,7},{7,3},{8,12},{12,8},{9,1... | collective-permute-start | bytes 589832 | tf_op jit(solution)/shard_map/ppermute | solution.py:287
  55.4 10.7 %collective-permute-start.12 = (bf16[16,4096]{1,0:T(8,128)(2,1)S(1)}, bf16[16,4096]{1,0:T(8,128)(2,1)S(1)}, u32[]{:S(2)}, u32[]{:S(2)}) collective-permute-start(bf16[16,4096]{1,0:T(8,128)(2,1)S(1)} %get-tuple-element.49), channel_id=1, source_target_pairs={{0,3},{1,0},{2,1},{3,2},{4,7},{5,4},{6,5},{7,6},{8,11},{9,8},{10,9... | collective-permute-start | bytes 393224 | tf_op jit(solution)/shard_map/ppermute | solution.py:309
  60.9 10.2 %collective-permute-start.9 = (bf16[16,4096]{1,0:T(8,128)(2,1)S(1)}, bf16[16,4096]{1,0:T(8,128)(2,1)S(1)}, u32[]{:S(2)}, u32[]{:S(2)}) collective-permute-start(bf16[16,4096]{1,0:T(8,128)(2,1)S(1)} %get-tuple-element.46), channel_id=1, source_target_pairs={{0,1},{1,2},{2,3},{3,0},{4,5},{5,6},{6,7},{7,4},{8,9},{9,10},{10,1... | collective-permute-start | bytes 393224 | tf_op jit(solution)/shard_map/ppermute | solution.py:309
  60.9 11.0 %collective-permute-start.11 = (bf16[16,4096]{1,0:T(8,128)(2,1)S(1)}, bf16[16,4096]{1,0:T(8,128)(2,1)S(1)}, u32[]{:S(2)}, u32[]{:S(2)}) collective-permute-start(bf16[16,4096]{1,0:T(8,128)(2,1)S(1)} %get-tuple-element.47), channel_id=1, source_target_pairs={{0,1},{1,2},{2,3},{3,0},{4,5},{5,6},{6,7},{7,4},{8,9},{9,10},{10,1... | collective-permute-start | bytes 393224 | tf_op jit(solution)/shard_map/ppermute | solution.py:309
  62.9 9.7 %collective-permute-start.14 = (bf16[16,4096]{1,0:T(8,128)(2,1)S(1)}, bf16[16,4096]{1,0:T(8,128)(2,1)S(1)}, u32[]{:S(2)}, u32[]{:S(2)}) collective-permute-start(bf16[16,4096]{1,0:T(8,128)(2,1)S(1)} %get-tuple-element.50), channel_id=1, source_target_pairs={{0,3},{1,0},{2,1},{3,2},{4,7},{5,4},{6,5},{7,6},{8,11},{9,8},{10,9... | collective-permute-start | bytes 393224 | tf_op jit(solution)/shard_map/ppermute | solution.py:309
  66.1 10.3 %collective-permute-start.13 = (bf16[16,4096]{1,0:T(8,128)(2,1)S(1)}, bf16[16,4096]{1,0:T(8,128)(2,1)S(1)}, u32[]{:S(2)}, u32[]{:S(2)}) collective-permute-start(bf16[16,4096]{1,0:T(8,128)(2,1)S(1)} %shard_map.88), channel_id=1, source_target_pairs={{0,3},{1,0},{2,1},{3,2},{4,7},{5,4},{6,5},{7,6},{8,11},{9,8},{10,9... | collective-permute-start | bytes 393224 | tf_op jit(solution)/shard_map/ppermute | solution.py:309
  71.1 9.6 %collective-permute-start.10 = (bf16[16,4096]{1,0:T(8,128)(2,1)S(1)}, bf16[16,4096]{1,0:T(8,128)(2,1)S(1)}, u32[]{:S(2)}, u32[]{:S(2)}) collective-permute-start(bf16[16,4096]{1,0:T(8,128)(2,1)S(1)} %shard_map.87), channel_id=1, source_target_pairs={{0,1},{1,2},{2,3},{3,0},{4,5},{5,6},{6,7},{7,4},{8,9},{9,10},{10,1... | collective-permute-start | bytes 393224 | tf_op jit(solution)/shard_map/ppermute | solution.py:309

commit v4 on v3

--- a/solution.py
+++ b/solution.py
@@ -216,21 +216,29 @@
     )(*[in_vmem(arg) for arg in args])
 
 
-def finish_body(here_ref, up_ref, up_free_ref, down_ref, down_free_ref, out_ref):
-    half = ROWS_O // 2
-    for span, a_ref, b_ref in ((slice(0, half), up_ref, down_free_ref), (slice(half, 2 * half), up_free_ref, down_ref)):
-        total = here_ref[span, :] + a_ref[...].astype(jnp.float32) + b_ref[...].astype(jnp.float32)
-        out_ref[span, :] = total.astype(jnp.bfloat16)
-
-
-def finish(*args):
-    return pl.pallas_call(
-        finish_body,
-        in_specs=[VMEM_SPEC] * 5,
-        out_shape=jax.ShapeDtypeStruct(args[0].shape, jnp.bfloat16),
-        compiler_params=pltpu.CompilerParams(vmem_limit_bytes=16 << 20),
-        name="finish",
-    )(*[in_vmem(arg) for arg in args])
+def finish_body(half, here_ref, a_ref, b_ref, *rest):
+    rows = a_ref.shape[0]
+    total = here_ref[half * rows : (half + 1) * rows, :] + a_ref[...].astype(jnp.float32) + b_ref[...].astype(jnp.float32)
+    rest[-1][...] = total.astype(jnp.bfloat16)
+
+
+def finish(half, here, a, b, out=None):
+    rows, model = a.shape
+    block = pl.BlockSpec((rows, model), lambda i: (half, 0))
+    args = [in_vmem(here), in_vmem(a), in_vmem(b)]
+    in_specs = [VMEM_SPEC] * 3
+    if out is not None:
+        args.append(out)
+        in_specs.append(pl.BlockSpec(memory_space=pl.ANY))
+    return pl.pallas_call(
+        lambda *refs: finish_body(half, *refs),
+        grid=(1,),
+        in_specs=in_specs,
+        out_specs=block,
+        out_shape=jax.ShapeDtypeStruct((2 * rows, model), jnp.bfloat16),
+        input_output_aliases={} if out is None else {3: 0},
+        compiler_params=pltpu.CompilerParams(vmem_limit_bytes=16 << 20),
+    )(*args)
 
 
 def pack_body(q_ref, k_ref, v_ref, probe_hbm, out_ref, probe_ref, sems):
@@ -292,10 +300,11 @@
     own_far = swap(own)
     bias = make_bias(place, received[:, ROWS_Q + 2 * ROWS_M :, :], pattern)
     state = attend(0, received, bias, (own, own_far), None)
-    left, right, *state = lax.optimization_barrier((left, right, *state))
+    left, *state = lax.optimization_barrier((left, *state))
     opposite_k = shift(left[:, :ROWS_M], 1)
+    left_far = swap(left)
+    right, *state = lax.optimization_barrier((right, *state))
     opposite_v = shift(right[:, ROWS_M:], 3)
-    left_far = swap(left)
     right_far = swap(right)
     state = attend(1, received, bias, (left, left_far), state)
     state = attend(2, received, bias, (right, right_far), state)
@@ -315,7 +324,8 @@
     down_free = plane_shift(down_free, 3)
     up = plane_shift(add(up, top), 1)
     down = plane_shift(add(down, bottom), 3)
-    return finish(here, up, up_free, down, down_free)
+    out = finish(1, here, up_free, down)
+    return finish(0, here, up, down_free, out)
 
 
 def solution(mesh):

time: 82.7 us -> 84.8 us (1.025)
  the two profiles are of different devices: /device:TPU:4 before, /device:TPU:40 now
where the time goes in v4:
time: 84.8 us; the launch traced here: 84.5 us
  blocking collectives  25.7 us (30%)
  starting transfers between devices  21.8 us (26%)
  waiting for transfers between devices  20.6 us (24%)
  Pallas kernels  15.2 us (18%)
    all_to_all x1, blocking collectives, local(): lax.all_to_all(pack(queries, mem_keys, mem_values, probes.T), B_AXES, 0,...  15.4 us
    ppermute x6, starting transfers between devices, plane_shift(): return lax.ppermute(array, 'h', [(i, (i + by) % NH) for i in range(NH)])  14.9 us
    ppermute x6, waiting for transfers between devices, plane_shift(): return lax.ppermute(array, 'h', [(i, (i + by) % NH) for i in range(NH)])  12 us
    all_to_all x1, blocking collectives, local(): recalled = lax.all_to_all(state, B_AXES, 0, 0, tiled=True)  10.3 us
    ppermute x4, waiting for transfers between devices, shift(): return lax.ppermute(array, 'x', [(i, (i + by) % NX) for i in range(NX)])  8.65 us
    pallas_call x5, Pallas kernels, attend(): pl.pallas_call(lambda *refs: chunk_body(k, slots, parts, first, last, *re...  8.29 us
    ppermute x4, starting transfers between devices, shift(): return lax.ppermute(array, 'x', [(i, (i + by) % NX) for i in range(NX)])  5.84 us
    pallas_call x1, Pallas kernels, make_bias(): pl.pallas_call(bias_body, in_specs=[SMEM_SPEC, VMEM_SPEC, VMEM_SPEC], out...  2.35 us
  transfers between devices with their start and end apart: 15, of which 7 were waited for; matrix products, arithmetic and copies ran while one was open for 0% of the time, Pallas kernels for 12%

profile of v4, /device:TPU:40, one launch (start us, length us, event | category | flops | bytes accessed | tf_op | source)
XLA Modules:
  0.0 84.5 jit_solution(13369598279651597662)
XLA Ops:
  0.0 1.3 %pack.1 = bf16[8,336,128]{2,1,0:T(8,128)(2,1)S(1)} custom-call(bf16[128,1024]{1,0:T(8,128)(2,1)} %q_ref.1, bf16[96,1024]{1,0:T(8,128)(2,1)} %k_ref.1, bf16[96,1024]{1,0:T(8,128)(2,1)} %v_ref.1, s32[8,128]{1,0:T(8,128)} %bitcast.6), custom_call_target="tpu_custom_call" | custom-call | tf_op jit(solution)/shard_map/pack/pallas_call | solution.py:276
  1.3 15.4 %all_to_all.10.refs_0_ = bf16[8,336,128]{2,1,0:T(8,128)(2,1)S(1)} all-to-all(bf16[8,336,128]{2,1,0:T(8,128)(2,1)S(1)} %pack.1), channel_id=1, replica_groups=mesh['x'=4,'zl'=2,'y'=4,'c'=2,'h'=4] {'zl','y'}, dimensions={0} | all-to-all | bytes 1376256 | tf_op jit(solution)/shard_map/all_to_all | solution.py:288
  16.7 0.1 collective-permute-start.1
  16.8 1.6 %collective-permute-start = (bf16[8,192,128]{2,1,0:T(8,128)(2,1)S(1)}, bf16[8,192,128]{2,1,0:T(8,128)(2,1)S(1)}, u32[]{:S(2)}, u32[]{:S(2)}) collective-permute-start(bf16[8,192,128]{2,1,0:T(8,128)(2,1)S(1)} %slice.17.refs_2_), channel_id=1, source_target_pairs={{0,64},{64,128},{128,192},{192,0},{1,65},{65,129},{129,193},{193,1... | collective-permute-start | bytes 1179656 | tf_op jit(solution)/shard_map/ppermute | solution.py:292
  18.4 1.7 %collective-permute-start.3 = (bf16[8,192,128]{2,1,0:T(8,128)(2,1)S(1)}, bf16[8,192,128]{2,1,0:T(8,128)(2,1)S(1)}, u32[]{:S(2)}, u32[]{:S(2)}) collective-permute-start(bf16[8,192,128]{2,1,0:T(8,128)(2,1)S(1)} %slice.17.refs_2_), channel_id=1, source_target_pairs={{0,192},{64,0},{128,64},{192,128},{1,193},{65,1},{129,65},{193,129... | collective-permute-start | bytes 1179656 | tf_op jit(solution)/shard_map/ppermute | solution.py:292
  20.1 0.1 pad_add_fusion.place_ref
  20.2 0.8 copy-done.1
  21.0 2.4 %bias.1.refs_1_ = bf16[4,1024,128]{2,1,0:T(8,128)(2,1)S(1)} custom-call(s32[3]{0:T(128)S(1)} %pad_add_fusion.place_ref, bf16[8,16,128]{2,1,0:T(8,128)(2,1)S(1)} %slice.16.probe_ref, s32[64,64]{1,0:T(8,128)S(1)} %copy-done.1), custom_call_target="tpu_custom_call" | custom-call | tf_op jit(solution)/shard_map/bias/pallas_call | solution.py:76
  23.3 0.0 collective-permute-done.1.refs_3_
  23.3 1.9 %shard_map.82 = (f32[1024,128]{1,0:T(8,128)S(1)}, f32[1024,256]{1,0:T(8,128)S(1)}) custom-call(bf16[8,336,128]{2,1,0:T(8,128)(2,1)S(1)} %all_to_all.10.refs_0_, bf16[4,1024,128]{2,1,0:T(8,128)(2,1)S(1)} %bias.1.refs_1_, bf16[8,192,128]{2,1,0:T(8,128)(2,1)S(1)} %slice.17.refs_2_, bf16[8,192,128]{2,1,0:T(8,128)(2,1)S(1)} %collective-permute-done.1.refs_3_), custom_call_target="tpu_custom_call" | custom-call | flops 1048576 | bytes 1024 | tf_op jit(solution)/shard_map/pallas_call | solution.py:156
  25.2 4.3 %collective-permute-done.refs_2_ = bf16[8,192,128]{2,1,0:T(8,128)(2,1)S(1)} collective-permute-done((bf16[8,192,128]{2,1,0:T(8,128)(2,1)S(1)}, bf16[8,192,128]{2,1,0:T(8,128)(2,1)S(1)}, u32[]{:S(2)}, u32[]{:S(2)}) %collective-permute-start) | collective-permute-done | bytes 393248 | tf_op jit(solution)/shard_map/ppermute | solution.py:292
  29.5 0.0 collective-permute-start.6
  29.5 0.0 collective-permute-done.3.refs_2_
  29.5 0.5 collective-permute-start.5
  30.1 0.0 slice-start
  30.1 0.0 copy-start
  30.1 0.0 copy-start.2
  30.1 2.5 %collective-permute-start.4 = (bf16[8,96,128]{2,1,0:T(8,128)(2,1)S(1)}, bf16[8,96,128]{2,1,0:T(8,128)(2,1)S(1)}, u32[]{:S(2)}, u32[]{:S(2)}) collective-permute-start(bf16[8,96,128]{2,1,0:T(8,128)(2,1)S(1)} %slice.15), channel_id=1, source_target_pairs={{0,192},{64,0},{128,64},{192,128},{1,193},{65,1},{129,65},{193,129... | collective-permute-start | bytes 589832 | tf_op jit(solution)/shard_map/ppermute | solution.py:292
  32.6 0.0 collective-permute-start.2
  32.7 0.0 collective-permute-done.6.refs_3_
  32.7 1.9 %shard_map.83 = (f32[1024,128]{1,0:T(8,128)S(1)}, f32[1024,256]{1,0:T(8,128)S(1)}) custom-call(bf16[8,336,128]{2,1,0:T(8,128)(2,1)S(1)} %all_to_all.10.refs_0_, bf16[4,1024,128]{2,1,0:T(8,128)(2,1)S(1)} %bias.1.refs_1_, bf16[8,192,128]{2,1,0:T(8,128)(2,1)S(1)} %collective-permute-done.refs_2_, bf16[8,192,128]{2,1,0:T(8,128)(2,1)S(1)} %collective-permute-done.6.refs_3_, ...), custom_call_target="tpu_custom_call" | custom-call | flops 1048576 | bytes 1024 | tf_op jit(solution)/shard_map/pallas_call | solution.py:156
  34.6 0.0 collective-permute-done.5.refs_3_
  34.6 0.0 slice-start.1
  34.6 1.9 %shard_map.84 = (f32[1024,128]{1,0:T(8,128)S(1)}, f32[1024,256]{1,0:T(8,128)S(1)}) custom-call(bf16[8,336,128]{2,1,0:T(8,128)(2,1)S(1)} %all_to_all.10.refs_0_, bf16[4,1024,128]{2,1,0:T(8,128)(2,1)S(1)} %bias.1.refs_1_, bf16[8,192,128]{2,1,0:T(8,128)(2,1)S(1)} %collective-permute-done.3.refs_2_, bf16[8,192,128]{2,1,0:T(8,128)(2,1)S(1)} %collective-permute-done.5.refs_3_, ...), custom_call_target="tpu_custom_call" | custom-call | flops 1048576 | bytes 1024 | tf_op jit(solution)/shard_map/pallas_call | solution.py:156
  36.6 0.9 %collective-permute-done.4.refs_3_ = bf16[8,96,128]{2,1,0:T(8,128)(2,1)S(1)} collective-permute-done((bf16[8,96,128]{2,1,0:T(8,128)(2,1)S(1)}, bf16[8,96,128]{2,1,0:T(8,128)(2,1)S(1)}, u32[]{:S(2)}, u32[]{:S(2)}) %collective-permute-start.4) | collective-permute-done | bytes 196640 | tf_op jit(solution)/shard_map/ppermute | solution.py:292
  37.5 3.4 %collective-permute-done.2.refs_2_ = bf16[8,96,128]{2,1,0:T(8,128)(2,1)S(1)} collective-permute-done((bf16[8,96,128]{2,1,0:T(8,128)(2,1)S(1)}, bf16[8,96,128]{2,1,0:T(8,128)(2,1)S(1)}, u32[]{:S(2)}, u32[]{:S(2)}) %collective-permute-start.2) | collective-permute-done | bytes 196640 | tf_op jit(solution)/shard_map/ppermute | solution.py:292
  40.9 0.0 collective-permute-start.7
  40.9 0.5 collective-permute-start.8
  41.4 1.3 %shard_map.85 = (f32[1024,128]{1,0:T(8,128)S(1)}, f32[1024,256]{1,0:T(8,128)S(1)}) custom-call(bf16[8,336,128]{2,1,0:T(8,128)(2,1)S(1)} %all_to_all.10.refs_0_, bf16[4,1024,128]{2,1,0:T(8,128)(2,1)S(1)} %bias.1.refs_1_, bf16[8,96,128]{2,1,0:T(8,128)(2,1)S(1)} %collective-permute-done.2.refs_2_, bf16[8,96,128]{2,1,0:T(8,128)(2,1)S(1)} %collective-permute-done.4.refs_3_, ...), custom_call_target="tpu_custom_call" | custom-call | flops 1048576 | bytes 1024 | tf_op jit(solution)/shard_map/pallas_call | solution.py:156
  42.7 0.0 collective-permute-done.7.refs_2_
  42.7 0.0 collective-permute-done.8.refs_3_
  42.7 1.3 %shard_map.86 = bf16[8,128,128]{2,1,0:T(8,128)(2,1)S(1)} custom-call(bf16[8,336,128]{2,1,0:T(8,128)(2,1)S(1)} %all_to_all.10.refs_0_, bf16[4,1024,128]{2,1,0:T(8,128)(2,1)S(1)} %bias.1.refs_1_, bf16[8,96,128]{2,1,0:T(8,128)(2,1)S(1)} %collective-permute-done.7.refs_2_, bf16[8,96,128]{2,1,0:T(8,128)(2,1)S(1)} %collective-permute-done.8.refs_3_, ...), custom_call_target="tpu_custom_call" | custom-call | flops 1048576 | bytes 1024 | tf_op jit(solution)/shard_map/pallas_call | solution.py:156
  44.0 10.3 %all_to_all.11.rec_ref = bf16[8,128,128]{2,1,0:T(8,128)(2,1)S(1)} all-to-all(bf16[8,128,128]{2,1,0:T(8,128)(2,1)S(1)} %shard_map.86), channel_id=1, replica_groups=mesh['x'=4,'zl'=2,'y'=4,'c'=2,'h'=4] {'zl','y'}, dimensions={0} | all-to-all | bytes 524288 | tf_op jit(solution)/shard_map/all_to_all | solution.py:315
  54.3 1.8 %project.1 = (bf16[16,4096]{1,0:T(8,128)(2,1)S(1)}, bf16[16,4096]{1,0:T(8,128)(2,1)S(1)}, bf16[16,4096]{1,0:T(8,128)(2,1)S(1)}, bf16[16,4096]{1,0:T(8,128)(2,1)S...) custom-call(s32[3]{0:T(128)S(1)} %pad_add_fusion.place_ref, ...), custom_call_target="tpu_custom_call" | custom-call | flops 1073741824 | bytes 10485760 | tf_op jit(solution)/shard_map/project/pallas_call | solution.py:194
  56.2 5.5 %collective-permute-start.13 = (bf16[16,4096]{1,0:T(8,128)(2,1)S(1)}, bf16[16,4096]{1,0:T(8,128)(2,1)S(1)}, u32[]{:S(2)}, u32[]{:S(2)}) collective-permute-start(bf16[16,4096]{1,0:T(8,128)(2,1)S(1)} %get-tuple-element.54), channel_id=1, source_target_pairs={{0,3},{1,0},{2,1},{3,2},{4,7},{5,4},{6,5},{7,6},{8,11},{9,8},{10,9... | collective-permute-start | bytes 393224 | tf_op jit(solution)/shard_map/ppermute | solution.py:318
  61.6 0.0 collective-permute-start.9
  61.6 2.0 %collective-permute-start.12 = (bf16[16,4096]{1,0:T(8,128)(2,1)S(1)}, bf16[16,4096]{1,0:T(8,128)(2,1)S(1)}, u32[]{:S(2)}, u32[]{:S(2)}) collective-permute-start(bf16[16,4096]{1,0:T(8,128)(2,1)S(1)} %get-tuple-element.52), channel_id=1, source_target_pairs={{0,1},{1,2},{2,3},{3,0},{4,5},{5,6},{6,7},{7,4},{8,9},{9,10},{10,1... | collective-permute-start | bytes 393224 | tf_op jit(solution)/shard_map/ppermute | solution.py:318
  63.6 2.2 %collective-permute-start.11 = (bf16[16,4096]{1,0:T(8,128)(2,1)S(1)}, bf16[16,4096]{1,0:T(8,128)(2,1)S(1)}, u32[]{:S(2)}, u32[]{:S(2)}) collective-permute-start(bf16[16,4096]{1,0:T(8,128)(2,1)S(1)} %get-tuple-element.51), channel_id=1, source_target_pairs={{0,3},{1,0},{2,1},{3,2},{4,7},{5,4},{6,5},{7,6},{8,11},{9,8},{10,9... | collective-permute-start | bytes 393224 | tf_op jit(solution)/shard_map/ppermute | solution.py:318
  65.8 1.1 %collective-permute-done.13.b_ref = bf16[16,4096]{1,0:T(8,128)(2,1)S(1)} collective-permute-done((bf16[16,4096]{1,0:T(8,128)(2,1)S(1)}, bf16[16,4096]{1,0:T(8,128)(2,1)S(1)}, u32[]{:S(2)}, u32[]{:S(2)}) %collective-permute-start.13) | collective-permute-done | bytes 131104 | tf_op jit(solution)/shard_map/ppermute | solution.py:318
  67.0 5.1 %collective-permute-start.14 = (bf16[16,4096]{1,0:T(8,128)(2,1)S(1)}, bf16[16,4096]{1,0:T(8,128)(2,1)S(1)}, u32[]{:S(2)}, u32[]{:S(2)}) collective-permute-start(bf16[16,4096]{1,0:T(8,128)(2,1)S(1)} %shard_map.88), channel_id=1, source_target_pairs={{0,3},{1,0},{2,1},{3,2},{4,7},{5,4},{6,5},{7,6},{8,11},{9,8},{10,9... | collective-permute-start | bytes 393224 | tf_op jit(solution)/shard_map/ppermute | solution.py:318
  72.1 3.6 %collective-permute-done.9.b_ref = bf16[16,4096]{1,0:T(8,128)(2,1)S(1)} collective-permute-done((bf16[16,4096]{1,0:T(8,128)(2,1)S(1)}, bf16[16,4096]{1,0:T(8,128)(2,1)S(1)}, u32[]{:S(2)}, u32[]{:S(2)}) %collective-permute-start.9) | collective-permute-done | bytes 131104 | tf_op jit(solution)/shard_map/ppermute | solution.py:318
  75.7 0.1 collective-permute-start.10
  75.8 2.8 %collective-permute-done.12.refs_1_ = bf16[16,4096]{1,0:T(8,128)(2,1)S(1)} collective-permute-done((bf16[16,4096]{1,0:T(8,128)(2,1)S(1)}, bf16[16,4096]{1,0:T(8,128)(2,1)S(1)}, u32[]{:S(2)}, u32[]{:S(2)}) %collective-permute-start.12) | collective-permute-done | bytes 131104 | tf_op jit(solution)/shard_map/ppermute | solution.py:318
  78.6 0.0 collective-permute-done.14.refs_2_
  78.6 0.7 shard_map.89.refs_3_
  79.3 0.0 collective-permute-done.11.refs_2_
  79.3 4.5 %collective-permute-done.10.refs_1_ = bf16[16,4096]{1,0:T(8,128)(2,1)S(1)} collective-permute-done((bf16[16,4096]{1,0:T(8,128)(2,1)S(1)}, bf16[16,4096]{1,0:T(8,128)(2,1)S(1)}, u32[]{:S(2)}, u32[]{:S(2)}) %collective-permute-start.10) | collective-permute-done | bytes 131104 | tf_op jit(solution)/shard_map/ppermute | solution.py:318
  83.8 0.7 shard_map.90
  (12 shorter events, 0.1 us)
Async XLA Ops:
  16.7 6.6 %collective-permute-start.1 = (bf16[8,192,128]{2,1,0:T(8,128)(2,1)S(1)}, bf16[8,192,128]{2,1,0:T(8,128)(2,1)S(1)}, u32[]{:S(2)}, u32[]{:S(2)}) collective-permute-start(bf16[8,192,128]{2,1,0:T(8,128)(2,1)S(1)} %slice.17.refs_2_), channel_id=1, source_target_pairs={{0,4},{4,0},{1,5},{5,1},{2,6},{6,2},{3,7},{7,3},{8,12},{12,8},{9,1... | collective-permute-start | bytes 1179656 | tf_op jit(solution)/shard_map/ppermute | solution.py:295
  16.8 12.7 %collective-permute-start = (bf16[8,192,128]{2,1,0:T(8,128)(2,1)S(1)}, bf16[8,192,128]{2,1,0:T(8,128)(2,1)S(1)}, u32[]{:S(2)}, u32[]{:S(2)}) collective-permute-start(bf16[8,192,128]{2,1,0:T(8,128)(2,1)S(1)} %slice.17.refs_2_), channel_id=1, source_target_pairs={{0,64},{64,128},{128,192},{192,0},{1,65},{65,129},{129,193},{193,1... | collective-permute-start | bytes 1179656 | tf_op jit(solution)/shard_map/ppermute | solution.py:292
  18.4 11.2 %collective-permute-start.3 = (bf16[8,192,128]{2,1,0:T(8,128)(2,1)S(1)}, bf16[8,192,128]{2,1,0:T(8,128)(2,1)S(1)}, u32[]{:S(2)}, u32[]{:S(2)}) collective-permute-start(bf16[8,192,128]{2,1,0:T(8,128)(2,1)S(1)} %slice.17.refs_2_), channel_id=1, source_target_pairs={{0,192},{64,0},{128,64},{192,128},{1,193},{65,1},{129,65},{193,129... | collective-permute-start | bytes 1179656 | tf_op jit(solution)/shard_map/ppermute | solution.py:292
  20.2 0.8 copy-start.1
  29.5 3.1 %collective-permute-start.6 = (bf16[8,192,128]{2,1,0:T(8,128)(2,1)S(1)}, bf16[8,192,128]{2,1,0:T(8,128)(2,1)S(1)}, u32[]{:S(2)}, u32[]{:S(2)}) collective-permute-start(bf16[8,192,128]{2,1,0:T(8,128)(2,1)S(1)} %collective-permute-done.refs_2_), channel_id=1, source_target_pairs={{0,4},{4,0},{1,5},{5,1},{2,6},{6,2},{3,7},{7,3},{8,12},{12,8},{9,1... | collective-permute-start | bytes 1179656 | tf_op jit(solution)/shard_map/ppermute | solution.py:295
  29.5 5.1 %collective-permute-start.5 = (bf16[8,192,128]{2,1,0:T(8,128)(2,1)S(1)}, bf16[8,192,128]{2,1,0:T(8,128)(2,1)S(1)}, u32[]{:S(2)}, u32[]{:S(2)}) collective-permute-start(bf16[8,192,128]{2,1,0:T(8,128)(2,1)S(1)} %collective-permute-done.3.refs_2_), channel_id=1, source_target_pairs={{0,4},{4,0},{1,5},{5,1},{2,6},{6,2},{3,7},{7,3},{8,12},{12,8},{9,1... | collective-permute-start | bytes 1179656 | tf_op jit(solution)/shard_map/ppermute | solution.py:295
  30.1 24.2 %slice-start = ((s8[8388608]{0:T(1024)(128)(4,1)}), s8[4194304]{0:T(1024)(128)(4,1)S(1)}, s32[]{:S(2)}) async-start(s8[8388608]{0:T(1024)(128)(4,1)} %bitcast.4), calls=%async_computation.2 | async-start | bytes 8388608
  30.1 24.2 %copy-start = (bf16[128,1024]{1,0:T(8,128)(2,1)S(1)}, bf16[128,1024]{1,0:T(8,128)(2,1)}, u32[]{:S(2)}) copy-start(bf16[128,1024]{1,0:T(8,128)(2,1)} %own_ref.1) | copy-start | bytes 786436
  30.1 24.2 %copy-start.2 = (f32[8]{0:T(128)S(1)}, f32[8]{0:T(128)}, u32[]{:S(2)}) copy-start(f32[8]{0:T(128)} %gate_ref.1) | copy-start | bytes 100
  30.1 7.4 %collective-permute-start.4 = (bf16[8,96,128]{2,1,0:T(8,128)(2,1)S(1)}, bf16[8,96,128]{2,1,0:T(8,128)(2,1)S(1)}, u32[]{:S(2)}, u32[]{:S(2)}) collective-permute-start(bf16[8,96,128]{2,1,0:T(8,128)(2,1)S(1)} %slice.15), channel_id=1, source_target_pairs={{0,192},{64,0},{128,64},{192,128},{1,193},{65,1},{129,65},{193,129... | collective-permute-start | bytes 589832 | tf_op jit(solution)/shard_map/ppermute | solution.py:292
  32.6 8.2 %collective-permute-start.2 = (bf16[8,96,128]{2,1,0:T(8,128)(2,1)S(1)}, bf16[8,96,128]{2,1,0:T(8,128)(2,1)S(1)}, u32[]{:S(2)}, u32[]{:S(2)}) collective-permute-start(bf16[8,96,128]{2,1,0:T(8,128)(2,1)S(1)} %slice.14), channel_id=1, source_target_pairs={{0,64},{64,128},{128,192},{192,0},{1,65},{65,129},{129,193},{193,1... | collective-permute-start | bytes 589832 | tf_op jit(solution)/shard_map/ppermute | solution.py:292
  34.6 19.7 %slice-start.1 = ((s8[8388608]{0:T(1024)(128)(4,1)}), s8[4194304]{0:T(1024)(128)(4,1)S(1)}, s32[]{:S(2)}) async-start(s8[8388608]{0:T(1024)(128)(4,1)} %bitcast.4), calls=%async_computation.3 | async-start | bytes 8388608
  40.9 1.8 %collective-permute-start.7 = (bf16[8,96,128]{2,1,0:T(8,128)(2,1)S(1)}, bf16[8,96,128]{2,1,0:T(8,128)(2,1)S(1)}, u32[]{:S(2)}, u32[]{:S(2)}) collective-permute-start(bf16[8,96,128]{2,1,0:T(8,128)(2,1)S(1)} %collective-permute-done.2.refs_2_), channel_id=1, source_target_pairs={{0,4},{4,0},{1,5},{5,1},{2,6},{6,2},{3,7},{7,3},{8,12},{12,8},{9,1... | collective-permute-start | bytes 589832 | tf_op jit(solution)/shard_map/ppermute | solution.py:295
  40.9 1.8 %collective-permute-start.8 = (bf16[8,96,128]{2,1,0:T(8,128)(2,1)S(1)}, bf16[8,96,128]{2,1,0:T(8,128)(2,1)S(1)}, u32[]{:S(2)}, u32[]{:S(2)}) collective-permute-start(bf16[8,96,128]{2,1,0:T(8,128)(2,1)S(1)} %collective-permute-done.4.refs_3_), channel_id=1, source_target_pairs={{0,4},{4,0},{1,5},{5,1},{2,6},{6,2},{3,7},{7,3},{8,12},{12,8},{9,1... | collective-permute-start | bytes 589832 | tf_op jit(solution)/shard_map/ppermute | solution.py:295
  56.2 10.8 %collective-permute-start.13 = (bf16[16,4096]{1,0:T(8,128)(2,1)S(1)}, bf16[16,4096]{1,0:T(8,128)(2,1)S(1)}, u32[]{:S(2)}, u32[]{:S(2)}) collective-permute-start(bf16[16,4096]{1,0:T(8,128)(2,1)S(1)} %get-tuple-element.54), channel_id=1, source_target_pairs={{0,3},{1,0},{2,1},{3,2},{4,7},{5,4},{6,5},{7,6},{8,11},{9,8},{10,9... | collective-permute-start | bytes 393224 | tf_op jit(solution)/shard_map/ppermute | solution.py:318
  61.6 14.1 %collective-permute-start.9 = (bf16[16,4096]{1,0:T(8,128)(2,1)S(1)}, bf16[16,4096]{1,0:T(8,128)(2,1)S(1)}, u32[]{:S(2)}, u32[]{:S(2)}) collective-permute-start(bf16[16,4096]{1,0:T(8,128)(2,1)S(1)} %get-tuple-element.50), channel_id=1, source_target_pairs={{0,1},{1,2},{2,3},{3,0},{4,5},{5,6},{6,7},{7,4},{8,9},{9,10},{10,1... | collective-permute-start | bytes 393224 | tf_op jit(solution)/shard_map/ppermute | solution.py:318
  61.6 17.0 %collective-permute-start.12 = (bf16[16,4096]{1,0:T(8,128)(2,1)S(1)}, bf16[16,4096]{1,0:T(8,128)(2,1)S(1)}, u32[]{:S(2)}, u32[]{:S(2)}) collective-permute-start(bf16[16,4096]{1,0:T(8,128)(2,1)S(1)} %get-tuple-element.52), channel_id=1, source_target_pairs={{0,1},{1,2},{2,3},{3,0},{4,5},{5,6},{6,7},{7,4},{8,9},{9,10},{10,1... | collective-permute-start | bytes 393224 | tf_op jit(solution)/shard_map/ppermute | solution.py:318
  63.6 15.7 %collective-permute-start.11 = (bf16[16,4096]{1,0:T(8,128)(2,1)S(1)}, bf16[16,4096]{1,0:T(8,128)(2,1)S(1)}, u32[]{:S(2)}, u32[]{:S(2)}) collective-permute-start(bf16[16,4096]{1,0:T(8,128)(2,1)S(1)} %get-tuple-element.51), channel_id=1, source_target_pairs={{0,3},{1,0},{2,1},{3,2},{4,7},{5,4},{6,5},{7,6},{8,11},{9,8},{10,9... | collective-permute-start | bytes 393224 | tf_op jit(solution)/shard_map/ppermute | solution.py:318
  67.0 11.6 %collective-permute-start.14 = (bf16[16,4096]{1,0:T(8,128)(2,1)S(1)}, bf16[16,4096]{1,0:T(8,128)(2,1)S(1)}, u32[]{:S(2)}, u32[]{:S(2)}) collective-permute-start(bf16[16,4096]{1,0:T(8,128)(2,1)S(1)} %shard_map.88), channel_id=1, source_target_pairs={{0,3},{1,0},{2,1},{3,2},{4,7},{5,4},{6,5},{7,6},{8,11},{9,8},{10,9... | collective-permute-start | bytes 393224 | tf_op jit(solution)/shard_map/ppermute | solution.py:318
  75.7 8.1 %collective-permute-start.10 = (bf16[16,4096]{1,0:T(8,128)(2,1)S(1)}, bf16[16,4096]{1,0:T(8,128)(2,1)S(1)}, u32[]{:S(2)}, u32[]{:S(2)}) collective-permute-start(bf16[16,4096]{1,0:T(8,128)(2,1)S(1)} %shard_map.87), channel_id=1, source_target_pairs={{0,1},{1,2},{2,3},{3,0},{4,5},{5,6},{6,7},{7,4},{8,9},{9,10},{10,1... | collective-permute-start | bytes 393224 | tf_op jit(solution)/shard_map/ppermute | solution.py:318

commit v5 on v4

--- a/solution.py
+++ b/solution.py
@@ -17,6 +17,7 @@
 B_AXES = ("zl", "y")
 NX, NB, NC, NH = 4, 8, 2, 4
 ROWS_Q, ROWS_M, ROWS_P, ROWS_O = 128, 96, 16, 32
+ROWS_F = 128
 NQ = NB * ROWS_Q
 HALF = NB * ROWS_M
 OFFSETS = (0, 3, 1, 2)
@@ -103,8 +104,11 @@
         keys = [r[:, :ROWS_M, :].reshape(HALF, HD) for r in kv_refs]
         values = [r[:, ROWS_M:, :].reshape(HALF, HD) for r in kv_refs]
     else:
-        keys = [r[...].reshape(HALF, HD) for r in kv_refs[0::2]]
-        values = [r[...].reshape(HALF, HD) for r in kv_refs[1::2]]
+        keys = [r[:, :ROWS_M, :].reshape(HALF, HD) for r in kv_refs[0::2]]
+        values = []
+        for a_ref, b_ref in zip(kv_refs[0::2], kv_refs[1::2]):
+            for n in range(NB):
+                values += [a_ref[n, ROWS_M:, :], b_ref[n]]
     keys = jnp.concatenate([jnp.concatenate(keys, axis=0), onehot], axis=1)
     values = jnp.concatenate([jnp.concatenate(values, axis=0), jnp.ones((size, 128), jnp.bfloat16)], axis=1)
     rows = received_ref[:, :ROWS_Q, :].reshape(NQ, HD)
@@ -164,41 +168,44 @@
     )(*[in_vmem(arg) for arg in args])
 
 
-def project_body(place_ref, gate_ref, rec_ref, own_ref, w_ref, top_ref, bottom_ref, up_ref, up_free_ref, down_ref, down_free_ref, here_ref):
+def project_body(order, place_ref, gate_ref, rec_ref, own_ref, w_ref, *outs):
     plane = place_ref[2]
-    order = [pl.multiple_of(lax.rem(plane + away, NH) * ROWS_O, ROWS_O) for away in (2, 1, 3, 0)]
+    starts = [pl.multiple_of(lax.rem(plane + away, NH) * ROWS_O, ROWS_O) for away in order]
     mixed = []
     for h in range(NB):
         gate = 1.0 / (1.0 + jnp.exp(jnp.full((1, 128), -gate_ref[h], jnp.float32)))
         span = slice(h * HD, (h + 1) * HD)
         rows = []
-        for start in order:
+        for start in starts:
             recalled = rec_ref[h, pl.ds(start, ROWS_O), :].astype(jnp.float32)
             blended = gate * recalled + (1.0 - gate) * own_ref[pl.ds(start, ROWS_O), span].astype(jnp.float32)
             rows.append(blended.astype(jnp.bfloat16))
         mixed.append(jnp.concatenate(rows, axis=0))
     mixed = jnp.concatenate(mixed, axis=1)
     width = 512
-    half = ROWS_O // 2
-    outs = (top_ref, bottom_ref, up_ref, up_free_ref, down_free_ref, down_ref)
     for i in range(w_ref.shape[1] // width):
         span = slice(i * width, (i + 1) * width)
         part = jnp.dot(mixed, w_ref[:, span], preferred_element_type=jnp.float32)
-        for n, out_ref in enumerate(outs):
-            out_ref[:, span] = part[n * half : (n + 1) * half].astype(jnp.bfloat16)
-        here_ref[:, span] = part[3 * ROWS_O :]
-
-
-def project(place, gate_bias, recalled, own_values, w_out):
-    half = pltpu.VMEM((ROWS_O // 2, w_out.shape[1]), jnp.bfloat16)
-    return pl.pallas_call(
-        project_body,
+        row = 0
+        for out_ref in outs:
+            size = out_ref.shape[0]
+            out_ref[:, span] = part[row : row + size].astype(out_ref.dtype)
+            row += size
+
+
+def project(order, place, gate_bias, recalled, own_values, w_out):
+    model = w_out.shape[1]
+    passed_on = [away for away in order if away]
+    outs = [pltpu.VMEM((ROWS_O // 2, model), jnp.bfloat16)] * (2 * len(passed_on))
+    if len(passed_on) < len(order):
+        outs.append(pltpu.VMEM((ROWS_O, model), jnp.float32))
+    return pl.pallas_call(
+        lambda *refs: project_body(order, *refs),
         in_specs=[SMEM_SPEC, SMEM_SPEC, VMEM_SPEC, VMEM_SPEC, VMEM_SPEC],
-        out_specs=[VMEM_SPEC] * 7,
-        out_shape=[half] * 6 + [pltpu.VMEM((ROWS_O, w_out.shape[1]), jnp.float32)],
-        cost_estimate=pl.CostEstimate(flops=2 * ROWS_Q * w_out.size, bytes_accessed=10 << 20, transcendentals=0),
-        compiler_params=pltpu.CompilerParams(vmem_limit_bytes=16 << 20),
-        name="project",
+        out_specs=[VMEM_SPEC] * len(outs),
+        out_shape=outs,
+        cost_estimate=pl.CostEstimate(flops=1 << 20, bytes_accessed=1 << 10, transcendentals=0),
+        compiler_params=pltpu.CompilerParams(vmem_limit_bytes=16 << 20),
     )(place, gate_bias, in_vmem(recalled), in_vmem(own_values), in_vmem(w_out))
 
 
@@ -301,10 +308,10 @@
     bias = make_bias(place, received[:, ROWS_Q + 2 * ROWS_M :, :], pattern)
     state = attend(0, received, bias, (own, own_far), None)
     left, *state = lax.optimization_barrier((left, *state))
-    opposite_k = shift(left[:, :ROWS_M], 1)
+    opposite_k = shift(left[:, :ROWS_F], 1)
     left_far = swap(left)
     right, *state = lax.optimization_barrier((right, *state))
-    opposite_v = shift(right[:, ROWS_M:], 3)
+    opposite_v = shift(right[:, ROWS_F:], 3)
     right_far = swap(right)
     state = attend(1, received, bias, (left, left_far), state)
     state = attend(2, received, bias, (right, right_far), state)
@@ -317,9 +324,11 @@
     def plane_shift(array, by):
         return lax.ppermute(array, "h", [(i, (i + by) % NH) for i in range(NH)])
 
-    top, bottom, up, up_free, down, down_free, here = project(place, gate_bias, recalled, own_values, w_out)
+    operands = (place, gate_bias, recalled, own_values, w_out)
+    top, bottom = project((2,), *operands)
     top = plane_shift(top, 1)
     bottom = plane_shift(bottom, 3)
+    up, up_free, down_free, down, here = project((1, 3, 0), *operands)
     up_free = plane_shift(up_free, 1)
     down_free = plane_shift(down_free, 3)
     up = plane_shift(add(up, top), 1)

time: 84.8 us -> 82.8 us (0.976)
  the two profiles are of different devices: /device:TPU:40 before, /device:TPU:32 now
where the time goes in v5:
time: 82.8 us; the launch traced here: 82.5 us
  blocking collectives  26.3 us (32%)
  starting transfers between devices  20.7 us (25%)
  Pallas kernels  17.5 us (21%)
  waiting for transfers between devices  16.8 us (20%)
  local copies, waits for them, and re-layouts  0.84 us (1%)
    all_to_all x1, blocking collectives, local(): lax.all_to_all(pack(queries, mem_keys, mem_values, probes.T), B_AXES, 0,...  16.2 us
    ppermute x6, starting transfers between devices, plane_shift(): return lax.ppermute(array, 'h', [(i, (i + by) % NH) for i in range(NH)])  12.7 us
    ppermute x6, waiting for transfers between devices, plane_shift(): return lax.ppermute(array, 'h', [(i, (i + by) % NH) for i in range(NH)])  10.5 us
    all_to_all x1, blocking collectives, local(): recalled = lax.all_to_all(state, B_AXES, 0, 0, tiled=True)  10.2 us
    pallas_call x5, Pallas kernels, attend(): pl.pallas_call(lambda *refs: chunk_body(k, slots, parts, first, last, *re...  8.29 us
    ppermute x4, starting transfers between devices, shift(): return lax.ppermute(array, 'x', [(i, (i + by) % NX) for i in range(NX)])  6.89 us
    ppermute x4, waiting for transfers between devices, shift(): return lax.ppermute(array, 'x', [(i, (i + by) % NX) for i in range(NX)])  6.31 us
    pallas_call x2, Pallas kernels, project(): pl.pallas_call(lambda *refs: project_body(order, *refs), in_specs=[SMEM_S...  4.07 us
  transfers between devices with their start and end apart: 15, of which 5 were waited for; matrix products, arithmetic and copies ran while one was open for 0% of the time, Pallas kernels for 15%

profile of v5, /device:TPU:32, one launch (start us, length us, event | category | flops | bytes accessed | tf_op | source)
XLA Modules:
  0.0 82.5 jit_solution(14295420925744517503)
XLA Ops:
  0.0 1.3 %pack.1 = bf16[8,336,128]{2,1,0:T(8,128)(2,1)S(1)} custom-call(bf16[128,1024]{1,0:T(8,128)(2,1)} %q_ref.1, bf16[96,1024]{1,0:T(8,128)(2,1)} %k_ref.1, bf16[96,1024]{1,0:T(8,128)(2,1)} %v_ref.1, s32[8,128]{1,0:T(8,128)} %bitcast.6), custom_call_target="tpu_custom_call" | custom-call | tf_op jit(solution)/shard_map/pack/pallas_call | solution.py:283
  1.3 16.2 %all_to_all.10.refs_0_ = bf16[8,336,128]{2,1,0:T(8,128)(2,1)S(1)} all-to-all(bf16[8,336,128]{2,1,0:T(8,128)(2,1)S(1)} %pack.1), channel_id=1, replica_groups=mesh['x'=4,'zl'=2,'y'=4,'c'=2,'h'=4] {'zl','y'}, dimensions={0} | all-to-all | bytes 1376256 | tf_op jit(solution)/shard_map/all_to_all | solution.py:295
  17.5 0.1 collective-permute-start.1
  17.6 1.6 %collective-permute-start = (bf16[8,192,128]{2,1,0:T(8,128)(2,1)S(1)}, bf16[8,192,128]{2,1,0:T(8,128)(2,1)S(1)}, u32[]{:S(2)}, u32[]{:S(2)}) collective-permute-start(bf16[8,192,128]{2,1,0:T(8,128)(2,1)S(1)} %slice.17.refs_2_), channel_id=1, source_target_pairs={{0,64},{64,128},{128,192},{192,0},{1,65},{65,129},{129,193},{193,1... | collective-permute-start | bytes 1179656 | tf_op jit(solution)/shard_map/ppermute | solution.py:299
  19.2 1.7 %collective-permute-start.3 = (bf16[8,192,128]{2,1,0:T(8,128)(2,1)S(1)}, bf16[8,192,128]{2,1,0:T(8,128)(2,1)S(1)}, u32[]{:S(2)}, u32[]{:S(2)}) collective-permute-start(bf16[8,192,128]{2,1,0:T(8,128)(2,1)S(1)} %slice.17.refs_2_), channel_id=1, source_target_pairs={{0,192},{64,0},{128,64},{192,128},{1,193},{65,1},{129,65},{193,129... | collective-permute-start | bytes 1179656 | tf_op jit(solution)/shard_map/ppermute | solution.py:299
  20.9 0.1 pad_add_fusion.place_ref.refs_0_
  21.0 0.8 copy-done.1
  21.8 2.4 %bias.1.refs_1_ = bf16[4,1024,128]{2,1,0:T(8,128)(2,1)S(1)} custom-call(s32[3]{0:T(128)S(1)} %pad_add_fusion.place_ref.refs_0_, bf16[8,16,128]{2,1,0:T(8,128)(2,1)S(1)} %slice.16.probe_ref, s32[64,64]{1,0:T(8,128)S(1)} %copy-done.1), custom_call_target="tpu_custom_call" | custom-call | tf_op jit(solution)/shard_map/bias/pallas_call | solution.py:77
  24.1 0.0 collective-permute-done.1.refs_3_
  24.1 1.9 %shard_map.82 = (f32[1024,128]{1,0:T(8,128)S(1)}, f32[1024,256]{1,0:T(8,128)S(1)}) custom-call(bf16[8,336,128]{2,1,0:T(8,128)(2,1)S(1)} %all_to_all.10.refs_0_, bf16[4,1024,128]{2,1,0:T(8,128)(2,1)S(1)} %bias.1.refs_1_, bf16[8,192,128]{2,1,0:T(8,128)(2,1)S(1)} %slice.17.refs_2_, bf16[8,192,128]{2,1,0:T(8,128)(2,1)S(1)} %collective-permute-done.1.refs_3_), custom_call_target="tpu_custom_call" | custom-call | flops 1048576 | bytes 1024 | tf_op jit(solution)/shard_map/pallas_call | solution.py:160
  26.0 4.3 %collective-permute-done.refs_2_ = bf16[8,192,128]{2,1,0:T(8,128)(2,1)S(1)} collective-permute-done((bf16[8,192,128]{2,1,0:T(8,128)(2,1)S(1)}, bf16[8,192,128]{2,1,0:T(8,128)(2,1)S(1)}, u32[]{:S(2)}, u32[]{:S(2)}) %collective-permute-start) | collective-permute-done | bytes 393248 | tf_op jit(solution)/shard_map/ppermute | solution.py:299
  30.3 0.0 collective-permute-start.6
  30.3 0.0 collective-permute-done.3.refs_2_
  30.3 0.5 collective-permute-start.5
  30.9 0.0 slice-start
  30.9 0.0 copy-start
  30.9 0.0 copy-start.2
  30.9 1.1 %collective-permute-start.2 = (bf16[8,128,128]{2,1,0:T(8,128)(2,1)S(1)}, bf16[8,128,128]{2,1,0:T(8,128)(2,1)S(1)}, u32[]{:S(2)}, u32[]{:S(2)}) collective-permute-start(bf16[8,128,128]{2,1,0:T(8,128)(2,1)S(1)} %slice.14), channel_id=1, source_target_pairs={{0,64},{64,128},{128,192},{192,0},{1,65},{65,129},{129,193},{193,1... | collective-permute-start | bytes 786440 | tf_op jit(solution)/shard_map/ppermute | solution.py:299
  32.0 2.5 %collective-permute-start.4 = (bf16[8,64,128]{2,1,0:T(8,128)(2,1)S(1)}, bf16[8,64,128]{2,1,0:T(8,128)(2,1)S(1)}, u32[]{:S(2)}, u32[]{:S(2)}) collective-permute-start(bf16[8,64,128]{2,1,0:T(8,128)(2,1)S(1)} %slice.15), channel_id=1, source_target_pairs={{0,192},{64,0},{128,64},{192,128},{1,193},{65,1},{129,65},{193,129... | collective-permute-start | bytes 393224 | tf_op jit(solution)/shard_map/ppermute | solution.py:299
  34.5 0.0 collective-permute-done.6.refs_3_
  34.5 1.9 %shard_map.83 = (f32[1024,128]{1,0:T(8,128)S(1)}, f32[1024,256]{1,0:T(8,128)S(1)}) custom-call(bf16[8,336,128]{2,1,0:T(8,128)(2,1)S(1)} %all_to_all.10.refs_0_, bf16[4,1024,128]{2,1,0:T(8,128)(2,1)S(1)} %bias.1.refs_1_, bf16[8,192,128]{2,1,0:T(8,128)(2,1)S(1)} %collective-permute-done.refs_2_, bf16[8,192,128]{2,1,0:T(8,128)(2,1)S(1)} %collective-permute-done.6.refs_3_, ...), custom_call_target="tpu_custom_call" | custom-call | flops 1048576 | bytes 1024 | tf_op jit(solution)/shard_map/pallas_call | solution.py:160
  36.4 0.0 collective-permute-done.5.refs_3_
  36.4 0.0 slice-start.1
  36.5 1.9 %shard_map.84 = (f32[1024,128]{1,0:T(8,128)S(1)}, f32[1024,256]{1,0:T(8,128)S(1)}) custom-call(bf16[8,336,128]{2,1,0:T(8,128)(2,1)S(1)} %all_to_all.10.refs_0_, bf16[4,1024,128]{2,1,0:T(8,128)(2,1)S(1)} %bias.1.refs_1_, bf16[8,192,128]{2,1,0:T(8,128)(2,1)S(1)} %collective-permute-done.3.refs_2_, bf16[8,192,128]{2,1,0:T(8,128)(2,1)S(1)} %collective-permute-done.5.refs_3_, ...), custom_call_target="tpu_custom_call" | custom-call | flops 1048576 | bytes 1024 | tf_op jit(solution)/shard_map/pallas_call | solution.py:160
  38.4 0.0 collective-permute-done.4.refs_3_
  38.4 2.0 %collective-permute-done.2.refs_2_ = bf16[8,128,128]{2,1,0:T(8,128)(2,1)S(1)} collective-permute-done((bf16[8,128,128]{2,1,0:T(8,128)(2,1)S(1)}, bf16[8,128,128]{2,1,0:T(8,128)(2,1)S(1)}, u32[]{:S(2)}, u32[]{:S(2)}) %collective-permute-start.2) | collective-permute-done | bytes 262176 | tf_op jit(solution)/shard_map/ppermute | solution.py:299
  40.4 0.0 collective-permute-start.7
  40.4 0.5 collective-permute-start.8
  40.9 1.3 %shard_map.85 = (f32[1024,128]{1,0:T(8,128)S(1)}, f32[1024,256]{1,0:T(8,128)S(1)}) custom-call(bf16[8,336,128]{2,1,0:T(8,128)(2,1)S(1)} %all_to_all.10.refs_0_, bf16[4,1024,128]{2,1,0:T(8,128)(2,1)S(1)} %bias.1.refs_1_, bf16[8,128,128]{2,1,0:T(8,128)(2,1)S(1)} %collective-permute-done.2.refs_2_, bf16[8,64,128]{2,1,0:T(8,128)(2,1)S(1)} %collective-permute-done.4.refs_3_, ...), custom_call_target="tpu_custom_call" | custom-call | flops 1048576 | bytes 1024 | tf_op jit(solution)/shard_map/pallas_call | solution.py:160
  42.2 0.0 collective-permute-done.8.refs_3_
  42.2 0.0 collective-permute-done.7.refs_2_
  42.2 1.3 %shard_map.86 = bf16[8,128,128]{2,1,0:T(8,128)(2,1)S(1)} custom-call(bf16[8,336,128]{2,1,0:T(8,128)(2,1)S(1)} %all_to_all.10.refs_0_, bf16[4,1024,128]{2,1,0:T(8,128)(2,1)S(1)} %bias.1.refs_1_, bf16[8,128,128]{2,1,0:T(8,128)(2,1)S(1)} %collective-permute-done.7.refs_2_, bf16[8,64,128]{2,1,0:T(8,128)(2,1)S(1)} %collective-permute-done.8.refs_3_, ...), custom_call_target="tpu_custom_call" | custom-call | flops 1048576 | bytes 1024 | tf_op jit(solution)/shard_map/pallas_call | solution.py:160
  43.5 10.2 %all_to_all.11.refs_2_ = bf16[8,128,128]{2,1,0:T(8,128)(2,1)S(1)} all-to-all(bf16[8,128,128]{2,1,0:T(8,128)(2,1)S(1)} %shard_map.86), channel_id=1, replica_groups=mesh['x'=4,'zl'=2,'y'=4,'c'=2,'h'=4] {'zl','y'}, dimensions={0} | all-to-all | bytes 524288 | tf_op jit(solution)/shard_map/all_to_all | solution.py:322
  53.7 2.1 %shard_map.88 = (bf16[16,4096]{1,0:T(8,128)(2,1)S(1)}, bf16[16,4096]{1,0:T(8,128)(2,1)S(1)}) custom-call(s32[3]{0:T(128)S(1)} %pad_add_fusion.place_ref.refs_0_, f32[8]{0:T(128)S(1)} %copy-done.2, bf16[8,128,128]{2,1,0:T(8,128)(2,1)S(1)} %all_to_all.11.refs_2_, bf16[128,1024]{1,0:T(8,128)(2,1)S(1)} %copy-done, bf16[1024,4096]{1,0:T(8,128)(2,1)S(1)} %bitcast.5), custom_call_target="tpu_custom_call" | custom-call | flops 1048576 | bytes 1024 | tf_op jit(solution)/shard_map/pallas_call | solution.py:202
  55.8 5.4 %collective-permute-start.13 = (bf16[16,4096]{1,0:T(8,128)(2,1)S(1)}, bf16[16,4096]{1,0:T(8,128)(2,1)S(1)}, u32[]{:S(2)}, u32[]{:S(2)}) collective-permute-start(bf16[16,4096]{1,0:T(8,128)(2,1)S(1)} %get-tuple-element.54), channel_id=1, source_target_pairs={{0,3},{1,0},{2,1},{3,2},{4,7},{5,4},{6,5},{7,6},{8,11},{9,8},{10,9... | collective-permute-start | bytes 393224 | tf_op jit(solution)/shard_map/ppermute | solution.py:325
  61.2 0.0 collective-permute-start.9
  61.2 2.0 %shard_map.87 = (bf16[16,4096]{1,0:T(8,128)(2,1)S(1)}, bf16[16,4096]{1,0:T(8,128)(2,1)S(1)}, bf16[16,4096]{1,0:T(8,128)(2,1)S(1)}, bf16[16,4096]{1,0:T(8,128)(2,1)S(1)}, f32[32,4096]{1,0:T(8,128)S(1)}) custom-call(s32[3]{0:T(128)S(1)} %pad_add_fusion.place_ref.refs_0_, f32[8]{0:T(128)S(1)} %copy-done.2, bf16[8,128,128]{2,1,0:T(8,128)(2,1)S(1)} %all_to_all.11.refs_2_, ...), custom_call_target="tpu_custom_call" | custom-call | flops 1048576 | bytes 1024 | tf_op jit(solution)/shard_map/pallas_call | solution.py:202
  63.2 2.1 %collective-permute-start.12 = (bf16[16,4096]{1,0:T(8,128)(2,1)S(1)}, bf16[16,4096]{1,0:T(8,128)(2,1)S(1)}, u32[]{:S(2)}, u32[]{:S(2)}) collective-permute-start(bf16[16,4096]{1,0:T(8,128)(2,1)S(1)} %get-tuple-element.52), channel_id=1, source_target_pairs={{0,1},{1,2},{2,3},{3,0},{4,5},{5,6},{6,7},{7,4},{8,9},{9,10},{10,1... | collective-permute-start | bytes 393224 | tf_op jit(solution)/shard_map/ppermute | solution.py:325
  65.3 2.2 %collective-permute-start.11 = (bf16[16,4096]{1,0:T(8,128)(2,1)S(1)}, bf16[16,4096]{1,0:T(8,128)(2,1)S(1)}, u32[]{:S(2)}, u32[]{:S(2)}) collective-permute-start(bf16[16,4096]{1,0:T(8,128)(2,1)S(1)} %get-tuple-element.51), channel_id=1, source_target_pairs={{0,3},{1,0},{2,1},{3,2},{4,7},{5,4},{6,5},{7,6},{8,11},{9,8},{10,9... | collective-permute-start | bytes 393224 | tf_op jit(solution)/shard_map/ppermute | solution.py:325
  67.5 2.9 %collective-permute-start.14 = (bf16[16,4096]{1,0:T(8,128)(2,1)S(1)}, bf16[16,4096]{1,0:T(8,128)(2,1)S(1)}, u32[]{:S(2)}, u32[]{:S(2)}) collective-permute-start(bf16[16,4096]{1,0:T(8,128)(2,1)S(1)} %shard_map.90), channel_id=1, source_target_pairs={{0,3},{1,0},{2,1},{3,2},{4,7},{5,4},{6,5},{7,6},{8,11},{9,8},{10,9... | collective-permute-start | bytes 393224 | tf_op jit(solution)/shard_map/ppermute | solution.py:325
  70.4 2.8 %collective-permute-done.9.b_ref = bf16[16,4096]{1,0:T(8,128)(2,1)S(1)} collective-permute-done((bf16[16,4096]{1,0:T(8,128)(2,1)S(1)}, bf16[16,4096]{1,0:T(8,128)(2,1)S(1)}, u32[]{:S(2)}, u32[]{:S(2)}) %collective-permute-start.9) | collective-permute-done | bytes 131104 | tf_op jit(solution)/shard_map/ppermute | solution.py:325
  73.3 0.1 collective-permute-start.10
  73.4 4.7 %collective-permute-done.12.refs_1_ = bf16[16,4096]{1,0:T(8,128)(2,1)S(1)} collective-permute-done((bf16[16,4096]{1,0:T(8,128)(2,1)S(1)}, bf16[16,4096]{1,0:T(8,128)(2,1)S(1)}, u32[]{:S(2)}, u32[]{:S(2)}) %collective-permute-start.12) | collective-permute-done | bytes 131104 | tf_op jit(solution)/shard_map/ppermute | solution.py:325
  78.1 0.0 collective-permute-done.14.refs_2_
  78.1 0.7 shard_map.91.refs_3_
  78.8 0.0 collective-permute-done.11.refs_2_
  78.8 3.0 %collective-permute-done.10.refs_1_ = bf16[16,4096]{1,0:T(8,128)(2,1)S(1)} collective-permute-done((bf16[16,4096]{1,0:T(8,128)(2,1)S(1)}, bf16[16,4096]{1,0:T(8,128)(2,1)S(1)}, u32[]{:S(2)}, u32[]{:S(2)}) %collective-permute-start.10) | collective-permute-done | bytes 131104 | tf_op jit(solution)/shard_map/ppermute | solution.py:325
  81.8 0.7 shard_map.92
  (13 shorter events, 0.1 us)
Async XLA Ops:
  17.5 6.6 %collective-permute-start.1 = (bf16[8,192,128]{2,1,0:T(8,128)(2,1)S(1)}, bf16[8,192,128]{2,1,0:T(8,128)(2,1)S(1)}, u32[]{:S(2)}, u32[]{:S(2)}) collective-permute-start(bf16[8,192,128]{2,1,0:T(8,128)(2,1)S(1)} %slice.17.refs_2_), channel_id=1, source_target_pairs={{0,4},{4,0},{1,5},{5,1},{2,6},{6,2},{3,7},{7,3},{8,12},{12,8},{9,1... | collective-permute-start | bytes 1179656 | tf_op jit(solution)/shard_map/ppermute | solution.py:302
  17.6 12.7 %collective-permute-start = (bf16[8,192,128]{2,1,0:T(8,128)(2,1)S(1)}, bf16[8,192,128]{2,1,0:T(8,128)(2,1)S(1)}, u32[]{:S(2)}, u32[]{:S(2)}) collective-permute-start(bf16[8,192,128]{2,1,0:T(8,128)(2,1)S(1)} %slice.17.refs_2_), channel_id=1, source_target_pairs={{0,64},{64,128},{128,192},{192,0},{1,65},{65,129},{129,193},{193,1... | collective-permute-start | bytes 1179656 | tf_op jit(solution)/shard_map/ppermute | solution.py:299
  19.2 11.2 %collective-permute-start.3 = (bf16[8,192,128]{2,1,0:T(8,128)(2,1)S(1)}, bf16[8,192,128]{2,1,0:T(8,128)(2,1)S(1)}, u32[]{:S(2)}, u32[]{:S(2)}) collective-permute-start(bf16[8,192,128]{2,1,0:T(8,128)(2,1)S(1)} %slice.17.refs_2_), channel_id=1, source_target_pairs={{0,192},{64,0},{128,64},{192,128},{1,193},{65,1},{129,65},{193,129... | collective-permute-start | bytes 1179656 | tf_op jit(solution)/shard_map/ppermute | solution.py:299
  21.0 0.8 copy-start.1
  30.3 4.2 %collective-permute-start.6 = (bf16[8,192,128]{2,1,0:T(8,128)(2,1)S(1)}, bf16[8,192,128]{2,1,0:T(8,128)(2,1)S(1)}, u32[]{:S(2)}, u32[]{:S(2)}) collective-permute-start(bf16[8,192,128]{2,1,0:T(8,128)(2,1)S(1)} %collective-permute-done.refs_2_), channel_id=1, source_target_pairs={{0,4},{4,0},{1,5},{5,1},{2,6},{6,2},{3,7},{7,3},{8,12},{12,8},{9,1... | collective-permute-start | bytes 1179656 | tf_op jit(solution)/shard_map/ppermute | solution.py:302
  30.3 6.1 %collective-permute-start.5 = (bf16[8,192,128]{2,1,0:T(8,128)(2,1)S(1)}, bf16[8,192,128]{2,1,0:T(8,128)(2,1)S(1)}, u32[]{:S(2)}, u32[]{:S(2)}) collective-permute-start(bf16[8,192,128]{2,1,0:T(8,128)(2,1)S(1)} %collective-permute-done.3.refs_2_), channel_id=1, source_target_pairs={{0,4},{4,0},{1,5},{5,1},{2,6},{6,2},{3,7},{7,3},{8,12},{12,8},{9,1... | collective-permute-start | bytes 1179656 | tf_op jit(solution)/shard_map/ppermute | solution.py:302
  30.9 22.8 %slice-start = ((s8[8388608]{0:T(1024)(128)(4,1)}), s8[4194304]{0:T(1024)(128)(4,1)S(1)}, s32[]{:S(2)}) async-start(s8[8388608]{0:T(1024)(128)(4,1)} %bitcast.4), calls=%async_computation.2 | async-start | bytes 8388608
  30.9 22.8 %copy-start = (bf16[128,1024]{1,0:T(8,128)(2,1)S(1)}, bf16[128,1024]{1,0:T(8,128)(2,1)}, u32[]{:S(2)}) copy-start(bf16[128,1024]{1,0:T(8,128)(2,1)} %refs_3_.3) | copy-start | bytes 786436
  30.9 22.8 %copy-start.2 = (f32[8]{0:T(128)S(1)}, f32[8]{0:T(128)}, u32[]{:S(2)}) copy-start(f32[8]{0:T(128)} %refs_1_.3) | copy-start | bytes 100
  30.9 9.5 %collective-permute-start.2 = (bf16[8,128,128]{2,1,0:T(8,128)(2,1)S(1)}, bf16[8,128,128]{2,1,0:T(8,128)(2,1)S(1)}, u32[]{:S(2)}, u32[]{:S(2)}) collective-permute-start(bf16[8,128,128]{2,1,0:T(8,128)(2,1)S(1)} %slice.14), channel_id=1, source_target_pairs={{0,64},{64,128},{128,192},{192,0},{1,65},{65,129},{129,193},{193,1... | collective-permute-start | bytes 786440 | tf_op jit(solution)/shard_map/ppermute | solution.py:299
  32.0 6.4 %collective-permute-start.4 = (bf16[8,64,128]{2,1,0:T(8,128)(2,1)S(1)}, bf16[8,64,128]{2,1,0:T(8,128)(2,1)S(1)}, u32[]{:S(2)}, u32[]{:S(2)}) collective-permute-start(bf16[8,64,128]{2,1,0:T(8,128)(2,1)S(1)} %slice.15), channel_id=1, source_target_pairs={{0,192},{64,0},{128,64},{192,128},{1,193},{65,1},{129,65},{193,129... | collective-permute-start | bytes 393224 | tf_op jit(solution)/shard_map/ppermute | solution.py:299
  36.4 17.2 %slice-start.1 = ((s8[8388608]{0:T(1024)(128)(4,1)}), s8[4194304]{0:T(1024)(128)(4,1)S(1)}, s32[]{:S(2)}) async-start(s8[8388608]{0:T(1024)(128)(4,1)} %bitcast.4), calls=%async_computation.3 | async-start | bytes 8388608
  40.4 1.8 %collective-permute-start.7 = (bf16[8,128,128]{2,1,0:T(8,128)(2,1)S(1)}, bf16[8,128,128]{2,1,0:T(8,128)(2,1)S(1)}, u32[]{:S(2)}, u32[]{:S(2)}) collective-permute-start(bf16[8,128,128]{2,1,0:T(8,128)(2,1)S(1)} %collective-permute-done.2.refs_2_), channel_id=1, source_target_pairs={{0,4},{4,0},{1,5},{5,1},{2,6},{6,2},{3,7},{7,3},{8,12},{12,8},{9,1... | collective-permute-start | bytes 786440 | tf_op jit(solution)/shard_map/ppermute | solution.py:302
  40.4 1.8 %collective-permute-start.8 = (bf16[8,64,128]{2,1,0:T(8,128)(2,1)S(1)}, bf16[8,64,128]{2,1,0:T(8,128)(2,1)S(1)}, u32[]{:S(2)}, u32[]{:S(2)}) collective-permute-start(bf16[8,64,128]{2,1,0:T(8,128)(2,1)S(1)} %collective-permute-done.4.refs_3_), channel_id=1, source_target_pairs={{0,4},{4,0},{1,5},{5,1},{2,6},{6,2},{3,7},{7,3},{8,12},{12,8},{9,1... | collective-permute-start | bytes 393224 | tf_op jit(solution)/shard_map/ppermute | solution.py:302
  55.8 11.7 %collective-permute-start.13 = (bf16[16,4096]{1,0:T(8,128)(2,1)S(1)}, bf16[16,4096]{1,0:T(8,128)(2,1)S(1)}, u32[]{:S(2)}, u32[]{:S(2)}) collective-permute-start(bf16[16,4096]{1,0:T(8,128)(2,1)S(1)} %get-tuple-element.54), channel_id=1, source_target_pairs={{0,3},{1,0},{2,1},{3,2},{4,7},{5,4},{6,5},{7,6},{8,11},{9,8},{10,9... | collective-permute-start | bytes 393224 | tf_op jit(solution)/shard_map/ppermute | solution.py:325
  61.2 12.1 %collective-permute-start.9 = (bf16[16,4096]{1,0:T(8,128)(2,1)S(1)}, bf16[16,4096]{1,0:T(8,128)(2,1)S(1)}, u32[]{:S(2)}, u32[]{:S(2)}) collective-permute-start(bf16[16,4096]{1,0:T(8,128)(2,1)S(1)} %get-tuple-element.50), channel_id=1, source_target_pairs={{0,1},{1,2},{2,3},{3,0},{4,5},{5,6},{6,7},{7,4},{8,9},{9,10},{10,1... | collective-permute-start | bytes 393224 | tf_op jit(solution)/shard_map/ppermute | solution.py:325
  63.2 14.9 %collective-permute-start.12 = (bf16[16,4096]{1,0:T(8,128)(2,1)S(1)}, bf16[16,4096]{1,0:T(8,128)(2,1)S(1)}, u32[]{:S(2)}, u32[]{:S(2)}) collective-permute-start(bf16[16,4096]{1,0:T(8,128)(2,1)S(1)} %get-tuple-element.52), channel_id=1, source_target_pairs={{0,1},{1,2},{2,3},{3,0},{4,5},{5,6},{6,7},{7,4},{8,9},{9,10},{10,1... | collective-permute-start | bytes 393224 | tf_op jit(solution)/shard_map/ppermute | solution.py:325
  65.3 13.5 %collective-permute-start.11 = (bf16[16,4096]{1,0:T(8,128)(2,1)S(1)}, bf16[16,4096]{1,0:T(8,128)(2,1)S(1)}, u32[]{:S(2)}, u32[]{:S(2)}) collective-permute-start(bf16[16,4096]{1,0:T(8,128)(2,1)S(1)} %get-tuple-element.51), channel_id=1, source_target_pairs={{0,3},{1,0},{2,1},{3,2},{4,7},{5,4},{6,5},{7,6},{8,11},{9,8},{10,9... | collective-permute-start | bytes 393224 | tf_op jit(solution)/shard_map/ppermute | solution.py:325
  67.5 10.6 %collective-permute-start.14 = (bf16[16,4096]{1,0:T(8,128)(2,1)S(1)}, bf16[16,4096]{1,0:T(8,128)(2,1)S(1)}, u32[]{:S(2)}, u32[]{:S(2)}) collective-permute-start(bf16[16,4096]{1,0:T(8,128)(2,1)S(1)} %shard_map.90), channel_id=1, source_target_pairs={{0,3},{1,0},{2,1},{3,2},{4,7},{5,4},{6,5},{7,6},{8,11},{9,8},{10,9... | collective-permute-start | bytes 393224 | tf_op jit(solution)/shard_map/ppermute | solution.py:325
  73.3 8.5 %collective-permute-start.10 = (bf16[16,4096]{1,0:T(8,128)(2,1)S(1)}, bf16[16,4096]{1,0:T(8,128)(2,1)S(1)}, u32[]{:S(2)}, u32[]{:S(2)}) collective-permute-start(bf16[16,4096]{1,0:T(8,128)(2,1)S(1)} %shard_map.89), channel_id=1, source_target_pairs={{0,1},{1,2},{2,3},{3,0},{4,5},{5,6},{6,7},{7,4},{8,9},{9,10},{10,1... | collective-permute-start | bytes 393224 | tf_op jit(solution)/shard_map/ppermute | solution.py:325
